TPU v7x, 512 devices: a whole 4x8x8 slice. The times are simulated.
512 devices in a mesh: tm: 64 (over y, z), chan: 8 (over x, core).
Axes of the slice: x: 4, y: 8, z: 8, core: 2. Of those that a mesh axis runs over, the one named last changes fastest.
Arguments:
- frames: bfloat16 [512, 16, 16, 256], P('tm'), may hold values from -6 to 6
- in_weight: bfloat16 [3, 3, 256, 1024], P(None, None, None, 'chan'), may hold values from -0.125 to 0.125
- decay_codes: int32 [1024], P('chan'), may hold values from 1 to 20
- out_weight: bfloat16 [3, 3, 1024, 256], P(None, None, 'chan'), may hold values from -0.00390625 to 0.00390625
- skip_gain: float32 [256], replicated, may hold values from 0.5 to 1.5
Outputs:
- mixed: bfloat16 [512, 16, 16, 256], P('tm', 'chan')
Inputs may be any that keep to these rules, and one draw needn't show every extreme that they name: `decay_codes`: a code k gives the channel the decay 1 - k / 4096.
All inputs are finite; a program needn't handle non-finite values.
Results may differ from a plain program's by a relative error of at most 0.0037.
Values sent between devices are 32-bit elements; how exact they have to be, the bound alone decides.
No kernel may reach another device: no remote copies, remote signals or barrier semaphores. Data moves between devices by JAX's collectives and lax.ppermute only.
A program may use at most 64 MiB of HBM per device.

v0:
```python
import jax
import jax.numpy as jnp
from jax import lax
from jax.sharding import Mesh
from jax.sharding import PartitionSpec as P

TM = ("tm_0", "tm_1")


def neutral_like(value, identity):
    return jax.tree.map(
        lambda part, zero: jnp.zeros_like(part) + jnp.asarray(zero, part.dtype), value, identity
    )


def entering(value, axes, combine, identity):
    before = start = neutral_like(value, identity)
    running = value
    for axis in reversed(axes):
        peers, position = (lax.axis_size(axis), lax.axis_index(axis))
        pieces = jax.tree.map(lambda part: lax.all_gather(part, axis), running)
        inside, running = (start, start)
        for k in range(peers):
            passed = k < position
            running = combine(running, jax.tree.map(lambda part: part[k], pieces))
            inside = jax.tree.map(lambda new, old: jnp.where(passed, new, old), running, inside)
        before = combine(inside, before)
    return before


def in_blocks(value, dim, peers):
    before, after = (value.shape[:dim], value.shape[dim + 1 :])
    return jnp.moveaxis(value.reshape(*before, peers, -1, *after), dim, 0)


def sum_at_owner(value, axis, dim):
    parts = in_blocks(value, dim, lax.axis_size(axis))
    arrived = lax.all_to_all(parts, axis, split_axis=0, concat_axis=0, tiled=True)
    return arrived.sum(axis=0)


def convolve(inputs, kernel, padding):
    return lax.conv_general_dilated(
        inputs,
        kernel,
        (1, 1),
        padding,
        dimension_numbers=("NHWC", "HWIO", "NHWC"),
        preferred_element_type=jnp.float32,
    )


def combine(earlier, following):
    return (earlier[0] * following[0], following[0] * earlier[1] + following[1])


def per_device(frames, in_weight, decay_codes, out_weight, skip_gain):
    drive_term = convolve(frames, in_weight, "SAME")
    decay_rate = 1.0 - decay_codes.astype(jnp.float32) / 4096.0
    frame_count = frames.shape[0]
    running = jnp.zeros(drive_term.shape[1:], jnp.float32)
    local_states = []
    for frame_index in range(frame_count):
        running = decay_rate * running + drive_term[frame_index]
        local_states.append(running)
    total_decay = decay_rate**frame_count
    identity = (jnp.ones_like(total_decay), jnp.zeros_like(running))
    carried = entering((total_decay, running), TM, combine, identity)
    carry_state = carried[1]
    corrected = []
    decay_power = decay_rate
    for frame_index in range(frame_count):
        corrected.append(local_states[frame_index] + decay_power * carry_state)
        decay_power = decay_power * decay_rate
    states = jnp.stack(corrected).astype(jnp.bfloat16)
    own_rows = states.shape[1] // lax.axis_size("chan")
    start_row = lax.axis_index("chan") * own_rows
    own_frames = lax.dynamic_slice_in_dim(frames, start_row, own_rows, 1).astype(jnp.float32)
    partial_value = convolve(states, out_weight, "SAME")
    summed = sum_at_owner(partial_value, "chan", 1)
    return jax.nn.gelu(summed + skip_gain * own_frames, approximate=False).astype(jnp.bfloat16)


def solution(mesh):
    finer = Mesh(mesh.devices.reshape(8, 8, mesh.shape["chan"]), ("tm_0", "tm_1", "chan"))
    placed = (
        P(TM, None, None, None),
        P(None, None, None, "chan"),
        P("chan"),
        P(None, None, "chan", None),
        P(),
    )
    return jax.shard_map(
        per_device,
        mesh=finer,
        in_specs=placed,
        out_specs=P(TM, "chan", None, None),
        check_vma=False,
    )
```

profile of v0, /device:TPU:1, one launch (start us, length us, event | category | flops | bytes accessed | tf_op | source)
XLA Modules:
  0.0 146.6 jit_solution(14704542714116837729)
XLA Ops:
  6.5 0.0 copy-start
  6.5 0.0 all-gather.6.cloned.1.call-start
  6.5 0.7 fusion.30
  7.3 4.1 %fusion.32 = f32[8,16,16,128]{3,0,2,1:T(8,128)S(1)} fusion(bf16[3,3,256,128]{3,2,1,0:T(8,128)(2,1)} %param.6, bf16[8,16,16,256]{3,2,1,0:T(8,128)(2,1)} %param.5), kind=kOutput, calls=%fused_computation.105 | convolution fusion | flops 1109393408 | bytes 2686976 | tf_op jit(solution)/shard_map/conv_general_dilated | solution.py:43
  11.3 0.7 fusion.36
  12.1 0.7 multiply_add_fusion.1
  12.8 0.0 all-gather.6.cloned.1.call-update
  12.8 0.0 all-gather.8.cloned.1.call-start
  12.9 19.4 %all-gather.1 = f32[8,1,128]{2,1,0:T(1,128)S(1)} all-gather(f32[1,1,128]{2,1,0:T(1,128)S(1)} %get-tuple-element.46), channel_id=2, replica_groups=mesh['tm_0'=8,'tm_1'=8,'chan'=8] {'tm_1'}, dimensions={0}, use_global_device_ids=true | all-gather | bytes 4608 | tf_op jit(solution)/shard_map/all_gather | solution.py:21
  32.3 23.4 %all-gather.6.cloned.1.call-done = f32[8,16,16,128]{3,2,1,0:T(8,128)} async-done(((f32[1,16,16,128]{3,2,1,0:T(8,128)}), f32[8,16,16,128]{3,2,1,0:T(8,128)}) %all-gather.6.cloned.1.call-update) | async-done | bytes 1048592 | tf_op jit(solution)/shard_map/all_gather | solution.py:21
  55.7 2.0 %slice_add_fusion.8 = (f32[1,16,16,128]{3,2,1,0:T(8,128)}, f32[1,16,16,128]{3,2,1,0:T(8,128)S(1)}) fusion(f32[8,16,16,128]{3,2,1,0:T(8,128)} %all-gather.6.cloned.1.call-done, f32[128]{0:T(128)S(1)} %get-tuple-element.34, f32[128]{0:T(128)S(1)} %get-tuple-element.39, f32[128]{0:T(128)S(1)} %get-tuple-element.36, f32[128]{0:T(128)S(1)} %get-tuple-element.35, ...), kind=kLoop, calls=%fused_computation.33 | loop fusion | flops 491520 | bytes 1314816 | tf_op jit(solution)/shard_map/add | solution.py:54
  57.7 0.0 all-gather.8.cloned.1.call-update
  57.8 12.4 %all-gather.2 = f32[8,1,128]{2,1,0:T(1,128)S(1)} all-gather(f32[1,1,128]{2,1,0:T(1,128)S(1)} %fusion.24), channel_id=1, replica_groups=mesh['tm_0'=8,'tm_1'=8,'chan'=8] {'tm_0'}, dimensions={0}, use_global_device_ids=true | all-gather | bytes 4608 | tf_op jit(solution)/shard_map/all_gather | solution.py:21
  70.2 26.4 %all-gather.8.cloned.1.call-done = f32[8,16,16,128]{3,2,1,0:T(8,128)} async-done(((f32[1,16,16,128]{3,2,1,0:T(8,128)}), f32[8,16,16,128]{3,2,1,0:T(8,128)}) %all-gather.8.cloned.1.call-update) | async-done | bytes 1048592 | tf_op jit(solution)/shard_map/all_gather | solution.py:21
  96.5 1.8 %fusion.15 = (bf16[8,16,16,128]{3,2,1,0:T(8,128)(2,1)S(1)}, f32[1,16,16,128]{3,2,1,0:T(8,128)S(1)}) fusion(f32[1,16,16,128]{3,2,1,0:T(8,128)S(1)} %bitcast.103, f32[128]{0:T(128)S(1)} %get-tuple-element.47, f32[128]{0:T(128)S(1)} %get-tuple-element.45, f32[1,16,16,128]{3,2,1,0:T(8,128)} %get-tuple-element.9, f32[1,16,16,128]{3,2,1,0:T(8,128)S(1)} %get-tuple-element.10, ...), kind=kLoop, calls=%fused_computation.56 | loop fusion | flops 1572863 | bytes 2433552
  98.6 0.0 copy-done.1
  98.6 0.0 copy-done
  98.6 2.9 %fusion = f32[8,16,16,256]{3,0,2,1:T(8,128)} fusion(bf16[3,3,128,256]{3,2,1,0:T(8,128)(2,1)S(1)} %copy-done, bf16[8,16,16,128]{3,2,1,0:T(8,128)(2,1)S(1)} %fusion.22), kind=kOutput, calls=%fused_computation | convolution fusion | flops 1109393408 | bytes 3211264 | tf_op jit(solution)/shard_map/conv_general_dilated | solution.py:43
  101.5 9.8 %all-to-all-start = ((f32[8,8,2,16,256]{4,1,3,2,0:T(8,128)}), f32[8,8,2,16,256]{4,1,3,2,0:T(8,128)S(1)}, u32[]{:S(2)}, u32[]{:S(2)}) async-start(f32[8,8,2,16,256]{4,1,3,2,0:T(8,128)} %bitcast.95), calls=%async_computation | async-start | bytes 4194304 | tf_op jit(solution)/shard_map/all_to_all | solution.py:38
  111.2 2.8 %copy.28 = bf16[8,16,16,256]{3,0,2,1:T(8,128)(2,1)} copy(bf16[8,16,16,256]{3,2,1,0:T(8,128)(2,1)} %param.5) | data formatting | bytes 2097152 | tf_op args[0]
  114.0 23.4 %all-to-all-done = f32[8,8,2,16,256]{4,1,3,2,0:T(8,128)S(1)} async-done(((f32[8,8,2,16,256]{4,1,3,2,0:T(8,128)}), f32[8,8,2,16,256]{4,1,3,2,0:T(8,128)S(1)}, u32[]{:S(2)}, u32[]{:S(2)}) %all-to-all-start) | async-done | bytes 2097184 | tf_op jit(solution)/shard_map/all_to_all | solution.py:38
  137.4 0.1 reduce_sum.9
  137.6 1.5 %fusion.4 = bf16[8,2,16,256]{3,0,2,1:T(8,128)(2,1)S(1)} fusion(f32[8,2,16,256]{3,0,2,1:T(8,128)S(1)} %reduce_sum.9, bf16[8,16,16,256]{3,0,2,1:T(8,128)(2,1)} %copy.28, s32[]{:T(128)S(6)} %select_n.359, f32[256]{0:T(256)S(1)} %copy-done.2), kind=kLoop, calls=%fused_computation.5 | loop fusion | flops 4456448 | bytes 525316 | tf_op jit(solution)/shard_map/convert_element_type | solution.py:81
  139.1 0.7 copy.39
  (14 shorter events, 0.3 us)
Async XLA Ops:
  6.5 92.1 %copy-start = (bf16[3,3,128,256]{3,2,1,0:T(8,128)(2,1)S(1)}, bf16[3,3,128,256]{3,2,1,0:T(8,128)(2,1)}, u32[]{:S(2)}) copy-start(bf16[3,3,128,256]{3,2,1,0:T(8,128)(2,1)} %param.8) | copy-start | bytes 1769476
  6.5 49.2 %all-gather.6.cloned.1.call-start = ((), (), s32[]{:S(2)}) async-start(), calls=%async_computation.1 | async-start | bytes 1179648 | tf_op jit(solution)/shard_map/all_gather | solution.py:21
  12.8 83.7 %all-gather.8.cloned.1.call-start = ((), (), s32[]{:S(2)}) async-start(), calls=%async_computation.2 | async-start | bytes 1179648 | tf_op jit(solution)/shard_map/all_gather | solution.py:21
  96.5 2.0 %copy-start.1 = (f32[1,16,16,128]{3,2,1,0:T(8,128)S(1)}, f32[1,16,16,128]{3,2,1,0:T(8,128)}, u32[]{:S(2)}) copy-start(f32[1,16,16,128]{3,2,1,0:T(8,128)} %get-tuple-element.11) | copy-start | bytes 393220
  101.5 36.0 %all-to-all-start = ((f32[8,8,2,16,256]{4,1,3,2,0:T(8,128)}), f32[8,8,2,16,256]{4,1,3,2,0:T(8,128)S(1)}, u32[]{:S(2)}, u32[]{:S(2)}) async-start(f32[8,8,2,16,256]{4,1,3,2,0:T(8,128)} %bitcast.95), calls=%async_computation | async-start | bytes 4194304 | tf_op jit(solution)/shard_map/all_to_all | solution.py:38
  111.2 26.4 %copy-start.2 = (f32[256]{0:T(256)S(1)}, f32[256]{0:T(256)}, u32[]{:S(2)}) copy-start(f32[256]{0:T(256)} %param.9) | copy-start | bytes 3076
Sparse Core Ops, SparseCore 0:
  12.9 42.7 all-gather.5
  57.9 38.6 all-gather.7
where the time goes:
time: 147 us
  waiting for transfers between devices  73.2 us (50%)
  blocking collectives  31.8 us (22%)
  between operations  13.5 us (9%)
  starting transfers between devices  9.8 us (7%)
  other arithmetic  7.19 us (5%)
  matrix products  6.94 us (5%)
  local copies, waits for them, and re-layouts  4.19 us (3%)
    all_gather x2, waiting for transfers between devices, entering(): pieces = jax.tree.map(lambda part: lax.all_gather(part, axis), running)  49.8 us
    all_gather x2, blocking collectives, entering(): pieces = jax.tree.map(lambda part: lax.all_gather(part, axis), running)  31.8 us
    all_to_all x1, waiting for transfers between devices, sum_at_owner(): lax.all_to_all(parts, axis, split_axis=0, concat_axis=0, tiled=True)  23.4 us
    all_to_all x1, starting transfers between devices, sum_at_owner(): lax.all_to_all(parts, axis, split_axis=0, concat_axis=0, tiled=True)  9.76 us
    conv_general_dilated x2, matrix products, convolve(): lax.conv_general_dilated(inputs, kernel, (1, 1), padding, dimension_numbe...  6.94 us
  transfers between devices with their start and end apart: 3, of which 3 were waited for; matrix products, arithmetic and copies ran while one was open for 2% of the time, Pallas kernels for 0%

commit v1 on v0

v1 whole, which is shorter than its diff:
```python
import jax
import jax.numpy as jnp
from jax import lax
from jax.experimental import pallas as pl
from jax.experimental.pallas import tpu as pltpu
from jax.sharding import Mesh
from jax.sharding import PartitionSpec as P

VMEM = pl.BlockSpec(memory_space=pltpu.VMEM)
SMEM = pl.BlockSpec(memory_space=pltpu.SMEM)
FRAMES, ROWS, COLS, CIN, PD = 8, 16, 16, 256, 128
PIX = ROWS * COLS
F32, BF16 = jnp.float32, jnp.bfloat16


def decay_of(codes):
    return 1.0 - codes.astype(F32) / 4096.0


def pow8(value):
    value = value * value
    value = value * value
    return value * value


def shifted_sum(left, centre, right):
    count = left.shape[0]
    column = lax.broadcasted_iota(jnp.int32, left.shape, 0) % COLS
    from_left = jnp.where(column == 0, 0.0, pltpu.roll(left, 1, 0))
    from_right = jnp.where(column == COLS - 1, 0.0, pltpu.roll(right, count - 1, 0))
    return from_left + centre + from_right


def drive_kernel(x_ref, w_ref, codes_ref, states_ref, end_ref, xpad, wcat):
    xpad[:, 0] = jnp.zeros((FRAMES, COLS, CIN), BF16)
    xpad[:, ROWS + 1] = jnp.zeros((FRAMES, COLS, CIN), BF16)
    xpad[:, 1 : ROWS + 1] = x_ref[...]
    for di in range(3):
        for dj in range(3):
            wcat[di, :, dj * PD : (dj + 1) * PD] = w_ref[di, dj]
    decay = decay_of(codes_ref[...])
    running = jnp.zeros((PIX, PD), F32)
    group = 2
    for first in range(0, FRAMES, group):
        total = jnp.zeros((group * PIX, 3 * PD), F32)
        for di in range(3):
            rows = xpad[first : first + group, di : di + ROWS].reshape(group * PIX, CIN)
            total = total + jnp.dot(rows, wcat[di], preferred_element_type=F32)
        drive = shifted_sum(total[:, :PD], total[:, PD : 2 * PD], total[:, 2 * PD :])
        for k in range(group):
            running = decay * running + drive[k * PIX : (k + 1) * PIX]
            states_ref[(first + k) * PIX : (first + k + 1) * PIX] = running
    states_ref[FRAMES * PIX :] = jnp.broadcast_to(decay, (8, PD))
    end_ref[...] = running.reshape(8, PIX // 8, PD)


def total_kernel(ends_ref, codes_ref, out_ref):
    a8 = pow8(decay_of(codes_ref[...]))
    total = ends_ref[0]
    for z in range(1, 8):
        total = a8 * total + ends_ref[z]
    for y in range(8):
        out_ref[y] = total


def carry_kernel(place_ref, ends_ref, totals_ref, codes_ref, out_ref):
    a8 = pow8(decay_of(codes_ref[...]))
    a64 = pow8(a8)
    own = place_ref[0]
    carry = jnp.zeros((PIX // 8, PD), F32)
    for y in range(8):
        carry = jnp.where(y < own, a64 * carry + totals_ref[y], carry)
    for z in range(8):
        out_ref[2 * z] = carry
        out_ref[2 * z + 1] = carry
        carry = a8 * carry + ends_ref[z]


def readout_kernel(place_ref, own_ref, other_ref, carry_ref, w_ref, out_ref, spad):
    core = place_ref[1]
    zeros = jnp.zeros((FRAMES, COLS, 2 * PD), BF16)
    spad[:, 0] = zeros
    spad[:, ROWS + 1] = zeros
    for side, (ref, which) in enumerate(((own_ref, core), (other_ref, 1 - core))):
        decay = ref[FRAMES * PIX : FRAMES * PIX + 1]
        carry = carry_ref[:, pl.ds(which, 1)].reshape(PIX, PD)
        for j in range(FRAMES):
            carry = decay * carry
            state = ref[j * PIX : (j + 1) * PIX] + carry
            spad[j, 1 : ROWS + 1, :, side * PD : (side + 1) * PD] = state.astype(BF16).reshape(ROWS, COLS, PD)
    taps = []
    rows = [
        jnp.concatenate(
            [
                spad[:, pl.ds(4 * x + 2 * core + di, 2)].reshape(FRAMES * 2 * COLS, 2 * PD)
                for x in range(4)
            ],
            axis=0,
        )
        for di in range(3)
    ]
    for dj in range(3):
        total = jnp.dot(rows[0], w_ref[0, dj], preferred_element_type=F32)
        for di in range(1, 3):
            total = total + jnp.dot(rows[di], w_ref[di, dj], preferred_element_type=F32)
        taps.append(total)
    out_ref[...] = shifted_sum(*taps)


def widen_kernel(w_ref, out_ref):
    out_ref[...] = w_ref[...].astype(F32)


def merge_kernel(own_ref, other_ref, out_ref):
    out_ref[:, :, :PD] = own_ref[...]
    out_ref[:, :, PD:] = other_ref[...].astype(BF16)


def call(kernel, out, args, scratch=(), smem=0, flops=0, moved=1 << 20):
    return pl.pallas_call(
        kernel,
        out_shape=out,
        in_specs=[SMEM] * smem + [VMEM] * (len(args) - smem),
        out_specs=jax.tree.map(lambda _: VMEM, out),
        scratch_shapes=list(scratch),
        compiler_params=pltpu.CompilerParams(vmem_limit_bytes=40 << 20),
        cost_estimate=pl.CostEstimate(flops=flops, bytes_accessed=moved, transcendentals=0),
    )(*args)


def shape(*dims, dtype=F32):
    return jax.ShapeDtypeStruct(dims, dtype)


def per_device(frames, in_weight, decay_codes, out_weight, skip_gain):
    codes = decay_codes.reshape(1, PD)
    place = jnp.stack([lax.axis_index("y"), lax.axis_index("c")]).astype(jnp.int32)
    flops = 2 * FRAMES * PIX * 9 * CIN * PD
    states, end = call(
        drive_kernel,
        (shape(FRAMES * PIX + 8, PD), shape(8, PIX // 8, PD)),
        (frames, in_weight, codes),
        scratch=(
            pltpu.VMEM((FRAMES, ROWS + 2, COLS, CIN), BF16),
            pltpu.VMEM((3, CIN, 3 * PD), BF16),
        ),
        flops=flops,
        moved=3 << 20,
    )
    swap = [(0, 1), (1, 0)]
    ends = lax.all_to_all(end, "z", 0, 0, tiled=True)
    weight_other = lax.ppermute(call(widen_kernel, shape(3, 3, PD, CIN), (out_weight,)), "c", swap)
    states_other = lax.ppermute(states, "c", swap)
    weights = call(merge_kernel, shape(3, 3, 2 * PD, CIN, dtype=BF16), (out_weight, weight_other))
    total = call(total_kernel, shape(8, PIX // 8, PD), (ends, codes))
    totals = lax.all_to_all(total, "y", 0, 0, tiled=True)
    carries = call(carry_kernel, shape(16, PIX // 8, PD), (place, ends, totals, codes), smem=1)
    carry = lax.all_to_all(carries, ("z", "c"), 0, 0, tiled=True).reshape(8, 2, PIX // 8, PD)
    partial_value = call(
        readout_kernel,
        shape(4 * FRAMES * 2 * COLS, CIN),
        (place, states, states_other, carry, weights),
        scratch=(pltpu.VMEM((FRAMES, ROWS + 2, COLS, 2 * PD), BF16),),
        smem=1,
        flops=flops,
        moved=4 << 20,
    ).reshape(4, FRAMES, 2, COLS, CIN)
    arrived = lax.all_to_all(partial_value, "x", 0, 0, tiled=True)
    start_row = 2 * (2 * lax.axis_index("x") + lax.axis_index("c"))
    own_frames = lax.dynamic_slice_in_dim(frames, start_row, 2, 1).astype(F32)
    return jax.nn.gelu(arrived.sum(axis=0) + skip_gain * own_frames, approximate=False).astype(BF16)


def solution(mesh):
    finer = Mesh(mesh.devices.reshape(8, 8, 4, 2), ("y", "z", "x", "c"))
    chan = ("x", "c")
    placed = (
        P(("y", "z"), None, None, None),
        P(None, None, None, chan),
        P(chan),
        P(None, None, chan, None),
        P(),
    )
    return jax.shard_map(
        per_device,
        mesh=finer,
        in_specs=placed,
        out_specs=P(("y", "z"), chan, None, None),
        check_vma=False,
    )
```

time: 147 us -> 89.2 us (0.61)
  waiting for transfers between devices: 73.2 us -> 35.1 us
  blocking collectives: 31.8 us -> 12.2 us
  starting transfers between devices: 9.8 us -> 28.7 us
  between operations: 13.5 us -> 0.09 us
  Pallas kernels: 0 us -> 9.18 us
  matrix products: 6.94 us -> 0 us
  other arithmetic: 7.19 us -> 2.34 us
  local copies, waits for them, and re-layouts: 4.19 us -> 1.08 us
    all_gather x2 -> x0, waiting for transfers between devices: 49.8 us -> none  [entering(): pieces = jax.tree.map(lambda part: lax.all_gather(part, axis), running)]
    all_gather x2 -> x0, blocking collectives: 31.8 us -> none  [entering(): pieces = jax.tree.map(lambda part: lax.all_gather(part, axis), running)]
    all_to_all x0 -> x1, blocking collectives: none -> 12.2 us  [per_device(): ends = lax.all_to_all(end, 'z', 0, 0, tiled=True)]
    all_to_all x1 -> x3, waiting for transfers between devices: 23.4 us -> 35 us  [the longest x1 15.5 us: per_device(): arrived = lax.all_to_all(partial_value, 'x', 0, 0, tiled=True)]
    ppermute x0 -> x2, starting transfers between devices: none -> 10.9 us  [the longest x1 8.88 us: per_device(): lax.ppermute(call(widen_kernel, shape(3, 3, PD, CIN), (out_weight,)), 'c'...]
    pallas_call x0 -> x6, Pallas kernels: none -> 9.18 us  [call(): pl.pallas_call(kernel, out_shape=out, in_specs=[SMEM] * smem + [VMEM] * (...]
    all_to_all x1 -> x3, starting transfers between devices: 9.76 us -> 17.8 us  [the longest x1 6.93 us: per_device(): lax.all_to_all(carries, ('z', 'c'), 0, 0, tiled=True)]
    conv_general_dilated x2 -> x0, matrix products: 6.94 us -> none  [convolve(): lax.conv_general_dilated(inputs, kernel, (1, 1), padding, dimension_numbe...]
  transfers between devices with their start and end apart: 3 -> 5, of which waited for: 3 -> 3; matrix products, arithmetic and copies ran while one was open for 2% -> 0% of each run, Pallas kernels for 0% -> 6%
where the time goes in v1:
time: 89.2 us; the launch traced here: 88.7 us
  waiting for transfers between devices  35.1 us (39%)
  starting transfers between devices  28.7 us (32%)
  blocking collectives  12.2 us (14%)
  Pallas kernels  9.18 us (10%)
  other arithmetic  2.34 us (3%)
  local copies, waits for them, and re-layouts  1.08 us (1%)
    all_to_all x1, waiting for transfers between devices, per_device(): arrived = lax.all_to_all(partial_value, 'x', 0, 0, tiled=True)  15.5 us
    all_to_all x1, blocking collectives, per_device(): ends = lax.all_to_all(end, 'z', 0, 0, tiled=True)  12.2 us
    all_to_all x1, waiting for transfers between devices, per_device(): lax.all_to_all(carries, ('z', 'c'), 0, 0, tiled=True)  11.6 us
    pallas_call x6, Pallas kernels, call(): pl.pallas_call(kernel, out_shape=out, in_specs=[SMEM] * smem + [VMEM] * (...  9.18 us
    ppermute x1, starting transfers between devices, per_device(): lax.ppermute(call(widen_kernel, shape(3, 3, PD, CIN), (out_weight,)), 'c'...  8.88 us
    all_to_all x1, waiting for transfers between devices, per_device(): totals = lax.all_to_all(total, 'y', 0, 0, tiled=True)  7.95 us
    all_to_all x1, starting transfers between devices, per_device(): lax.all_to_all(carries, ('z', 'c'), 0, 0, tiled=True)  6.93 us
    all_to_all x1, starting transfers between devices, per_device(): totals = lax.all_to_all(total, 'y', 0, 0, tiled=True)  6.82 us
  transfers between devices with their start and end apart: 5, of which 3 were waited for; matrix products, arithmetic and copies ran while one was open for 0% of the time, Pallas kernels for 6%

profile of v1, /device:TPU:1, one launch (start us, length us, event | category | flops | bytes accessed | tf_op | source)
XLA Modules:
  0.0 88.7 jit_solution(8833504983973646011)
XLA Ops:
  0.0 1.1 %copy-done = bf16[3,3,128,256]{3,2,1,0:T(8,128)(2,1)S(1)} copy-done((bf16[3,3,128,256]{3,2,1,0:T(8,128)(2,1)S(1)}, bf16[3,3,128,256]{3,2,1,0:T(8,128)(2,1)}, u32[]{:S(2)}) %copy-start) | copy-done | bytes 589848
  1.1 0.1 shard_map.58
  1.2 8.9 %collective-permute-start.1 = (f32[3,3,128,256]{3,2,1,0:T(8,128)S(1)}, f32[3,3,128,256]{3,2,1,0:T(8,128)S(1)}, u32[]{:S(2)}, u32[]{:S(2)}) collective-permute-start(f32[3,3,128,256]{3,2,1,0:T(8,128)S(1)} %shard_map.58), channel_id=1, source_target_pairs={{0,1},{1,0},{2,3},{3,2},{4,5},{5,4},{6,7},{7,6},{8,9},{9,8},{10,11... | collective-permute-start | bytes 3538952 | tf_op jit(solution)/shard_map/ppermute | solution.py:152
  10.0 0.0 copy-done.2
  10.0 0.0 copy-done.3
  10.1 0.0 copy-done.4
  10.1 2.8 %shard_map.55 = (f32[2056,128]{1,0:T(8,128)}, f32[8,32,128]{2,1,0:T(8,128)S(1)}) custom-call(bf16[8,16,16,256]{3,2,1,0:T(8,128)(2,1)S(1)} %copy-done.2, bf16[3,3,256,128]{3,2,1,0:T(8,128)(2,1)S(1)} %copy-done.4, s32[1,128]{1,0:T(1,128)S(1)} %bitcast.6), custom_call_target="tpu_custom_call" | custom-call | flops 1207959552 | bytes 3145728 | tf_op jit(solution)/shard_map/pallas_call | solution.py:120
  12.9 2.0 %collective-permute-start = (f32[2056,128]{1,0:T(8,128)}, f32[2056,128]{1,0:T(8,128)}, u32[]{:S(2)}, u32[]{:S(2)}) collective-permute-start(f32[2056,128]{1,0:T(8,128)} %get-tuple-element.7.own_ref), channel_id=1, source_target_pairs={{0,1},{1,0},{2,3},{3,2},{4,5},{5,4},{6,7},{7,6},{8,9},{9,8},{10,11... | collective-permute-start | bytes 3158024 | tf_op jit(solution)/shard_map/ppermute | solution.py:153
  15.0 12.2 %all_to_all.20.ends_ref = f32[8,32,128]{2,1,0:T(8,128)S(1)} all-to-all(f32[8,32,128]{2,1,0:T(8,128)S(1)} %get-tuple-element.8), channel_id=1, replica_groups=mesh['y'=8,'z'=8,'x'=4,'c'=2] {'z'}, dimensions={0} | all-to-all | bytes 262144 | tf_op jit(solution)/shard_map/all_to_all | solution.py:151
  27.2 0.7 shard_map.56
  27.9 6.8 %all-to-all-start.1 = ((f32[8,32,128]{2,1,0:T(8,128)}), f32[8,32,128]{2,1,0:T(8,128)S(1)}, u32[]{:S(2)}, u32[]{:S(2)}) async-start(f32[8,32,128]{2,1,0:T(8,128)} %shard_map.56), calls=%async_computation.1 | async-start | bytes 262144 | tf_op jit(solution)/shard_map/all_to_all | solution.py:156
  34.7 0.1 pad_add_fusion.place_ref
  34.8 8.0 %all-to-all-done.1.totals_ref = f32[8,32,128]{2,1,0:T(8,128)S(1)} async-done(((f32[8,32,128]{2,1,0:T(8,128)}), f32[8,32,128]{2,1,0:T(8,128)S(1)}, u32[]{:S(2)}, u32[]{:S(2)}) %all-to-all-start.1) | async-done | bytes 131104 | tf_op jit(solution)/shard_map/all_to_all | solution.py:156
  42.7 1.3 %shard_map.57 = f32[16,32,128]{2,1,0:T(8,128)} custom-call(s32[2]{0:T(128)S(1)} %pad_add_fusion.place_ref, f32[8,32,128]{2,1,0:T(8,128)S(1)} %all_to_all.20.ends_ref, f32[8,32,128]{2,1,0:T(8,128)S(1)} %all-to-all-done.1.totals_ref, s32[1,128]{1,0:T(1,128)S(1)} %bitcast.8), custom_call_target="tpu_custom_call" | custom-call | bytes 1048576 | tf_op jit(solution)/shard_map/pallas_call | solution.py:120
  44.0 6.9 %all-to-all-start.2 = ((f32[16,32,128]{2,1,0:T(8,128)}), f32[16,32,128]{2,1,0:T(8,128)S(1)}, u32[]{:S(2)}, u32[]{:S(2)}) async-start(f32[16,32,128]{2,1,0:T(8,128)} %shard_map.57), calls=%async_computation.2 | async-start | bytes 524288 | tf_op jit(solution)/shard_map/all_to_all | solution.py:158
  51.0 0.0 collective-permute-done.1.other_ref
  51.0 0.1 shard_map.59.w_ref
  51.1 11.6 %all-to-all-done.2 = f32[16,32,128]{2,1,0:T(8,128)S(1)} async-done(((f32[16,32,128]{2,1,0:T(8,128)}), f32[16,32,128]{2,1,0:T(8,128)S(1)}, u32[]{:S(2)}, u32[]{:S(2)}) %all-to-all-start.2) | async-done | bytes 262176 | tf_op jit(solution)/shard_map/all_to_all | solution.py:158
  62.7 0.0 collective-permute-done.other_ref
  62.7 4.2 %shard_map.60 = f32[1024,256]{1,0:T(8,128)} custom-call(s32[2]{0:T(128)S(1)} %pad_add_fusion.place_ref, f32[2056,128]{1,0:T(8,128)} %get-tuple-element.7.own_ref, f32[2056,128]{1,0:T(8,128)} %collective-permute-done.other_ref, f32[8,2,32,128]{3,2,1,0:T(8,128)S(1)} %bitcast.5, bf16[3,3,256,256]{3,2,1,0:T(8,128)(2,1)S(1)} %shard_map.59.w_ref), custom_call_target="tpu_custom_call" | custom-call | flops 1207959552 | bytes 4194304 | tf_op jit(solution)/shard_map/pallas_call | solution.py:120
  66.9 4.0 %all-to-all-start.3 = ((f32[4,8,2,16,256]{4,3,2,1,0:T(8,128)}), f32[4,8,2,16,256]{4,3,2,1,0:T(8,128)S(1)}, u32[]{:S(2)}, u32[]{:S(2)}) async-start(f32[4,8,2,16,256]{4,3,2,1,0:T(8,128)} %bitcast.4), calls=%async_computation.3 | async-start | bytes 2097152 | tf_op jit(solution)/shard_map/all_to_all | solution.py:168
  70.9 15.5 %all-to-all-done.3 = f32[4,8,2,16,256]{4,3,2,1,0:T(8,128)S(1)} async-done(((f32[4,8,2,16,256]{4,3,2,1,0:T(8,128)}), f32[4,8,2,16,256]{4,3,2,1,0:T(8,128)S(1)}, u32[]{:S(2)}, u32[]{:S(2)}) %all-to-all-start.3) | async-done | bytes 1048608 | tf_op jit(solution)/shard_map/all_to_all | solution.py:168
  86.4 0.1 reduce_sum.9
  86.5 2.2 %fusion.2 = bf16[8,2,16,256]{3,2,1,0:T(8,128)(2,1)} fusion(f32[8,2,16,256]{3,2,1,0:T(8,128)S(1)} %reduce_sum.9, bf16[8,16,16,256]{3,2,1,0:T(8,128)(2,1)} %x_ref.1, s32[]{:T(128)S(6)} %select_n.3, f32[256]{0:T(256)S(1)} %copy-done.5), kind=kLoop, calls=%fused_computation.3 | loop fusion | flops 4456448 | bytes 525316 | tf_op jit(solution)/shard_map/convert_element_type | solution.py:171
  (8 shorter events, 0.0 us)
Async XLA Ops:
  0.0 1.1 %copy-start = (bf16[3,3,128,256]{3,2,1,0:T(8,128)(2,1)S(1)}, bf16[3,3,128,256]{3,2,1,0:T(8,128)(2,1)}, u32[]{:S(2)}) copy-start(bf16[3,3,128,256]{3,2,1,0:T(8,128)(2,1)} %own_ref.1) | copy-start | bytes 1769476
  1.1 9.0 %copy-start.2 = (bf16[8,16,16,256]{3,2,1,0:T(8,128)(2,1)S(1)}, bf16[8,16,16,256]{3,2,1,0:T(8,128)(2,1)}, u32[]{:S(2)}) copy-start(bf16[8,16,16,256]{3,2,1,0:T(8,128)(2,1)} %x_ref.1) | copy-start | bytes 3145732
  1.1 9.0 %copy-start.3 = (s32[128]{0:T(128)S(1)}, s32[128]{0:T(128)}, u32[]{:S(2)}) copy-start(s32[128]{0:T(128)} %param.7) | copy-start | bytes 1540
  1.1 9.0 %copy-start.4 = (bf16[3,3,256,128]{3,2,1,0:T(8,128)(2,1)S(1)}, bf16[3,3,256,128]{3,2,1,0:T(8,128)(2,1)}, u32[]{:S(2)}) copy-start(bf16[3,3,256,128]{3,2,1,0:T(8,128)(2,1)} %w_ref.2) | copy-start | bytes 1769476
  1.2 49.8 %collective-permute-start.1 = (f32[3,3,128,256]{3,2,1,0:T(8,128)S(1)}, f32[3,3,128,256]{3,2,1,0:T(8,128)S(1)}, u32[]{:S(2)}, u32[]{:S(2)}) collective-permute-start(f32[3,3,128,256]{3,2,1,0:T(8,128)S(1)} %shard_map.58), channel_id=1, source_target_pairs={{0,1},{1,0},{2,3},{3,2},{4,5},{5,4},{6,7},{7,6},{8,9},{9,8},{10,11... | collective-permute-start | bytes 3538952 | tf_op jit(solution)/shard_map/ppermute | solution.py:152
  12.9 38.1 %copy-start.1 = (bf16[3,3,128,256]{3,2,1,0:T(8,128)(2,1)S(1)}, bf16[3,3,128,256]{3,2,1,0:T(8,128)(2,1)}, u32[]{:S(2)}) copy-start(bf16[3,3,128,256]{3,2,1,0:T(8,128)(2,1)} %own_ref.1) | copy-start | bytes 1769476
  12.9 49.8 %collective-permute-start = (f32[2056,128]{1,0:T(8,128)}, f32[2056,128]{1,0:T(8,128)}, u32[]{:S(2)}, u32[]{:S(2)}) collective-permute-start(f32[2056,128]{1,0:T(8,128)} %get-tuple-element.7.own_ref), channel_id=1, source_target_pairs={{0,1},{1,0},{2,3},{3,2},{4,5},{5,4},{6,7},{7,6},{8,9},{9,8},{10,11... | collective-permute-start | bytes 3158024 | tf_op jit(solution)/shard_map/ppermute | solution.py:153
  27.9 14.8 %all-to-all-start.1 = ((f32[8,32,128]{2,1,0:T(8,128)}), f32[8,32,128]{2,1,0:T(8,128)S(1)}, u32[]{:S(2)}, u32[]{:S(2)}) async-start(f32[8,32,128]{2,1,0:T(8,128)} %shard_map.56), calls=%async_computation.1 | async-start | bytes 262144 | tf_op jit(solution)/shard_map/all_to_all | solution.py:156
  44.0 18.7 %all-to-all-start.2 = ((f32[16,32,128]{2,1,0:T(8,128)}), f32[16,32,128]{2,1,0:T(8,128)S(1)}, u32[]{:S(2)}, u32[]{:S(2)}) async-start(f32[16,32,128]{2,1,0:T(8,128)} %shard_map.57), calls=%async_computation.2 | async-start | bytes 524288 | tf_op jit(solution)/shard_map/all_to_all | solution.py:158
  66.9 19.5 %all-to-all-start.3 = ((f32[4,8,2,16,256]{4,3,2,1,0:T(8,128)}), f32[4,8,2,16,256]{4,3,2,1,0:T(8,128)S(1)}, u32[]{:S(2)}, u32[]{:S(2)}) async-start(f32[4,8,2,16,256]{4,3,2,1,0:T(8,128)} %bitcast.4), calls=%async_computation.3 | async-start | bytes 2097152 | tf_op jit(solution)/shard_map/all_to_all | solution.py:168
  70.9 15.6 %copy-start.5 = (f32[256]{0:T(256)S(1)}, f32[256]{0:T(256)}, u32[]{:S(2)}) copy-start(f32[256]{0:T(256)} %param.9) | copy-start | bytes 3076

commit v2 on v1

--- a/solution.py
+++ b/solution.py
@@ -10,6 +10,9 @@
 SMEM = pl.BlockSpec(memory_space=pltpu.SMEM)
 FRAMES, ROWS, COLS, CIN, PD = 8, 16, 16, 256, 128
 PIX = ROWS * COLS
+DECAY_AT = FRAMES * PIX
+WEIGHT_AT = DECAY_AT + 8
+SHARED = WEIGHT_AT + 18 * PD
 F32, BF16 = jnp.float32, jnp.bfloat16
 
 
@@ -31,7 +34,7 @@
     return from_left + centre + from_right
 
 
-def drive_kernel(x_ref, w_ref, codes_ref, states_ref, end_ref, xpad, wcat):
+def drive_kernel(place_ref, x_ref, w_ref, codes_ref, wout_ref, gain_ref, states_ref, end_ref, skip_ref, xpad, wcat):
     xpad[:, 0] = jnp.zeros((FRAMES, COLS, CIN), BF16)
     xpad[:, ROWS + 1] = jnp.zeros((FRAMES, COLS, CIN), BF16)
     xpad[:, 1 : ROWS + 1] = x_ref[...]
@@ -50,17 +53,35 @@
         for k in range(group):
             running = decay * running + drive[k * PIX : (k + 1) * PIX]
             states_ref[(first + k) * PIX : (first + k + 1) * PIX] = running
-    states_ref[FRAMES * PIX :] = jnp.broadcast_to(decay, (8, PD))
     end_ref[...] = running.reshape(8, PIX // 8, PD)
-
-
-def total_kernel(ends_ref, codes_ref, out_ref):
+    states_ref[DECAY_AT:WEIGHT_AT] = jnp.broadcast_to(decay, (8, PD))
+    for tap in range(9):
+        for half in range(2):
+            at = WEIGHT_AT + (2 * tap + half) * PD
+            states_ref[at : at + PD] = wout_ref[tap // 3, tap % 3, :, half * PD : (half + 1) * PD].astype(F32)
+    own = x_ref[:, pl.ds(place_ref[2], 2)].reshape(FRAMES * 2 * COLS, CIN)
+    skip_ref[...] = own.astype(F32) * gain_ref[...]
+
+
+def total_kernel(ends_ref, codes_ref, wout_ref, other_ref, out_ref, w_ref):
     a8 = pow8(decay_of(codes_ref[...]))
     total = ends_ref[0]
     for z in range(1, 8):
         total = a8 * total + ends_ref[z]
     for y in range(8):
         out_ref[y] = total
+    w_ref[:, :, :PD] = wout_ref[...]
+    for tap in range(9):
+        for half in range(2):
+            at = WEIGHT_AT + (2 * tap + half) * PD
+            w_ref[tap // 3, tap % 3, PD:, half * PD : (half + 1) * PD] = other_ref[at : at + PD].astype(BF16)
+
+
+def mix_kernel(parts_ref, skip_ref, out_ref):
+    value = parts_ref[0] + parts_ref[1] + parts_ref[2] + parts_ref[3] + skip_ref[...]
+    half = 0.5 * value
+    mixed = half + half * lax.erf(value * (0.5**0.5))
+    out_ref[...] = mixed.astype(BF16)
 
 
 def carry_kernel(place_ref, ends_ref, totals_ref, codes_ref, out_ref):
@@ -82,7 +103,7 @@
     spad[:, 0] = zeros
     spad[:, ROWS + 1] = zeros
     for side, (ref, which) in enumerate(((own_ref, core), (other_ref, 1 - core))):
-        decay = ref[FRAMES * PIX : FRAMES * PIX + 1]
+        decay = ref[DECAY_AT : DECAY_AT + 1]
         carry = carry_ref[:, pl.ds(which, 1)].reshape(PIX, PD)
         for j in range(FRAMES):
             carry = decay * carry
@@ -107,15 +128,6 @@
     out_ref[...] = shifted_sum(*taps)
 
 
-def widen_kernel(w_ref, out_ref):
-    out_ref[...] = w_ref[...].astype(F32)
-
-
-def merge_kernel(own_ref, other_ref, out_ref):
-    out_ref[:, :, :PD] = own_ref[...]
-    out_ref[:, :, PD:] = other_ref[...].astype(BF16)
-
-
 def call(kernel, out, args, scratch=(), smem=0, flops=0, moved=1 << 20):
     return pl.pallas_call(
         kernel,
@@ -123,7 +135,7 @@
         in_specs=[SMEM] * smem + [VMEM] * (len(args) - smem),
         out_specs=jax.tree.map(lambda _: VMEM, out),
         scratch_shapes=list(scratch),
-        compiler_params=pltpu.CompilerParams(vmem_limit_bytes=40 << 20),
+        compiler_params=pltpu.CompilerParams(vmem_limit_bytes=24 << 20),
         cost_estimate=pl.CostEstimate(flops=flops, bytes_accessed=moved, transcendentals=0),
     )(*args)
 
@@ -134,41 +146,45 @@
 
 def per_device(frames, in_weight, decay_codes, out_weight, skip_gain):
     codes = decay_codes.reshape(1, PD)
-    place = jnp.stack([lax.axis_index("y"), lax.axis_index("c")]).astype(jnp.int32)
+    y, x, core = lax.axis_index("y"), lax.axis_index("x"), lax.axis_index("c")
+    place = jnp.stack([y, core, 4 * x + 2 * core]).astype(jnp.int32)
     flops = 2 * FRAMES * PIX * 9 * CIN * PD
-    states, end = call(
+    slices = shape(8, PIX // 8, PD)
+    owned = FRAMES * 2 * COLS
+    states, end, skip = call(
         drive_kernel,
-        (shape(FRAMES * PIX + 8, PD), shape(8, PIX // 8, PD)),
-        (frames, in_weight, codes),
+        (shape(SHARED, PD), slices, shape(owned, CIN)),
+        (place, frames, in_weight, codes, out_weight, skip_gain.reshape(1, CIN)),
         scratch=(
             pltpu.VMEM((FRAMES, ROWS + 2, COLS, CIN), BF16),
             pltpu.VMEM((3, CIN, 3 * PD), BF16),
         ),
+        smem=1,
         flops=flops,
         moved=3 << 20,
     )
-    swap = [(0, 1), (1, 0)]
     ends = lax.all_to_all(end, "z", 0, 0, tiled=True)
-    weight_other = lax.ppermute(call(widen_kernel, shape(3, 3, PD, CIN), (out_weight,)), "c", swap)
-    states_other = lax.ppermute(states, "c", swap)
-    weights = call(merge_kernel, shape(3, 3, 2 * PD, CIN, dtype=BF16), (out_weight, weight_other))
-    total = call(total_kernel, shape(8, PIX // 8, PD), (ends, codes))
+    states_other = lax.ppermute(states, "c", [(0, 1), (1, 0)])
+    total, weights = call(
+        total_kernel,
+        (slices, shape(3, 3, 2 * PD, CIN, dtype=BF16)),
+        (ends, codes, out_weight, states_other),
+    )
     totals = lax.all_to_all(total, "y", 0, 0, tiled=True)
     carries = call(carry_kernel, shape(16, PIX // 8, PD), (place, ends, totals, codes), smem=1)
     carry = lax.all_to_all(carries, ("z", "c"), 0, 0, tiled=True).reshape(8, 2, PIX // 8, PD)
     partial_value = call(
         readout_kernel,
-        shape(4 * FRAMES * 2 * COLS, CIN),
+        shape(4 * owned, CIN),
         (place, states, states_other, carry, weights),
         scratch=(pltpu.VMEM((FRAMES, ROWS + 2, COLS, 2 * PD), BF16),),
         smem=1,
         flops=flops,
         moved=4 << 20,
-    ).reshape(4, FRAMES, 2, COLS, CIN)
+    ).reshape(4, owned, CIN)
     arrived = lax.all_to_all(partial_value, "x", 0, 0, tiled=True)
-    start_row = 2 * (2 * lax.axis_index("x") + lax.axis_index("c"))
-    own_frames = lax.dynamic_slice_in_dim(frames, start_row, 2, 1).astype(F32)
-    return jax.nn.gelu(arrived.sum(axis=0) + skip_gain * own_frames, approximate=False).astype(BF16)
+    mixed = call(mix_kernel, shape(owned, CIN, dtype=BF16), (arrived, skip))
+    return mixed.reshape(FRAMES, 2, COLS, CIN)
 
 
 def solution(mesh):

time: 89.2 us -> 84 us (0.942)
  blocking collectives: 12.2 us -> 63.9 us
  waiting for transfers between devices: 35.1 us -> 0.01 us
  starting transfers between devices: 28.7 us -> 8.75 us
  local copies, waits for them, and re-layouts: 1.08 us -> 4.69 us
  Pallas kernels: 9.18 us -> 6.11 us
  other arithmetic: 2.34 us -> 0.08 us
    all_to_all x0 -> x3, blocking collectives: none -> 51 us  [the longest x1 19.3 us: per_device(): arrived = lax.all_to_all(partial_value, 'x', 0, 0, tiled=True)]
    all_to_all x3 -> x0, waiting for transfers between devices: 35 us -> none  [the longest x1 15.5 us: per_device(): arrived = lax.all_to_all(partial_value, 'x', 0, 0, tiled=True)]
    all_to_all x3 -> x0, starting transfers between devices: 17.8 us -> none  [the longest x1 6.93 us: per_device(): lax.all_to_all(carries, ('z', 'c'), 0, 0, tiled=True)]
    unnamed x12, local copies, waits for them, and re-layouts: 1.08 us -> 4.69 us
    pallas_call x6 -> x5, Pallas kernels: 9.18 us -> 6.11 us  [call(): pl.pallas_call(kernel, out_shape=out, in_specs=[SMEM] * smem + [VMEM] * (...]
    ppermute x2 -> x1, starting transfers between devices: 10.9 us -> 8.75 us  [per_device(): states_other = lax.ppermute(states, 'c', [(0, 1), (1, 0)])]
    convert_element_type x1 -> x0, other arithmetic: 2.17 us -> none  [per_device(): jax.nn.gelu(arrived.sum(axis=0) + skip_gain * own_frames, approximate=False)]
  transfers between devices with their start and end apart: 5 -> 1, of which waited for: 3 -> 0; matrix products, arithmetic and copies ran while one was open for 0% -> 0% of each run, Pallas kernels for 6% -> 0%
where the time goes in v2:
time: 84 us; the launch traced here: 83.6 us
  blocking collectives  63.9 us (76%)
  starting transfers between devices  8.75 us (10%)
  Pallas kernels  6.11 us (7%)
  local copies, waits for them, and re-layouts  4.69 us (6%)
    all_to_all x1, blocking collectives, per_device(): arrived = lax.all_to_all(partial_value, 'x', 0, 0, tiled=True)  19.3 us
    all_to_all x1, blocking collectives, per_device(): lax.all_to_all(carries, ('z', 'c'), 0, 0, tiled=True)  17.2 us
    all_to_all x1, blocking collectives, per_device(): totals = lax.all_to_all(total, 'y', 0, 0, tiled=True)  14.5 us
    all_to_all x1, blocking collectives, per_device(): ends = lax.all_to_all(end, 'z', 0, 0, tiled=True)  12.9 us
    ppermute x1, starting transfers between devices, per_device(): states_other = lax.ppermute(states, 'c', [(0, 1), (1, 0)])  8.75 us
    pallas_call x5, Pallas kernels, call(): pl.pallas_call(kernel, out_shape=out, in_specs=[SMEM] * smem + [VMEM] * (...  6.11 us
    unnamed x12, local copies, waits for them, and re-layouts  4.69 us
  transfers between devices with their start and end apart: 1, of which 0 were waited for; matrix products, arithmetic and copies ran while one was open for 0% of the time, Pallas kernels for 0%

profile of v2, /device:TPU:1, one launch (start us, length us, event | category | flops | bytes accessed | tf_op | source)
XLA Modules:
  0.0 83.6 jit_solution(16896209166695947200)
XLA Ops:
  0.0 0.1 pad_add_fusion.place_ref
  0.1 0.0 copy-start
  0.1 1.1 %copy-done = bf16[3,3,128,256]{3,2,1,0:T(8,128)(2,1)S(1)} copy-done((bf16[3,3,128,256]{3,2,1,0:T(8,128)(2,1)S(1)}, bf16[3,3,128,256]{3,2,1,0:T(8,128)(2,1)}, u32[]{:S(2)}) %copy-start) | copy-done | bytes 589848
  1.1 0.0 copy-start.2
  1.1 0.7 copy-done.2
  1.8 0.0 copy-start.3
  1.8 1.2 %copy-done.3 = bf16[8,16,16,256]{3,2,1,0:T(8,128)(2,1)S(1)} copy-done((bf16[8,16,16,256]{3,2,1,0:T(8,128)(2,1)S(1)}, bf16[8,16,16,256]{3,2,1,0:T(8,128)(2,1)}, u32[]{:S(2)}) %copy-start.3) | copy-done | bytes 1048600
  3.0 0.0 copy-start.4
  3.0 1.1 %copy-done.4 = bf16[3,3,256,128]{3,2,1,0:T(8,128)(2,1)S(1)} copy-done((bf16[3,3,256,128]{3,2,1,0:T(8,128)(2,1)S(1)}, bf16[3,3,256,128]{3,2,1,0:T(8,128)(2,1)}, u32[]{:S(2)}) %copy-start.4) | copy-done | bytes 589848
  4.1 0.0 copy-start.5
  4.1 0.7 copy-done.5
  4.8 0.0 copy-start.1
  4.8 2.4 %shard_map.55 = (f32[4360,128]{1,0:T(8,128)S(1)}, f32[8,32,128]{2,1,0:T(8,128)S(1)}, f32[256,256]{1,0:T(8,128)S(1)}) custom-call(s32[3]{0:T(128)S(1)} %pad_add_fusion.place_ref, bf16[8,16,16,256]{3,2,1,0:T(8,128)(2,1)S(1)} %copy-done.3, bf16[3,3,256,128]{3,2,1,0:T(8,128)(2,1)S(1)} %copy-done.4, s32[1,128]{1,0:T(1,128)S(1)} %bitcast.10, ...), custom_call_target="tpu_custom_call" | custom-call | flops 1207959552 | bytes 3145728 | tf_op jit(solution)/shard_map/pallas_call | solution.py:132
  7.2 8.7 %collective-permute-start = (f32[4360,128]{1,0:T(8,128)S(1)}, f32[4360,128]{1,0:T(8,128)S(1)}, u32[]{:S(2)}, u32[]{:S(2)}) collective-permute-start(f32[4360,128]{1,0:T(8,128)S(1)} %get-tuple-element.10.own_ref), channel_id=1, source_target_pairs={{0,1},{1,0},{2,3},{3,2},{4,5},{5,4},{6,7},{7,6},{8,9},{9,8},{10,11... | collective-permute-start | bytes 6696968 | tf_op jit(solution)/shard_map/ppermute | solution.py:167
  16.0 12.9 %all_to_all.20.ends_ref = f32[8,32,128]{2,1,0:T(8,128)S(1)} all-to-all(f32[8,32,128]{2,1,0:T(8,128)S(1)} %get-tuple-element.11), channel_id=1, replica_groups=mesh['y'=8,'z'=8,'x'=4,'c'=2] {'z'}, dimensions={0} | all-to-all | bytes 262144 | tf_op jit(solution)/shard_map/all_to_all | solution.py:166
  28.9 0.0 collective-permute-done.other_ref
  28.9 0.0 copy-done.1
  28.9 0.1 shard_map.56
  29.1 14.5 %all_to_all.21.totals_ref = f32[8,32,128]{2,1,0:T(8,128)S(1)} all-to-all(f32[8,32,128]{2,1,0:T(8,128)S(1)} %get-tuple-element.12), channel_id=1, replica_groups=mesh['y'=8,'z'=8,'x'=4,'c'=2] {'y'}, dimensions={0} | all-to-all | bytes 262144 | tf_op jit(solution)/shard_map/all_to_all | solution.py:173
  43.6 0.6 shard_map.57
  44.2 17.2 %all_to_all.22 = f32[16,32,128]{2,1,0:T(8,128)S(1)} all-to-all(f32[16,32,128]{2,1,0:T(8,128)S(1)} %shard_map.57), channel_id=1, replica_groups=mesh['y'=8,'z'=8,'x'=4,'c'=2] {'z','c'}, dimensions={0} | all-to-all | bytes 524288 | tf_op jit(solution)/shard_map/all_to_all | solution.py:175
  61.4 2.2 %shard_map.58 = f32[1024,256]{1,0:T(8,128)S(1)} custom-call(s32[3]{0:T(128)S(1)} %pad_add_fusion.place_ref, f32[4360,128]{1,0:T(8,128)S(1)} %get-tuple-element.10.own_ref, f32[4360,128]{1,0:T(8,128)S(1)} %collective-permute-done.other_ref, f32[8,2,32,128]{3,2,1,0:T(8,128)S(1)} %bitcast.9, bf16[3,3,256,256]{3,2,1,0:T(8,128)(2,1)S(1)} %get-tuple-element.13.w_ref), custom_call_target="tpu_custom_call" | custom-call | flops 1207959552 | bytes 4194304 | tf_op jit(solution)/shard_map/pallas_call | solution.py:132
  63.6 19.3 %all_to_all.23.parts_ref = f32[4,256,256]{2,1,0:T(8,128)S(1)} all-to-all(f32[4,256,256]{2,1,0:T(8,128)S(1)} %bitcast.8), channel_id=1, replica_groups=mesh['y'=8,'z'=8,'x'=4,'c'=2] {'x'}, dimensions={0} | all-to-all | bytes 2097152 | tf_op jit(solution)/shard_map/all_to_all | solution.py:185
  82.9 0.7 shard_map.59
Async XLA Ops:
  0.1 1.1 %copy-start = (bf16[3,3,128,256]{3,2,1,0:T(8,128)(2,1)S(1)}, bf16[3,3,128,256]{3,2,1,0:T(8,128)(2,1)}, u32[]{:S(2)}) copy-start(bf16[3,3,128,256]{3,2,1,0:T(8,128)(2,1)} %wout_ref.3) | copy-start | bytes 1769476
  1.1 0.7 copy-start.2
  1.8 1.2 %copy-start.3 = (bf16[8,16,16,256]{3,2,1,0:T(8,128)(2,1)S(1)}, bf16[8,16,16,256]{3,2,1,0:T(8,128)(2,1)}, u32[]{:S(2)}) copy-start(bf16[8,16,16,256]{3,2,1,0:T(8,128)(2,1)} %x_ref.1) | copy-start | bytes 3145732
  3.0 1.1 %copy-start.4 = (bf16[3,3,256,128]{3,2,1,0:T(8,128)(2,1)S(1)}, bf16[3,3,256,128]{3,2,1,0:T(8,128)(2,1)}, u32[]{:S(2)}) copy-start(bf16[3,3,256,128]{3,2,1,0:T(8,128)(2,1)} %w_ref.1) | copy-start | bytes 1769476
  4.1 0.7 copy-start.5
  4.8 24.2 %copy-start.1 = (bf16[3,3,128,256]{3,2,1,0:T(8,128)(2,1)S(1)}, bf16[3,3,128,256]{3,2,1,0:T(8,128)(2,1)}, u32[]{:S(2)}) copy-start(bf16[3,3,128,256]{3,2,1,0:T(8,128)(2,1)} %wout_ref.3) | copy-start | bytes 1769476
  7.2 21.7 %collective-permute-start = (f32[4360,128]{1,0:T(8,128)S(1)}, f32[4360,128]{1,0:T(8,128)S(1)}, u32[]{:S(2)}, u32[]{:S(2)}) collective-permute-start(f32[4360,128]{1,0:T(8,128)S(1)} %get-tuple-element.10.own_ref), channel_id=1, source_target_pairs={{0,1},{1,0},{2,3},{3,2},{4,5},{5,4},{6,7},{7,6},{8,9},{9,8},{10,11... | collective-permute-start | bytes 6696968 | tf_op jit(solution)/shard_map/ppermute | solution.py:167

commit v3 on v2

v3 whole, which is shorter than its diff:
```python
import jax
import jax.numpy as jnp
from jax import lax
from jax.experimental import pallas as pl
from jax.experimental.pallas import tpu as pltpu
from jax.sharding import Mesh
from jax.sharding import PartitionSpec as P

FRAMES, ROWS, COLS, CIN, PD = 8, 16, 16, 256, 128
PIX = ROWS * COLS
DECAY_AT = FRAMES * PIX
WEIGHT_AT = DECAY_AT + 8
SHARED = WEIGHT_AT + 18 * PD
F32, BF16 = jnp.float32, jnp.bfloat16


def decay_of(codes):
    return 1.0 - codes.astype(F32) / 4096.0


def pow8(value):
    value = value * value
    value = value * value
    return value * value


def shifted_sum(left, centre, right):
    count = left.shape[0]
    column = lax.broadcasted_iota(jnp.int32, left.shape, 0) % COLS
    from_left = jnp.where(column == 0, 0.0, pltpu.roll(left, 1, 0))
    from_right = jnp.where(column == COLS - 1, 0.0, pltpu.roll(right, count - 1, 0))
    return from_left + centre + from_right


def drive_kernel(place_ref, x_hbm, w_hbm, codes_hbm, wout_hbm, gain_hbm,
                 shared_hbm, end_ref, skip_ref, decay_ref,
                 xpad, wcat, wout, codes, gain, shared, frame_sem, tap_sem, small_sem, out_sem):
    taps = [(di, dj) for di in range(3) for dj in range(3)]
    copies = [
        pltpu.make_async_copy(w_hbm.at[di, dj], wcat.at[di, :, pl.ds(dj * PD, PD)], tap_sem.at[3 * di + dj])
        for di, dj in taps
    ]
    frames = [
        pltpu.make_async_copy(x_hbm.at[j], xpad.at[j, pl.ds(1, ROWS)], frame_sem.at[j]) for j in range(FRAMES)
    ]
    small = [
        pltpu.make_async_copy(src, dst, small_sem.at[i])
        for i, (src, dst) in enumerate(((codes_hbm, codes), (wout_hbm, wout), (gain_hbm, gain)))
    ]
    group = 2
    edges = [*range(0, DECAY_AT, group * PIX), DECAY_AT, SHARED]
    sends = [
        pltpu.make_async_copy(shared.at[pl.ds(at, to - at)], shared_hbm.at[pl.ds(at, to - at)], out_sem.at[i])
        for i, (at, to) in enumerate(zip(edges[:-1], edges[1:], strict=True))
    ]
    for copy in [small[0], *frames[:2], *copies, small[1], *frames[2:], small[2]]:
        copy.start()
    xpad[:, 0] = jnp.zeros((FRAMES, COLS, CIN), BF16)
    xpad[:, ROWS + 1] = jnp.zeros((FRAMES, COLS, CIN), BF16)
    small[0].wait()
    decay = decay_of(codes[...])
    decay_ref[...] = decay
    shared[DECAY_AT:WEIGHT_AT] = jnp.broadcast_to(decay, (8, PD))
    for copy in copies:
        copy.wait()
    running = jnp.zeros((PIX, PD), F32)
    for first in range(0, FRAMES, group):
        total = jnp.zeros((group * PIX, 3 * PD), F32)
        for copy in frames[first : first + group]:
            copy.wait()
        for di in range(3):
            rows = xpad[first : first + group, di : di + ROWS].reshape(group * PIX, CIN)
            total = total + jnp.dot(rows, wcat[di], preferred_element_type=F32)
        drive = shifted_sum(total[:, :PD], total[:, PD : 2 * PD], total[:, 2 * PD :])
        for k in range(group):
            running = decay * running + drive[k * PIX : (k + 1) * PIX]
            shared[(first + k) * PIX : (first + k + 1) * PIX] = running
        sends[first // group].start()
        if first == 0:
            small[1].wait()
            for tap in range(9):
                for half in range(2):
                    at = WEIGHT_AT + (2 * tap + half) * PD
                    shared[at : at + PD] = wout[tap // 3, tap % 3, :, half * PD : (half + 1) * PD].astype(F32)
            sends[-1].start()
    end_ref[...] = running.reshape(8, PIX // 8, PD)
    small[2].wait()
    own = xpad[:, pl.ds(place_ref[2] + 1, 2)].reshape(FRAMES * 2 * COLS, CIN)
    skip_ref[...] = own.astype(F32) * gain[...]
    for copy in sends:
        copy.wait()


def total_kernel(ends_ref, decay_ref, out_ref):
    a8 = pow8(decay_ref[...])
    total = ends_ref[0]
    for z in range(1, 8):
        total = a8 * total + ends_ref[z]
    for y in range(8):
        out_ref[y] = total


def mix_kernel(parts_ref, skip_ref, out_ref):
    value = parts_ref[0] + parts_ref[1] + parts_ref[2] + parts_ref[3] + skip_ref[...]
    half = 0.5 * value
    mixed = half + half * lax.erf(value * (0.5**0.5))
    out_ref[...] = mixed.astype(BF16)


def carry_kernel(place_ref, ends_ref, totals_ref, decay_ref, wout_ref, other_ref, out_ref, w_ref):
    a8 = pow8(decay_ref[...])
    a64 = pow8(a8)
    own = place_ref[0]
    carry = jnp.zeros((PIX // 8, PD), F32)
    for y in range(8):
        carry = jnp.where(y < own, a64 * carry + totals_ref[y], carry)
    for z in range(8):
        out_ref[z] = carry
        carry = a8 * carry + ends_ref[z]
    w_ref[:, :, :PD] = wout_ref[...]
    for tap in range(9):
        for half in range(2):
            at = WEIGHT_AT + (2 * tap + half) * PD
            w_ref[tap // 3, tap % 3, PD:, half * PD : (half + 1) * PD] = other_ref[at : at + PD].astype(BF16)


def readout_kernel(place_ref, own_ref, other_ref, decay_ref, carry_ref, carry_other_ref, w_ref, out_ref, spad):
    core = place_ref[1]
    zeros = jnp.zeros((FRAMES, COLS, 2 * PD), BF16)
    spad[:, 0] = zeros
    spad[:, ROWS + 1] = zeros
    sides = (
        (own_ref, carry_ref, decay_ref[...]),
        (other_ref, carry_other_ref, other_ref[DECAY_AT : DECAY_AT + 1]),
    )
    for side, (ref, carried, decay) in enumerate(sides):
        carry = carried[...].reshape(PIX, PD)
        for j in range(FRAMES):
            carry = decay * carry
            state = ref[j * PIX : (j + 1) * PIX] + carry
            spad[j, 1 : ROWS + 1, :, side * PD : (side + 1) * PD] = state.astype(BF16).reshape(ROWS, COLS, PD)
    taps = []
    rows = [
        jnp.concatenate(
            [
                spad[:, pl.ds(4 * x + 2 * core + di, 2)].reshape(FRAMES * 2 * COLS, 2 * PD)
                for x in range(4)
            ],
            axis=0,
        )
        for di in range(3)
    ]
    for dj in range(3):
        total = jnp.dot(rows[0], w_ref[0, dj], preferred_element_type=F32)
        for di in range(1, 3):
            total = total + jnp.dot(rows[di], w_ref[di, dj], preferred_element_type=F32)
        taps.append(total)
    out_ref[...] = shifted_sum(*taps)


def call(kernel, out, args, spaces=None, scratch=(), flops=0, moved=1 << 20, limit=24, outs=None):
    return pl.pallas_call(
        kernel,
        out_shape=out,
        in_specs=[pl.BlockSpec(memory_space=space) for space in spaces or [pltpu.VMEM] * len(args)],
        out_specs=outs or jax.tree.map(lambda _: pl.BlockSpec(memory_space=pltpu.VMEM), out),
        scratch_shapes=list(scratch),
        compiler_params=pltpu.CompilerParams(vmem_limit_bytes=limit << 20),
        cost_estimate=pl.CostEstimate(flops=flops, bytes_accessed=moved, transcendentals=0),
    )(*args)


def shape(*dims, dtype=F32):
    return jax.ShapeDtypeStruct(dims, dtype)


def per_device(frames, in_weight, decay_codes, out_weight, skip_gain):
    codes = decay_codes.reshape(1, PD)
    y, x, core = lax.axis_index("y"), lax.axis_index("x"), lax.axis_index("c")
    place = jnp.stack([y, core, 4 * x + 2 * core]).astype(jnp.int32)
    flops = 2 * FRAMES * PIX * 9 * CIN * PD
    slices = shape(8, PIX // 8, PD)
    owned = FRAMES * 2 * COLS
    shared, end, skip, decay = call(
        drive_kernel,
        (shape(SHARED, PD), slices, shape(owned, CIN), shape(1, PD)),
        (place, frames, in_weight, codes, out_weight, skip_gain.reshape(1, CIN)),
        spaces=[pltpu.SMEM] + [pltpu.HBM] * 5,
        scratch=(
            pltpu.VMEM((FRAMES, ROWS + 2, COLS, CIN), BF16),
            pltpu.VMEM((3, CIN, 3 * PD), BF16),
            pltpu.VMEM((3, 3, PD, CIN), BF16),
            pltpu.VMEM((1, PD), jnp.int32),
            pltpu.VMEM((1, CIN), F32),
            pltpu.VMEM((SHARED, PD), F32),
            pltpu.SemaphoreType.DMA((FRAMES,)),
            pltpu.SemaphoreType.DMA((9,)),
            pltpu.SemaphoreType.DMA((3,)),
            pltpu.SemaphoreType.DMA((5,)),
        ),
        flops=flops,
        moved=3 << 20,
        limit=59,
        outs=tuple(pl.BlockSpec(memory_space=space) for space in (pltpu.HBM,) + (pltpu.VMEM,) * 3),
    )
    swap = [(0, 1), (1, 0)]
    ends = lax.all_to_all(end, "z", 0, 0, tiled=True)
    other = lax.ppermute(shared, "c", swap)
    total = call(total_kernel, slices, (ends, decay))
    totals = lax.all_to_all(total, "y", 0, 0, tiled=True)
    carries, weights = call(
        carry_kernel,
        (slices, shape(3, 3, 2 * PD, CIN, dtype=BF16)),
        (place, ends, totals, decay, out_weight, other),
        spaces=[pltpu.SMEM] + [pltpu.VMEM] * 5,
    )
    carry = lax.all_to_all(carries, "z", 0, 0, tiled=True)
    carry_other = lax.ppermute(carry, "c", swap)
    partial_value = call(
        readout_kernel,
        shape(4 * owned, CIN),
        (place, shared, other, decay, carry, carry_other, weights),
        spaces=[pltpu.SMEM] + [pltpu.VMEM] * 6,
        scratch=(pltpu.VMEM((FRAMES, ROWS + 2, COLS, 2 * PD), BF16),),
        flops=flops,
        moved=4 << 20,
    ).reshape(4, owned, CIN)
    arrived = lax.all_to_all(partial_value, "x", 0, 0, tiled=True)
    mixed = call(mix_kernel, shape(owned, CIN, dtype=BF16), (arrived, skip))
    return mixed.reshape(FRAMES, 2, COLS, CIN)


def solution(mesh):
    finer = Mesh(mesh.devices.reshape(8, 8, 4, 2), ("y", "z", "x", "c"))
    chan = ("x", "c")
    placed = (
        P(("y", "z"), None, None, None),
        P(None, None, None, chan),
        P(chan),
        P(None, None, chan, None),
        P(),
    )
    return jax.shard_map(
        per_device,
        mesh=finer,
        in_specs=placed,
        out_specs=P(("y", "z"), chan, None, None),
        check_vma=False,
    )
```

time: 84 us -> 84.8 us (level)
  blocking collectives: 63.9 us -> 56.3 us
  starting transfers between devices: 8.75 us -> 14.8 us
  Pallas kernels: 6.11 us -> 10.1 us
  local copies, waits for them, and re-layouts: 4.69 us -> 1.37 us
  waiting for transfers between devices: 0.01 us -> 0.97 us
    all_to_all x1, blocking collectives: 17.2 us -> 10.4 us  [per_device(): carry = lax.all_to_all(carries, 'z', 0, 0, tiled=True)]
    ppermute x1 -> x2, starting transfers between devices: 8.75 us -> 14.8 us  [the longest x1 8.88 us: per_device(): other = lax.ppermute(shared, 'c', swap)]
    pallas_call x5, Pallas kernels: 6.11 us -> 10.1 us  [call(): pl.pallas_call(kernel, out_shape=out, in_specs=[pl.BlockSpec(memory_space...]
    unnamed x12 -> x14, local copies, waits for them, and re-layouts: 4.69 us -> 1.37 us
    all_to_all x1, blocking collectives: 19.3 us -> 18.2 us  [per_device(): arrived = lax.all_to_all(partial_value, 'x', 0, 0, tiled=True)]
    ppermute x1 -> x2, waiting for transfers between devices: 0.01 us -> 0.97 us  [the longest x1 0.96 us: per_device(): carry_other = lax.ppermute(carry, 'c', swap)]
  transfers between devices with their start and end apart: 1 -> 2, of which waited for: 0 -> 1; matrix products, arithmetic and copies ran while one was open for 0% -> 0% of each run, Pallas kernels for 0% -> 0%
where the time goes in v3:
time: 84.8 us; the launch traced here: 84.3 us
  blocking collectives  56.3 us (66%)
  starting transfers between devices  14.8 us (17%)
  Pallas kernels  10.1 us (12%)
  local copies, waits for them, and re-layouts  1.37 us (2%)
  waiting for transfers between devices  0.97 us (1%)
    all_to_all x1, blocking collectives, per_device(): arrived = lax.all_to_all(partial_value, 'x', 0, 0, tiled=True)  18.2 us
    all_to_all x1, blocking collectives, per_device(): totals = lax.all_to_all(total, 'y', 0, 0, tiled=True)  14.5 us
    all_to_all x1, blocking collectives, per_device(): ends = lax.all_to_all(end, 'z', 0, 0, tiled=True)  13.2 us
    all_to_all x1, blocking collectives, per_device(): carry = lax.all_to_all(carries, 'z', 0, 0, tiled=True)  10.4 us
    pallas_call x5, Pallas kernels, call(): pl.pallas_call(kernel, out_shape=out, in_specs=[pl.BlockSpec(memory_space...  10.1 us
    ppermute x1, starting transfers between devices, per_device(): other = lax.ppermute(shared, 'c', swap)  8.88 us
    ppermute x1, starting transfers between devices, per_device(): carry_other = lax.ppermute(carry, 'c', swap)  5.97 us
  transfers between devices with their start and end apart: 2, of which 1 were waited for; matrix products, arithmetic and copies ran while one was open for 0% of the time, Pallas kernels for 0%

profile of v3, /device:TPU:1, one launch (start us, length us, event | category | flops | bytes accessed | tf_op | source)
XLA Modules:
  0.0 84.3 jit_solution(4026658219234562692)
XLA Ops:
  0.0 0.7 pad_add_fusion.place_ref
  0.7 0.0 copy-start.1
  0.7 6.5 %shard_map.55 = (f32[4360,128]{1,0:T(8,128)}, f32[8,32,128]{2,1,0:T(8,128)}, f32[256,256]{1,0:T(8,128)}, f32[1,128]{1,0:T(1,128)}) custom-call(s32[3]{0:T(128)} %pad_add_fusion.place_ref, bf16[8,16,16,256]{3,2,1,0:T(8,128)(2,1)} %x_hbm.1, bf16[3,3,256,128]{3,2,1,0:T(8,128)(2,1)} %w_hbm.1, s32[1,128]{1,0:T(1,128)} %bitcast.9, ...), custom_call_target="tpu_custom_call" | custom-call | flops 1207959552 | bytes 3145728 | tf_op jit(solution)/shard_map/pallas_call | solution.py:162
  7.1 0.0 copy-start
  7.1 8.9 %collective-permute-start = (f32[4360,128]{1,0:T(8,128)}, f32[4360,128]{1,0:T(8,128)S(1)}, u32[]{:S(2)}, u32[]{:S(2)}) collective-permute-start(f32[4360,128]{1,0:T(8,128)} %get-tuple-element.11.own_ref), channel_id=1, source_target_pairs={{0,1},{1,0},{2,3},{3,2},{4,5},{5,4},{6,7},{7,6},{8,9},{9,8},{10,11... | collective-permute-start | bytes 6696968 | tf_op jit(solution)/shard_map/ppermute | solution.py:208
  16.0 13.2 %all_to_all.20.ends_ref = f32[8,32,128]{2,1,0:T(8,128)S(1)} all-to-all(f32[8,32,128]{2,1,0:T(8,128)} %get-tuple-element.13), channel_id=1, replica_groups=mesh['y'=8,'z'=8,'x'=4,'c'=2] {'z'}, dimensions={0} | all-to-all | bytes 262144 | tf_op jit(solution)/shard_map/all_to_all | solution.py:207
  29.2 0.7 copy-done.3
  29.9 14.5 %all_to_all.21.totals_ref = f32[8,32,128]{2,1,0:T(8,128)S(1)} all-to-all(f32[8,32,128]{2,1,0:T(8,128)S(1)} %shard_map.56), channel_id=1, replica_groups=mesh['y'=8,'z'=8,'x'=4,'c'=2] {'y'}, dimensions={0} | all-to-all | bytes 262144 | tf_op jit(solution)/shard_map/all_to_all | solution.py:210
  44.5 0.0 collective-permute-done.other_ref
  44.5 0.0 copy-done.1
  44.5 0.0 copy-done.6
  44.5 0.0 copy-start.4
  44.5 0.7 copy-done.4
  45.1 0.7 shard_map.57
  45.8 10.4 %all_to_all.22.carry_ref = f32[8,32,128]{2,1,0:T(8,128)S(1)} all-to-all(f32[8,32,128]{2,1,0:T(8,128)S(1)} %get-tuple-element.14), channel_id=1, replica_groups=mesh['y'=8,'z'=8,'x'=4,'c'=2] {'z'}, dimensions={0} | all-to-all | bytes 262144 | tf_op jit(solution)/shard_map/all_to_all | solution.py:217
  56.2 6.0 %collective-permute-start.1 = (f32[8,32,128]{2,1,0:T(8,128)S(1)}, f32[8,32,128]{2,1,0:T(8,128)S(1)}, u32[]{:S(2)}, u32[]{:S(2)}) collective-permute-start(f32[8,32,128]{2,1,0:T(8,128)S(1)} %all_to_all.22.carry_ref), channel_id=1, source_target_pairs={{0,1},{1,0},{2,3},{3,2},{4,5},{5,4},{6,7},{7,6},{8,9},{9,8},{10,11... | collective-permute-start | bytes 393224 | tf_op jit(solution)/shard_map/ppermute | solution.py:218
  62.2 1.0 %collective-permute-done.1.carry_other_ref = f32[8,32,128]{2,1,0:T(8,128)S(1)} collective-permute-done((f32[8,32,128]{2,1,0:T(8,128)S(1)}, f32[8,32,128]{2,1,0:T(8,128)S(1)}, u32[]{:S(2)}, u32[]{:S(2)}) %collective-permute-start.1) | collective-permute-done | bytes 131104 | tf_op jit(solution)/shard_map/ppermute | solution.py:218
  63.1 0.0 copy-done
  63.2 0.0 copy-done.5
  63.2 2.2 %shard_map.58 = f32[1024,256]{1,0:T(8,128)S(1)} custom-call(s32[3]{0:T(128)S(1)} %copy-done.6, f32[4360,128]{1,0:T(8,128)S(1)} %copy-done, f32[4360,128]{1,0:T(8,128)S(1)} %collective-permute-done.other_ref, f32[1,128]{1,0:T(1,128)S(1)} %copy-done.5, f32[8,32,128]{2,1,0:T(8,128)S(1)} %all_to_all.22.carry_ref, ...), custom_call_target="tpu_custom_call" | custom-call | flops 1207959552 | bytes 4194304 | tf_op jit(solution)/shard_map/pallas_call | solution.py:162
  65.4 0.0 copy-start.2
  65.4 18.2 %all_to_all.23.parts_ref = f32[4,256,256]{2,1,0:T(8,128)S(1)} all-to-all(f32[4,256,256]{2,1,0:T(8,128)S(1)} %bitcast.7), channel_id=1, replica_groups=mesh['y'=8,'z'=8,'x'=4,'c'=2] {'x'}, dimensions={0} | all-to-all | bytes 2097152 | tf_op jit(solution)/shard_map/all_to_all | solution.py:228
  83.6 0.0 copy-done.2
  83.6 0.7 shard_map.59
  (4 shorter events, 0.0 us)
Async XLA Ops:
  0.7 43.8 %copy-start.1 = (bf16[3,3,128,256]{3,2,1,0:T(8,128)(2,1)S(1)}, bf16[3,3,128,256]{3,2,1,0:T(8,128)(2,1)}, u32[]{:S(2)}) copy-start(bf16[3,3,128,256]{3,2,1,0:T(8,128)(2,1)} %wout_ref.1) | copy-start | bytes 1769476
  0.7 43.8 %copy-start.6 = (s32[3]{0:T(128)S(1)}, s32[3]{0:T(128)}, u32[]{:S(2)}) copy-start(s32[3]{0:T(128)} %pad_add_fusion.place_ref) | copy-start | bytes 40
  7.1 56.0 %copy-start = (f32[4360,128]{1,0:T(8,128)S(1)}, f32[4360,128]{1,0:T(8,128)}, u32[]{:S(2)}) copy-start(f32[4360,128]{1,0:T(8,128)} %get-tuple-element.11.own_ref) | copy-start | bytes 6696964
  7.1 37.3 %collective-permute-start = (f32[4360,128]{1,0:T(8,128)}, f32[4360,128]{1,0:T(8,128)S(1)}, u32[]{:S(2)}, u32[]{:S(2)}) collective-permute-start(f32[4360,128]{1,0:T(8,128)} %get-tuple-element.11.own_ref), channel_id=1, source_target_pairs={{0,1},{1,0},{2,3},{3,2},{4,5},{5,4},{6,7},{7,6},{8,9},{9,8},{10,11... | collective-permute-start | bytes 6696968 | tf_op jit(solution)/shard_map/ppermute | solution.py:208
  29.2 0.7 copy-start.3
  44.5 0.7 copy-start.4
  45.1 18.0 %copy-start.5 = (f32[1,128]{1,0:T(1,128)S(1)}, f32[1,128]{1,0:T(1,128)}, u32[]{:S(2)}) copy-start(f32[1,128]{1,0:T(1,128)} %get-tuple-element.12.decay_ref) | copy-start | bytes 1540
  56.2 6.9 %collective-permute-start.1 = (f32[8,32,128]{2,1,0:T(8,128)S(1)}, f32[8,32,128]{2,1,0:T(8,128)S(1)}, u32[]{:S(2)}, u32[]{:S(2)}) collective-permute-start(f32[8,32,128]{2,1,0:T(8,128)S(1)} %all_to_all.22.carry_ref), channel_id=1, source_target_pairs={{0,1},{1,0},{2,3},{3,2},{4,5},{5,4},{6,7},{7,6},{8,9},{9,8},{10,11... | collective-permute-start | bytes 393224 | tf_op jit(solution)/shard_map/ppermute | solution.py:218
  65.4 18.2 %copy-start.2 = (f32[256,256]{1,0:T(8,128)S(1)}, f32[256,256]{1,0:T(8,128)}, u32[]{:S(2)}) copy-start(f32[256,256]{1,0:T(8,128)} %get-tuple-element.16.skip_ref) | copy-start | bytes 786436

commit v4 on v3

v4 whole, which is shorter than its diff:
```python
import functools


import jax
import jax.numpy as jnp
from jax import lax
from jax.experimental import pallas as pl
from jax.experimental.pallas import tpu as pltpu
from jax.sharding import Mesh
from jax.sharding import PartitionSpec as P

FRAMES, ROWS, COLS, CIN, PD = 8, 16, 16, 256, 128
PIX = ROWS * COLS
DECAY_AT = FRAMES * PIX
WEIGHT_AT = DECAY_AT + 8
SHARED = WEIGHT_AT + 18 * PD
F32, BF16 = jnp.float32, jnp.bfloat16


def decay_of(codes):
    return 1.0 - codes.astype(F32) / 4096.0


def pow8(value):
    value = value * value
    value = value * value
    return value * value


def shifted_sum(left, centre, right):
    count = left.shape[0]
    column = lax.broadcasted_iota(jnp.int32, left.shape, 0) % COLS
    from_left = jnp.where(column == 0, 0.0, pltpu.roll(left, 1, 0))
    from_right = jnp.where(column == COLS - 1, 0.0, pltpu.roll(right, count - 1, 0))
    return from_left + centre + from_right


def drive_kernel(x_hbm, w_hbm, codes_hbm, wout_hbm, shared_hbm, end_ref,
                 xpad, wcat, wout, codes, shared, frame_sem, tap_sem, small_sem, out_sem):
    taps = [(di, dj) for di in range(3) for dj in range(3)]
    copies = [
        pltpu.make_async_copy(w_hbm.at[di, dj], wcat.at[di, :, pl.ds(dj * PD, PD)], tap_sem.at[3 * di + dj])
        for di, dj in taps
    ]
    frames = [
        pltpu.make_async_copy(x_hbm.at[j], xpad.at[j, pl.ds(1, ROWS)], frame_sem.at[j]) for j in range(FRAMES)
    ]
    small = [
        pltpu.make_async_copy(src, dst, small_sem.at[i])
        for i, (src, dst) in enumerate(((codes_hbm, codes), (wout_hbm, wout)))
    ]
    group = 2
    edges = [*range(0, DECAY_AT, group * PIX), DECAY_AT, SHARED]
    sends = [
        pltpu.make_async_copy(shared.at[pl.ds(at, to - at)], shared_hbm.at[pl.ds(at, to - at)], out_sem.at[i])
        for i, (at, to) in enumerate(zip(edges[:-1], edges[1:], strict=True))
    ]
    for copy in [small[0], *frames[:2], *copies, small[1], *frames[2:]]:
        copy.start()
    xpad[:, 0] = jnp.zeros((FRAMES, COLS, CIN), BF16)
    xpad[:, ROWS + 1] = jnp.zeros((FRAMES, COLS, CIN), BF16)
    small[0].wait()
    decay = decay_of(codes[...])
    shared[DECAY_AT:WEIGHT_AT] = jnp.broadcast_to(decay, (8, PD))
    for copy in copies:
        copy.wait()
    running = jnp.zeros((PIX, PD), F32)
    for first in range(0, FRAMES, group):
        total = jnp.zeros((group * PIX, 3 * PD), F32)
        for copy in frames[first : first + group]:
            copy.wait()
        for di in range(3):
            rows = xpad[first : first + group, di : di + ROWS].reshape(group * PIX, CIN)
            total = total + jnp.dot(rows, wcat[di], preferred_element_type=F32)
        drive = shifted_sum(total[:, :PD], total[:, PD : 2 * PD], total[:, 2 * PD :])
        for k in range(group):
            running = decay * running + drive[k * PIX : (k + 1) * PIX]
            shared[(first + k) * PIX : (first + k + 1) * PIX] = running
        sends[first // group].start()
        if first == 0:
            small[1].wait()
            for tap in range(9):
                for half in range(2):
                    at = WEIGHT_AT + (2 * tap + half) * PD
                    shared[at : at + PD] = wout[tap // 3, tap % 3, :, half * PD : (half + 1) * PD].astype(F32)
            sends[-1].start()
    end_ref[...] = running.reshape(8, PIX // 8, PD)
    for copy in sends:
        copy.wait()


def total_kernel(ends_ref, codes_ref, out_ref):
    a8 = pow8(decay_of(codes_ref[...]))
    total = ends_ref[0]
    for z in range(1, 8):
        total = a8 * total + ends_ref[z]
    for y in range(8):
        out_ref[y] = total


def mix_kernel(own_ref, first_ref, second_ref, third_ref, out_ref):
    value = own_ref[...] + first_ref[...] + second_ref[...] + third_ref[...]
    half = 0.5 * value
    mixed = half + half * lax.erf(value * (0.5**0.5))
    out_ref[...] = mixed.astype(BF16)


def carry_kernel(ends_ref, totals_ref, codes_ref, wout_ref, other_ref, out_ref, w_ref):
    a8 = pow8(decay_of(codes_ref[...]))
    a64 = pow8(a8)
    own = lax.axis_index("y")
    carry = jnp.zeros((PIX // 8, PD), F32)
    for y in range(8):
        carry = jnp.where(y < own, a64 * carry + totals_ref[y], carry)
    for z in range(8):
        out_ref[z] = carry
        carry = a8 * carry + ends_ref[z]
    w_ref[:, :, :PD] = wout_ref[...]
    for tap in range(9):
        for half in range(2):
            at = WEIGHT_AT + (2 * tap + half) * PD
            w_ref[tap // 3, tap % 3, PD:, half * PD : (half + 1) * PD] = other_ref[at : at + PD].astype(BF16)


def readout(offset, own_ref, other_ref, codes_ref, carry_ref, carry_other_ref, w_ref, spad):
    chip = (lax.axis_index("x") + offset) % 4
    above = 4 * chip + 2 * lax.axis_index("c") - 1
    sides = (
        (own_ref, carry_ref, decay_of(codes_ref[...])),
        (other_ref, carry_other_ref, other_ref[DECAY_AT : DECAY_AT + 1]),
    )
    for row in range(4):
        inside = jnp.logical_and(above + row >= 0, above + row < ROWS)
        at = jnp.clip(above + row, 0, ROWS - 1)
        for side, (ref, carried, decay) in enumerate(sides):
            half = pl.ds(pl.multiple_of(at % 2 * COLS, COLS), COLS)
            carry = jnp.where(inside, carried[at // 2, half], 0.0)
            for j in range(FRAMES):
                carry = decay * carry
                state = ref[pl.ds(pl.multiple_of(at * COLS + j * PIX, COLS), COLS)]
                state = jnp.where(inside, state, 0.0) + carry
                spad[j, row, :, side * PD : (side + 1) * PD] = state.astype(BF16)
    rows = [spad[:, di : di + 2].reshape(FRAMES * 2 * COLS, 2 * PD) for di in range(3)]
    taps = []
    for dj in range(3):
        total = jnp.dot(rows[0], w_ref[0, dj], preferred_element_type=F32)
        for di in range(1, 3):
            total = total + jnp.dot(rows[di], w_ref[di, dj], preferred_element_type=F32)
        taps.append(total)
    return shifted_sum(*taps)


def far_kernel(offset, own_ref, other_ref, codes_ref, carry_ref, carry_other_ref, w_ref, after_ref, out_ref, spad):
    out_ref[...] = readout(offset, own_ref, other_ref, codes_ref, carry_ref, carry_other_ref, w_ref, spad)


def near_kernel(own_ref, other_ref, codes_ref, carry_ref, carry_other_ref, w_ref, after_ref, x_hbm, gain_ref,
                out_ref, spad, frames, sem):
    start = 4 * lax.axis_index("x") + 2 * lax.axis_index("c")
    copy = pltpu.make_async_copy(x_hbm.at[:, pl.ds(start, 2)], frames, sem)
    copy.start()
    value = readout(0, own_ref, other_ref, codes_ref, carry_ref, carry_other_ref, w_ref, spad)
    copy.wait()
    out_ref[...] = value + frames[...].reshape(FRAMES * 2 * COLS, CIN).astype(F32) * gain_ref[...]


def call(kernel, out, args, spaces=None, scratch=(), flops=0, moved=1 << 20, limit=24, outs=None):
    return pl.pallas_call(
        kernel,
        out_shape=out,
        in_specs=[pl.BlockSpec(memory_space=space) for space in spaces or [pltpu.VMEM] * len(args)],
        out_specs=outs or jax.tree.map(lambda _: pl.BlockSpec(memory_space=pltpu.VMEM), out),
        scratch_shapes=list(scratch),
        compiler_params=pltpu.CompilerParams(vmem_limit_bytes=limit << 20),
        cost_estimate=pl.CostEstimate(flops=flops, bytes_accessed=moved, transcendentals=0),
    )(*args)


def shape(*dims, dtype=F32):
    return jax.ShapeDtypeStruct(dims, dtype)


def per_device(frames, in_weight, decay_codes, out_weight, skip_gain):
    codes = decay_codes.reshape(1, PD)
    flops = 2 * FRAMES * PIX * 9 * CIN * PD
    slices = shape(8, PIX // 8, PD)
    owned = FRAMES * 2 * COLS
    shared, end = call(
        drive_kernel,
        (shape(SHARED, PD), slices),
        (frames, in_weight, codes, out_weight),
        spaces=[pltpu.HBM] * 4,
        scratch=(
            pltpu.VMEM((FRAMES, ROWS + 2, COLS, CIN), BF16),
            pltpu.VMEM((3, CIN, 3 * PD), BF16),
            pltpu.VMEM((3, 3, PD, CIN), BF16),
            pltpu.VMEM((1, PD), jnp.int32),
            pltpu.VMEM((SHARED, PD), F32),
            pltpu.SemaphoreType.DMA((FRAMES,)),
            pltpu.SemaphoreType.DMA((9,)),
            pltpu.SemaphoreType.DMA((2,)),
            pltpu.SemaphoreType.DMA((5,)),
        ),
        flops=flops,
        moved=3 << 20,
        limit=59,
        outs=tuple(pl.BlockSpec(memory_space=space) for space in (pltpu.HBM, pltpu.VMEM)),
    )
    swap = [(0, 1), (1, 0)]
    ends = lax.all_to_all(end, "z", 0, 0, tiled=True)
    other = lax.ppermute(shared, "c", swap)
    total = call(total_kernel, slices, (ends, codes))
    totals = lax.all_to_all(total, "y", 0, 0, tiled=True)
    carries, weights = call(
        carry_kernel,
        (slices, shape(3, 3, 2 * PD, CIN, dtype=BF16)),
        (ends, totals, codes, out_weight, other),
    )
    carry = lax.all_to_all(carries, "z", 0, 0, tiled=True)
    carry_other = lax.ppermute(carry, "c", swap)
    inputs = (shared, other, codes, carry, carry_other, weights)
    padded = pltpu.VMEM((FRAMES, 4, COLS, 2 * PD), BF16)
    piece, arrived = carry_other, []
    for offset in (2, 1, 3):
        piece = call(
            functools.partial(far_kernel, offset),
            shape(owned, CIN),
            (*inputs, piece),
            spaces=[pltpu.VMEM] * 6 + [pl.ANY],
            scratch=(padded,),
            flops=flops // 4,
        )
        arrived.append(lax.ppermute(piece, "x", [(i, (i + offset) % 4) for i in range(4)]))
    own = call(
        near_kernel,
        shape(owned, CIN),
        (*inputs, piece, frames, skip_gain.reshape(1, CIN)),
        spaces=[pltpu.VMEM] * 6 + [pl.ANY, pltpu.HBM, pltpu.VMEM],
        scratch=(padded, pltpu.VMEM((FRAMES, 2, COLS, CIN), BF16), pltpu.SemaphoreType.DMA),
        flops=flops // 4,
    )
    mixed = call(mix_kernel, shape(owned, CIN, dtype=BF16), (own, *arrived))
    return mixed.reshape(FRAMES, 2, COLS, CIN)


def solution(mesh):
    finer = Mesh(mesh.devices.reshape(8, 8, 4, 2), ("y", "z", "x", "c"))
    chan = ("x", "c")
    placed = (
        P(("y", "z"), None, None, None),
        P(None, None, None, chan),
        P(chan),
        P(None, None, chan, None),
        P(),
    )
    return jax.shard_map(
        per_device,
        mesh=finer,
        in_specs=placed,
        out_specs=P(("y", "z"), chan, None, None),
        check_vma=False,
    )
```

time: 84.8 us -> 81.9 us (0.966)
  blocking collectives: 56.3 us -> 38.1 us
  starting transfers between devices: 14.8 us -> 24.8 us
  waiting for transfers between devices: 0.97 us -> 9.78 us
  Pallas kernels: 10.1 us -> 8.65 us
  local copies, waits for them, and re-layouts: 1.37 us -> 0.02 us
    all_to_all x1 -> x0, blocking collectives: 18.2 us -> none  [per_device(): arrived = lax.all_to_all(partial_value, 'x', 0, 0, tiled=True)]
    ppermute x0 -> x3, starting transfers between devices: none -> 9.93 us  [per_device(): lax.ppermute(piece, 'x', [(i, (i + offset) % 4) for i in range(4)])]
    ppermute x0 -> x3, waiting for transfers between devices: none -> 8.82 us  [per_device(): lax.ppermute(piece, 'x', [(i, (i + offset) % 4) for i in range(4)])]
    pallas_call x5 -> x8, Pallas kernels: 10.1 us -> 8.65 us  [call(): pl.pallas_call(kernel, out_shape=out, in_specs=[pl.BlockSpec(memory_space...]
    unnamed x14 -> x10, local copies, waits for them, and re-layouts: 1.37 us -> 0.02 us
  transfers between devices with their start and end apart: 2 -> 5, of which waited for: 1 -> 3; matrix products, arithmetic and copies ran while one was open for 0% -> 0% of each run, Pallas kernels for 0% -> 1%
where the time goes in v4:
time: 81.9 us; the launch traced here: 81.5 us
  blocking collectives  38.1 us (47%)
  starting transfers between devices  24.8 us (30%)
  waiting for transfers between devices  9.78 us (12%)
  Pallas kernels  8.65 us (11%)
    all_to_all x1, blocking collectives, per_device(): totals = lax.all_to_all(total, 'y', 0, 0, tiled=True)  14.5 us
    all_to_all x1, blocking collectives, per_device(): ends = lax.all_to_all(end, 'z', 0, 0, tiled=True)  13.2 us
    all_to_all x1, blocking collectives, per_device(): carry = lax.all_to_all(carries, 'z', 0, 0, tiled=True)  10.4 us
    ppermute x3, starting transfers between devices, per_device(): lax.ppermute(piece, 'x', [(i, (i + offset) % 4) for i in range(4)])  9.93 us
    ppermute x1, starting transfers between devices, per_device(): other = lax.ppermute(shared, 'c', swap)  8.87 us
    ppermute x3, waiting for transfers between devices, per_device(): lax.ppermute(piece, 'x', [(i, (i + offset) % 4) for i in range(4)])  8.82 us
    pallas_call x8, Pallas kernels, call(): pl.pallas_call(kernel, out_shape=out, in_specs=[pl.BlockSpec(memory_space...  8.65 us
    ppermute x1, starting transfers between devices, per_device(): carry_other = lax.ppermute(carry, 'c', swap)  5.97 us
  transfers between devices with their start and end apart: 5, of which 3 were waited for; matrix products, arithmetic and copies ran while one was open for 0% of the time, Pallas kernels for 1%

profile of v4, /device:TPU:1, one launch (start us, length us, event | category | flops | bytes accessed | tf_op | source)
XLA Modules:
  0.0 81.5 jit_solution(13772201419742197841)
XLA Ops:
  0.0 5.5 %shard_map.55 = (f32[4360,128]{1,0:T(8,128)}, f32[8,32,128]{2,1,0:T(8,128)}) custom-call(bf16[8,16,16,256]{3,2,1,0:T(8,128)(2,1)} %x_hbm.3, bf16[3,3,256,128]{3,2,1,0:T(8,128)(2,1)} %w_hbm.1, s32[1,128]{1,0:T(1,128)} %bitcast.3, bf16[3,3,128,256]{3,2,1,0:T(8,128)(2,1)} %wout_ref.1), custom_call_target="tpu_custom_call" | custom-call | flops 1207959552 | bytes 3145728 | tf_op jit(solution)/shard_map/pallas_call | solution.py:168
  5.5 0.0 copy-start
  5.5 8.9 %collective-permute-start = (f32[4360,128]{1,0:T(8,128)}, f32[4360,128]{1,0:T(8,128)S(1)}, u32[]{:S(2)}, u32[]{:S(2)}) collective-permute-start(f32[4360,128]{1,0:T(8,128)} %get-tuple-element.9.own_ref), channel_id=1, source_target_pairs={{0,1},{1,0},{2,3},{3,2},{4,5},{5,4},{6,7},{7,6},{8,9},{9,8},{10,11... | collective-permute-start | bytes 6696968 | tf_op jit(solution)/shard_map/ppermute | solution.py:211
  14.4 13.2 %all_to_all.15.ends_ref = f32[8,32,128]{2,1,0:T(8,128)S(1)} all-to-all(f32[8,32,128]{2,1,0:T(8,128)} %get-tuple-element.10), channel_id=1, replica_groups=mesh['y'=8,'z'=8,'x'=4,'c'=2] {'z'}, dimensions={0} | all-to-all | bytes 262144 | tf_op jit(solution)/shard_map/all_to_all | solution.py:210
  27.6 14.5 %all_to_all.16.totals_ref = f32[8,32,128]{2,1,0:T(8,128)S(1)} all-to-all(f32[8,32,128]{2,1,0:T(8,128)S(1)} %shard_map.56), channel_id=1, replica_groups=mesh['y'=8,'z'=8,'x'=4,'c'=2] {'y'}, dimensions={0} | all-to-all | bytes 262144 | tf_op jit(solution)/shard_map/all_to_all | solution.py:213
  42.1 0.0 collective-permute-done.other_ref
  42.1 0.0 copy-done.2
  42.1 0.1 shard_map.57
  42.3 10.4 %all_to_all.17.carry_ref = f32[8,32,128]{2,1,0:T(8,128)S(1)} all-to-all(f32[8,32,128]{2,1,0:T(8,128)S(1)} %get-tuple-element.11), channel_id=1, replica_groups=mesh['y'=8,'z'=8,'x'=4,'c'=2] {'z'}, dimensions={0} | all-to-all | bytes 262144 | tf_op jit(solution)/shard_map/all_to_all | solution.py:219
  52.6 6.0 %collective-permute-start.1 = (f32[8,32,128]{2,1,0:T(8,128)S(1)}, f32[8,32,128]{2,1,0:T(8,128)S(1)}, u32[]{:S(2)}, u32[]{:S(2)}) collective-permute-start(f32[8,32,128]{2,1,0:T(8,128)S(1)} %all_to_all.17.carry_ref), channel_id=1, source_target_pairs={{0,1},{1,0},{2,3},{3,2},{4,5},{5,4},{6,7},{7,6},{8,9},{9,8},{10,11... | collective-permute-start | bytes 393224 | tf_op jit(solution)/shard_map/ppermute | solution.py:220
  58.6 1.0 %collective-permute-done.1.carry_other_ref.after_ref = f32[8,32,128]{2,1,0:T(8,128)S(1)} collective-permute-done((f32[8,32,128]{2,1,0:T(8,128)S(1)}, f32[8,32,128]{2,1,0:T(8,128)S(1)}, u32[]{:S(2)}, u32[]{:S(2)}) %collective-permute-start.1) | collective-permute-done | bytes 131104 | tf_op jit(solution)/shard_map/ppermute | solution.py:220
  59.6 0.5 shard_map.58.after_ref
  60.1 0.6 shard_map.59.after_ref
  60.7 0.0 copy-start.1
  60.7 0.0 copy-start.4
  60.7 0.6 shard_map.60.after_ref
  61.3 4.4 %collective-permute-start.4 = (f32[256,256]{1,0:T(8,128)S(1)}, f32[256,256]{1,0:T(8,128)S(1)}, u32[]{:S(2)}, u32[]{:S(2)}) collective-permute-start(f32[256,256]{1,0:T(8,128)S(1)} %shard_map.60.after_ref), channel_id=1, source_target_pairs={{0,6},{2,0},{4,2},{6,4},{1,7},{3,1},{5,3},{7,5},{8,14},{10,8},{12,... | collective-permute-start | bytes 786440 | tf_op jit(solution)/shard_map/ppermute | solution.py:233
  65.7 1.9 %collective-permute-start.3 = (f32[256,256]{1,0:T(8,128)S(1)}, f32[256,256]{1,0:T(8,128)S(1)}, u32[]{:S(2)}, u32[]{:S(2)}) collective-permute-start(f32[256,256]{1,0:T(8,128)S(1)} %shard_map.59.after_ref), channel_id=1, source_target_pairs={{0,2},{2,4},{4,6},{6,0},{1,3},{3,5},{5,7},{7,1},{8,10},{10,12},{12... | collective-permute-start | bytes 786440 | tf_op jit(solution)/shard_map/ppermute | solution.py:233
  67.6 3.6 %collective-permute-start.2 = (f32[256,256]{1,0:T(8,128)S(1)}, f32[256,256]{1,0:T(8,128)S(1)}, u32[]{:S(2)}, u32[]{:S(2)}) collective-permute-start(f32[256,256]{1,0:T(8,128)S(1)} %shard_map.58.after_ref), channel_id=1, source_target_pairs={{0,4},{2,6},{4,0},{6,2},{1,5},{3,7},{5,1},{7,3},{8,12},{10,14},{12... | collective-permute-start | bytes 786440 | tf_op jit(solution)/shard_map/ppermute | solution.py:233
  71.3 0.6 shard_map.61.own_ref
  71.9 0.0 collective-permute-done.4.third_ref
  71.9 5.1 %collective-permute-done.3.second_ref = f32[256,256]{1,0:T(8,128)S(1)} collective-permute-done((f32[256,256]{1,0:T(8,128)S(1)}, f32[256,256]{1,0:T(8,128)S(1)}, u32[]{:S(2)}, u32[]{:S(2)}) %collective-permute-start.3) | collective-permute-done | bytes 262176 | tf_op jit(solution)/shard_map/ppermute | solution.py:233
  77.0 3.8 %collective-permute-done.2.first_ref = f32[256,256]{1,0:T(8,128)S(1)} collective-permute-done((f32[256,256]{1,0:T(8,128)S(1)}, f32[256,256]{1,0:T(8,128)S(1)}, u32[]{:S(2)}, u32[]{:S(2)}) %collective-permute-start.2) | collective-permute-done | bytes 262176 | tf_op jit(solution)/shard_map/ppermute | solution.py:233
  80.7 0.7 shard_map.62
  (7 shorter events, 0.0 us)
Async XLA Ops:
  0.0 27.5 %copy-start.3 = (s32[128]{0:T(128)S(1)}, s32[128]{0:T(128)}, u32[]{:S(2)}) copy-start(s32[128]{0:T(128)} %param.7) | copy-start | bytes 1540
  0.0 42.1 %copy-start.2 = (bf16[3,3,128,256]{3,2,1,0:T(8,128)(2,1)S(1)}, bf16[3,3,128,256]{3,2,1,0:T(8,128)(2,1)}, u32[]{:S(2)}) copy-start(bf16[3,3,128,256]{3,2,1,0:T(8,128)(2,1)} %wout_ref.1) | copy-start | bytes 1769476
  5.5 54.1 %copy-start = (f32[4360,128]{1,0:T(8,128)S(1)}, f32[4360,128]{1,0:T(8,128)}, u32[]{:S(2)}) copy-start(f32[4360,128]{1,0:T(8,128)} %get-tuple-element.9.own_ref) | copy-start | bytes 6696964
  5.5 36.6 %collective-permute-start = (f32[4360,128]{1,0:T(8,128)}, f32[4360,128]{1,0:T(8,128)S(1)}, u32[]{:S(2)}, u32[]{:S(2)}) collective-permute-start(f32[4360,128]{1,0:T(8,128)} %get-tuple-element.9.own_ref), channel_id=1, source_target_pairs={{0,1},{1,0},{2,3},{3,2},{4,5},{5,4},{6,7},{7,6},{8,9},{9,8},{10,11... | collective-permute-start | bytes 6696968 | tf_op jit(solution)/shard_map/ppermute | solution.py:211
  52.6 6.9 %collective-permute-start.1 = (f32[8,32,128]{2,1,0:T(8,128)S(1)}, f32[8,32,128]{2,1,0:T(8,128)S(1)}, u32[]{:S(2)}, u32[]{:S(2)}) collective-permute-start(f32[8,32,128]{2,1,0:T(8,128)S(1)} %all_to_all.17.carry_ref), channel_id=1, source_target_pairs={{0,1},{1,0},{2,3},{3,2},{4,5},{5,4},{6,7},{7,6},{8,9},{9,8},{10,11... | collective-permute-start | bytes 393224 | tf_op jit(solution)/shard_map/ppermute | solution.py:220
  60.7 10.5 %copy-start.1 = (bf16[8,16,16,256]{3,2,1,0:T(8,128)(2,1)S(1)}, bf16[8,16,16,256]{3,2,1,0:T(8,128)(2,1)}, u32[]{:S(2)}) copy-start(bf16[8,16,16,256]{3,2,1,0:T(8,128)(2,1)} %x_hbm.3) | copy-start | bytes 3145732
  60.7 10.5 %copy-start.4 = (f32[256]{0:T(256)S(1)}, f32[256]{0:T(256)}, u32[]{:S(2)}) copy-start(f32[256]{0:T(256)} %param.9) | copy-start | bytes 3076
  61.3 10.6 %collective-permute-start.4 = (f32[256,256]{1,0:T(8,128)S(1)}, f32[256,256]{1,0:T(8,128)S(1)}, u32[]{:S(2)}, u32[]{:S(2)}) collective-permute-start(f32[256,256]{1,0:T(8,128)S(1)} %shard_map.60.after_ref), channel_id=1, source_target_pairs={{0,6},{2,0},{4,2},{6,4},{1,7},{3,1},{5,3},{7,5},{8,14},{10,8},{12,... | collective-permute-start | bytes 786440 | tf_op jit(solution)/shard_map/ppermute | solution.py:233
  65.7 11.3 %collective-permute-start.3 = (f32[256,256]{1,0:T(8,128)S(1)}, f32[256,256]{1,0:T(8,128)S(1)}, u32[]{:S(2)}, u32[]{:S(2)}) collective-permute-start(f32[256,256]{1,0:T(8,128)S(1)} %shard_map.59.after_ref), channel_id=1, source_target_pairs={{0,2},{2,4},{4,6},{6,0},{1,3},{3,5},{5,7},{7,1},{8,10},{10,12},{12... | collective-permute-start | bytes 786440 | tf_op jit(solution)/shard_map/ppermute | solution.py:233
  67.6 13.1 %collective-permute-start.2 = (f32[256,256]{1,0:T(8,128)S(1)}, f32[256,256]{1,0:T(8,128)S(1)}, u32[]{:S(2)}, u32[]{:S(2)}) collective-permute-start(f32[256,256]{1,0:T(8,128)S(1)} %shard_map.58.after_ref), channel_id=1, source_target_pairs={{0,4},{2,6},{4,0},{6,2},{1,5},{3,7},{5,1},{7,3},{8,12},{10,14},{12... | collective-permute-start | bytes 786440 | tf_op jit(solution)/shard_map/ppermute | solution.py:233

commit v5 on v4

--- a/solution.py
+++ b/solution.py
@@ -14,6 +14,7 @@
 DECAY_AT = FRAMES * PIX
 WEIGHT_AT = DECAY_AT + 8
 SHARED = WEIGHT_AT + 18 * PD
+ORDER = (1, 3, 2)
 F32, BF16 = jnp.float32, jnp.bfloat16
 
 
@@ -35,7 +36,7 @@
     return from_left + centre + from_right
 
 
-def drive_kernel(x_hbm, w_hbm, codes_hbm, wout_hbm, shared_hbm, end_ref,
+def drive_kernel(x_hbm, w_hbm, codes_hbm, wout_hbm, shared_hbm, end_hbm,
                  xpad, wcat, wout, codes, shared, frame_sem, tap_sem, small_sem, out_sem):
     taps = [(di, dj) for di in range(3) for dj in range(3)]
     copies = [
@@ -55,37 +56,45 @@
         pltpu.make_async_copy(shared.at[pl.ds(at, to - at)], shared_hbm.at[pl.ds(at, to - at)], out_sem.at[i])
         for i, (at, to) in enumerate(zip(edges[:-1], edges[1:], strict=True))
     ]
-    for copy in [small[0], *frames[:2], *copies, small[1], *frames[2:]]:
+    last, part = DECAY_AT - PIX, PIX // 8
+    ends = [
+        pltpu.make_async_copy(shared.at[pl.ds(last + i * part, part)], end_hbm.at[i], out_sem.at[len(sends) + i])
+        for i in range(8)
+    ]
+    for copy in [small[0], *frames[:group], *copies, *frames[group:], small[1]]:
         copy.start()
     xpad[:, 0] = jnp.zeros((FRAMES, COLS, CIN), BF16)
     xpad[:, ROWS + 1] = jnp.zeros((FRAMES, COLS, CIN), BF16)
     small[0].wait()
     decay = decay_of(codes[...])
     shared[DECAY_AT:WEIGHT_AT] = jnp.broadcast_to(decay, (8, PD))
-    for copy in copies:
-        copy.wait()
     running = jnp.zeros((PIX, PD), F32)
     for first in range(0, FRAMES, group):
         total = jnp.zeros((group * PIX, 3 * PD), F32)
         for copy in frames[first : first + group]:
             copy.wait()
         for di in range(3):
+            if first == 0:
+                for copy in copies[3 * di : 3 * di + 3]:
+                    copy.wait()
             rows = xpad[first : first + group, di : di + ROWS].reshape(group * PIX, CIN)
             total = total + jnp.dot(rows, wcat[di], preferred_element_type=F32)
         drive = shifted_sum(total[:, :PD], total[:, PD : 2 * PD], total[:, 2 * PD :])
         for k in range(group):
             running = decay * running + drive[k * PIX : (k + 1) * PIX]
             shared[(first + k) * PIX : (first + k + 1) * PIX] = running
+        if first + group == FRAMES:
+            for copy in ends:
+                copy.start()
         sends[first // group].start()
-        if first == 0:
+        if first == FRAMES // 2:
             small[1].wait()
             for tap in range(9):
                 for half in range(2):
                     at = WEIGHT_AT + (2 * tap + half) * PD
                     shared[at : at + PD] = wout[tap // 3, tap % 3, :, half * PD : (half + 1) * PD].astype(F32)
             sends[-1].start()
-    end_ref[...] = running.reshape(8, PIX // 8, PD)
-    for copy in sends:
+    for copy in ends + sends:
         copy.wait()
 
 
@@ -123,7 +132,7 @@
 
 
 def readout(offset, own_ref, other_ref, codes_ref, carry_ref, carry_other_ref, w_ref, spad):
-    chip = (lax.axis_index("x") + offset) % 4
+    chip = lax.axis_index("x") ^ offset
     above = 4 * chip + 2 * lax.axis_index("c") - 1
     sides = (
         (own_ref, carry_ref, decay_of(codes_ref[...])),
@@ -199,12 +208,12 @@
             pltpu.SemaphoreType.DMA((FRAMES,)),
             pltpu.SemaphoreType.DMA((9,)),
             pltpu.SemaphoreType.DMA((2,)),
-            pltpu.SemaphoreType.DMA((5,)),
+            pltpu.SemaphoreType.DMA((13,)),
         ),
         flops=flops,
         moved=3 << 20,
         limit=59,
-        outs=tuple(pl.BlockSpec(memory_space=space) for space in (pltpu.HBM, pltpu.VMEM)),
+        outs=tuple(pl.BlockSpec(memory_space=space) for space in (pltpu.HBM, pltpu.HBM)),
     )
     swap = [(0, 1), (1, 0)]
     ends = lax.all_to_all(end, "z", 0, 0, tiled=True)
@@ -221,7 +230,7 @@
     inputs = (shared, other, codes, carry, carry_other, weights)
     padded = pltpu.VMEM((FRAMES, 4, COLS, 2 * PD), BF16)
     piece, arrived = carry_other, []
-    for offset in (2, 1, 3):
+    for offset in ORDER:
         piece = call(
             functools.partial(far_kernel, offset),
             shape(owned, CIN),
@@ -230,7 +239,7 @@
             scratch=(padded,),
             flops=flops // 4,
         )
-        arrived.append(lax.ppermute(piece, "x", [(i, (i + offset) % 4) for i in range(4)]))
+        arrived.append(lax.ppermute(piece, "x", [(i, i ^ offset) for i in range(4)]))
     own = call(
         near_kernel,
         shape(owned, CIN),

time: 81.9 us -> 79 us (0.965)
  waiting for transfers between devices: 9.78 us -> 8.21 us
    ppermute x3, waiting for transfers between devices: 8.82 us -> 7.24 us  [per_device(): lax.ppermute(piece, 'x', [(i, i ^ offset) for i in range(4)])]
where the time goes in v5:
time: 79 us; the launch traced here: 78.6 us
  blocking collectives  38.1 us (48%)
  starting transfers between devices  24.2 us (31%)
  waiting for transfers between devices  8.21 us (10%)
  Pallas kernels  7.99 us (10%)
    all_to_all x1, blocking collectives, per_device(): totals = lax.all_to_all(total, 'y', 0, 0, tiled=True)  14.6 us
    all_to_all x1, blocking collectives, per_device(): ends = lax.all_to_all(end, 'z', 0, 0, tiled=True)  13.2 us
    all_to_all x1, blocking collectives, per_device(): carry = lax.all_to_all(carries, 'z', 0, 0, tiled=True)  10.4 us
    ppermute x3, starting transfers between devices, per_device(): lax.ppermute(piece, 'x', [(i, i ^ offset) for i in range(4)])  9.34 us
    ppermute x1, starting transfers between devices, per_device(): other = lax.ppermute(shared, 'c', swap)  8.88 us
    pallas_call x8, Pallas kernels, call(): pl.pallas_call(kernel, out_shape=out, in_specs=[pl.BlockSpec(memory_space...  7.99 us
    ppermute x3, waiting for transfers between devices, per_device(): lax.ppermute(piece, 'x', [(i, i ^ offset) for i in range(4)])  7.24 us
    ppermute x1, starting transfers between devices, per_device(): carry_other = lax.ppermute(carry, 'c', swap)  5.97 us
  transfers between devices with their start and end apart: 5, of which 3 were waited for; matrix products, arithmetic and copies ran while one was open for 0% of the time, Pallas kernels for 1%

profile of v5, /device:TPU:1, one launch (start us, length us, event | category | flops | bytes accessed | tf_op | source)
XLA Modules:
  0.0 78.6 jit_solution(9126180700602675926)
XLA Ops:
  0.0 4.8 %shard_map.55 = (f32[4360,128]{1,0:T(8,128)}, f32[8,32,128]{2,1,0:T(8,128)}) custom-call(bf16[8,16,16,256]{3,2,1,0:T(8,128)(2,1)} %x_hbm.3, bf16[3,3,256,128]{3,2,1,0:T(8,128)(2,1)} %w_hbm.1, s32[1,128]{1,0:T(1,128)} %bitcast.3, bf16[3,3,128,256]{3,2,1,0:T(8,128)(2,1)} %wout_ref.1), custom_call_target="tpu_custom_call" | custom-call | flops 1207959552 | bytes 3145728 | tf_op jit(solution)/shard_map/pallas_call | solution.py:177
  4.9 8.9 %collective-permute-start = (f32[4360,128]{1,0:T(8,128)}, f32[4360,128]{1,0:T(8,128)S(1)}, u32[]{:S(2)}, u32[]{:S(2)}) collective-permute-start(f32[4360,128]{1,0:T(8,128)} %get-tuple-element.9.own_ref), channel_id=1, source_target_pairs={{0,1},{1,0},{2,3},{3,2},{4,5},{5,4},{6,7},{7,6},{8,9},{9,8},{10,11... | collective-permute-start | bytes 6696968 | tf_op jit(solution)/shard_map/ppermute | solution.py:220
  13.7 13.2 %all_to_all.15.ends_ref = f32[8,32,128]{2,1,0:T(8,128)S(1)} all-to-all(f32[8,32,128]{2,1,0:T(8,128)} %get-tuple-element.10), channel_id=1, replica_groups=mesh['y'=8,'z'=8,'x'=4,'c'=2] {'z'}, dimensions={0} | all-to-all | bytes 262144 | tf_op jit(solution)/shard_map/all_to_all | solution.py:219
  26.9 14.6 %all_to_all.16.totals_ref = f32[8,32,128]{2,1,0:T(8,128)S(1)} all-to-all(f32[8,32,128]{2,1,0:T(8,128)S(1)} %shard_map.56), channel_id=1, replica_groups=mesh['y'=8,'z'=8,'x'=4,'c'=2] {'y'}, dimensions={0} | all-to-all | bytes 262144 | tf_op jit(solution)/shard_map/all_to_all | solution.py:222
  41.5 0.0 collective-permute-done.other_ref
  41.5 0.1 shard_map.57
  41.6 10.4 %all_to_all.17.carry_ref = f32[8,32,128]{2,1,0:T(8,128)S(1)} all-to-all(f32[8,32,128]{2,1,0:T(8,128)S(1)} %get-tuple-element.11), channel_id=1, replica_groups=mesh['y'=8,'z'=8,'x'=4,'c'=2] {'z'}, dimensions={0} | all-to-all | bytes 262144 | tf_op jit(solution)/shard_map/all_to_all | solution.py:228
  52.0 6.0 %collective-permute-start.1 = (f32[8,32,128]{2,1,0:T(8,128)S(1)}, f32[8,32,128]{2,1,0:T(8,128)S(1)}, u32[]{:S(2)}, u32[]{:S(2)}) collective-permute-start(f32[8,32,128]{2,1,0:T(8,128)S(1)} %all_to_all.17.carry_ref), channel_id=1, source_target_pairs={{0,1},{1,0},{2,3},{3,2},{4,5},{5,4},{6,7},{7,6},{8,9},{9,8},{10,11... | collective-permute-start | bytes 393224 | tf_op jit(solution)/shard_map/ppermute | solution.py:229
  58.0 1.0 %collective-permute-done.1.carry_other_ref.after_ref = f32[8,32,128]{2,1,0:T(8,128)S(1)} collective-permute-done((f32[8,32,128]{2,1,0:T(8,128)S(1)}, f32[8,32,128]{2,1,0:T(8,128)S(1)}, u32[]{:S(2)}, u32[]{:S(2)}) %collective-permute-start.1) | collective-permute-done | bytes 131104 | tf_op jit(solution)/shard_map/ppermute | solution.py:229
  59.0 0.5 shard_map.58.after_ref
  59.5 0.5 shard_map.59.after_ref
  60.1 0.0 copy-start.1
  60.1 0.0 copy-start.4
  60.1 0.5 shard_map.60.after_ref
  60.6 4.6 %collective-permute-start.4 = (f32[256,256]{1,0:T(8,128)S(1)}, f32[256,256]{1,0:T(8,128)S(1)}, u32[]{:S(2)}, u32[]{:S(2)}) collective-permute-start(f32[256,256]{1,0:T(8,128)S(1)} %shard_map.60.after_ref), channel_id=1, source_target_pairs={{0,4},{2,6},{4,0},{6,2},{1,5},{3,7},{5,1},{7,3},{8,12},{10,14},{12... | collective-permute-start | bytes 786440 | tf_op jit(solution)/shard_map/ppermute | solution.py:242
  65.3 2.8 %collective-permute-start.3 = (f32[256,256]{1,0:T(8,128)S(1)}, f32[256,256]{1,0:T(8,128)S(1)}, u32[]{:S(2)}, u32[]{:S(2)}) collective-permute-start(f32[256,256]{1,0:T(8,128)S(1)} %shard_map.59.after_ref), channel_id=1, source_target_pairs={{0,6},{2,4},{4,2},{6,0},{1,7},{3,5},{5,3},{7,1},{8,14},{10,12},{12... | collective-permute-start | bytes 786440 | tf_op jit(solution)/shard_map/ppermute | solution.py:242
  68.1 1.9 %collective-permute-start.2 = (f32[256,256]{1,0:T(8,128)S(1)}, f32[256,256]{1,0:T(8,128)S(1)}, u32[]{:S(2)}, u32[]{:S(2)}) collective-permute-start(f32[256,256]{1,0:T(8,128)S(1)} %shard_map.58.after_ref), channel_id=1, source_target_pairs={{0,2},{2,0},{4,6},{6,4},{1,3},{3,1},{5,7},{7,5},{8,10},{10,8},{12,... | collective-permute-start | bytes 786440 | tf_op jit(solution)/shard_map/ppermute | solution.py:242
  70.0 0.0 copy-done.1
  70.0 0.0 copy-done.4
  70.0 0.6 shard_map.61.own_ref
  70.6 0.9 %collective-permute-done.4.third_ref = f32[256,256]{1,0:T(8,128)S(1)} collective-permute-done((f32[256,256]{1,0:T(8,128)S(1)}, f32[256,256]{1,0:T(8,128)S(1)}, u32[]{:S(2)}, u32[]{:S(2)}) %collective-permute-start.4) | collective-permute-done | bytes 262176 | tf_op jit(solution)/shard_map/ppermute | solution.py:242
  71.5 6.3 %collective-permute-done.3.second_ref = f32[256,256]{1,0:T(8,128)S(1)} collective-permute-done((f32[256,256]{1,0:T(8,128)S(1)}, f32[256,256]{1,0:T(8,128)S(1)}, u32[]{:S(2)}, u32[]{:S(2)}) %collective-permute-start.3) | collective-permute-done | bytes 262176 | tf_op jit(solution)/shard_map/ppermute | solution.py:242
  77.9 0.0 collective-permute-done.2.first_ref
  77.9 0.7 shard_map.62
  (7 shorter events, 0.0 us)
Async XLA Ops:
  0.0 26.9 %copy-start.3 = (s32[128]{0:T(128)S(1)}, s32[128]{0:T(128)}, u32[]{:S(2)}) copy-start(s32[128]{0:T(128)} %param.7) | copy-start | bytes 1540
  0.0 41.5 %copy-start.2 = (bf16[3,3,128,256]{3,2,1,0:T(8,128)(2,1)S(1)}, bf16[3,3,128,256]{3,2,1,0:T(8,128)(2,1)}, u32[]{:S(2)}) copy-start(bf16[3,3,128,256]{3,2,1,0:T(8,128)(2,1)} %wout_ref.1) | copy-start | bytes 1769476
  4.8 54.1 %copy-start = (f32[4360,128]{1,0:T(8,128)S(1)}, f32[4360,128]{1,0:T(8,128)}, u32[]{:S(2)}) copy-start(f32[4360,128]{1,0:T(8,128)} %get-tuple-element.9.own_ref) | copy-start | bytes 6696964
  4.9 36.6 %collective-permute-start = (f32[4360,128]{1,0:T(8,128)}, f32[4360,128]{1,0:T(8,128)S(1)}, u32[]{:S(2)}, u32[]{:S(2)}) collective-permute-start(f32[4360,128]{1,0:T(8,128)} %get-tuple-element.9.own_ref), channel_id=1, source_target_pairs={{0,1},{1,0},{2,3},{3,2},{4,5},{5,4},{6,7},{7,6},{8,9},{9,8},{10,11... | collective-permute-start | bytes 6696968 | tf_op jit(solution)/shard_map/ppermute | solution.py:220
  52.0 6.9 %collective-permute-start.1 = (f32[8,32,128]{2,1,0:T(8,128)S(1)}, f32[8,32,128]{2,1,0:T(8,128)S(1)}, u32[]{:S(2)}, u32[]{:S(2)}) collective-permute-start(f32[8,32,128]{2,1,0:T(8,128)S(1)} %all_to_all.17.carry_ref), channel_id=1, source_target_pairs={{0,1},{1,0},{2,3},{3,2},{4,5},{5,4},{6,7},{7,6},{8,9},{9,8},{10,11... | collective-permute-start | bytes 393224 | tf_op jit(solution)/shard_map/ppermute | solution.py:229
  60.1 9.9 %copy-start.1 = (bf16[8,16,16,256]{3,2,1,0:T(8,128)(2,1)S(1)}, bf16[8,16,16,256]{3,2,1,0:T(8,128)(2,1)}, u32[]{:S(2)}) copy-start(bf16[8,16,16,256]{3,2,1,0:T(8,128)(2,1)} %x_hbm.3) | copy-start | bytes 3145732
  60.1 9.9 %copy-start.4 = (f32[256]{0:T(256)S(1)}, f32[256]{0:T(256)}, u32[]{:S(2)}) copy-start(f32[256]{0:T(256)} %param.9) | copy-start | bytes 3076
  60.6 10.9 %collective-permute-start.4 = (f32[256,256]{1,0:T(8,128)S(1)}, f32[256,256]{1,0:T(8,128)S(1)}, u32[]{:S(2)}, u32[]{:S(2)}) collective-permute-start(f32[256,256]{1,0:T(8,128)S(1)} %shard_map.60.after_ref), channel_id=1, source_target_pairs={{0,4},{2,6},{4,0},{6,2},{1,5},{3,7},{5,1},{7,3},{8,12},{10,14},{12... | collective-permute-start | bytes 786440 | tf_op jit(solution)/shard_map/ppermute | solution.py:242
  65.3 12.6 %collective-permute-start.3 = (f32[256,256]{1,0:T(8,128)S(1)}, f32[256,256]{1,0:T(8,128)S(1)}, u32[]{:S(2)}, u32[]{:S(2)}) collective-permute-start(f32[256,256]{1,0:T(8,128)S(1)} %shard_map.59.after_ref), channel_id=1, source_target_pairs={{0,6},{2,4},{4,2},{6,0},{1,7},{3,5},{5,3},{7,1},{8,14},{10,12},{12... | collective-permute-start | bytes 786440 | tf_op jit(solution)/shard_map/ppermute | solution.py:242
  68.1 9.8 %collective-permute-start.2 = (f32[256,256]{1,0:T(8,128)S(1)}, f32[256,256]{1,0:T(8,128)S(1)}, u32[]{:S(2)}, u32[]{:S(2)}) collective-permute-start(f32[256,256]{1,0:T(8,128)S(1)} %shard_map.58.after_ref), channel_id=1, source_target_pairs={{0,2},{2,0},{4,6},{6,4},{1,3},{3,1},{5,7},{7,5},{8,10},{10,8},{12,... | collective-permute-start | bytes 786440 | tf_op jit(solution)/shard_map/ppermute | solution.py:242

commit v6 on v5

--- a/solution.py
+++ b/solution.py
@@ -14,7 +14,7 @@
 DECAY_AT = FRAMES * PIX
 WEIGHT_AT = DECAY_AT + 8
 SHARED = WEIGHT_AT + 18 * PD
-ORDER = (1, 3, 2)
+ORDER = (2, 1, 3)
 F32, BF16 = jnp.float32, jnp.bfloat16
 
 
@@ -50,8 +50,8 @@
         pltpu.make_async_copy(src, dst, small_sem.at[i])
         for i, (src, dst) in enumerate(((codes_hbm, codes), (wout_hbm, wout)))
     ]
-    group = 2
-    edges = [*range(0, DECAY_AT, group * PIX), DECAY_AT, SHARED]
+    group = FRAMES // 2
+    edges = [*range(0, DECAY_AT, PIX), DECAY_AT, SHARED]
     sends = [
         pltpu.make_async_copy(shared.at[pl.ds(at, to - at)], shared_hbm.at[pl.ds(at, to - at)], out_sem.at[i])
         for i, (at, to) in enumerate(zip(edges[:-1], edges[1:], strict=True))
@@ -61,7 +61,7 @@
         pltpu.make_async_copy(shared.at[pl.ds(last + i * part, part)], end_hbm.at[i], out_sem.at[len(sends) + i])
         for i in range(8)
     ]
-    for copy in [small[0], *frames[:group], *copies, *frames[group:], small[1]]:
+    for copy in [small[0], *copies[:3], *frames[:group], *copies[3:], *frames[group:], small[1]]:
         copy.start()
     xpad[:, 0] = jnp.zeros((FRAMES, COLS, CIN), BF16)
     xpad[:, ROWS + 1] = jnp.zeros((FRAMES, COLS, CIN), BF16)
@@ -70,9 +70,9 @@
     shared[DECAY_AT:WEIGHT_AT] = jnp.broadcast_to(decay, (8, PD))
     running = jnp.zeros((PIX, PD), F32)
     for first in range(0, FRAMES, group):
-        total = jnp.zeros((group * PIX, 3 * PD), F32)
         for copy in frames[first : first + group]:
             copy.wait()
+        total = jnp.zeros((group * PIX, 3 * PD), F32)
         for di in range(3):
             if first == 0:
                 for copy in copies[3 * di : 3 * di + 3]:
@@ -81,19 +81,21 @@
             total = total + jnp.dot(rows, wcat[di], preferred_element_type=F32)
         drive = shifted_sum(total[:, :PD], total[:, PD : 2 * PD], total[:, 2 * PD :])
         for k in range(group):
+            frame = first + k
             running = decay * running + drive[k * PIX : (k + 1) * PIX]
-            shared[(first + k) * PIX : (first + k + 1) * PIX] = running
-        if first + group == FRAMES:
-            for copy in ends:
-                copy.start()
-        sends[first // group].start()
-        if first == FRAMES // 2:
+            shared[frame * PIX : (frame + 1) * PIX] = running
+            if frame < FRAMES - 1:
+                sends[frame].start()
+        if first == 0:
             small[1].wait()
             for tap in range(9):
                 for half in range(2):
                     at = WEIGHT_AT + (2 * tap + half) * PD
                     shared[at : at + PD] = wout[tap // 3, tap % 3, :, half * PD : (half + 1) * PD].astype(F32)
             sends[-1].start()
+    for copy in ends:
+        copy.start()
+    sends[FRAMES - 1].start()
     for copy in ends + sends:
         copy.wait()
 
@@ -132,7 +134,7 @@
 
 
 def readout(offset, own_ref, other_ref, codes_ref, carry_ref, carry_other_ref, w_ref, spad):
-    chip = lax.axis_index("x") ^ offset
+    chip = (lax.axis_index("x") + offset) % 4
     above = 4 * chip + 2 * lax.axis_index("c") - 1
     sides = (
         (own_ref, carry_ref, decay_of(codes_ref[...])),
@@ -208,7 +210,7 @@
             pltpu.SemaphoreType.DMA((FRAMES,)),
             pltpu.SemaphoreType.DMA((9,)),
             pltpu.SemaphoreType.DMA((2,)),
-            pltpu.SemaphoreType.DMA((13,)),
+            pltpu.SemaphoreType.DMA((17,)),
         ),
         flops=flops,
         moved=3 << 20,
@@ -239,7 +241,7 @@
             scratch=(padded,),
             flops=flops // 4,
         )
-        arrived.append(lax.ppermute(piece, "x", [(i, i ^ offset) for i in range(4)]))
+        arrived.append(lax.ppermute(piece, "x", [(i, (i + offset) % 4) for i in range(4)]))
     own = call(
         near_kernel,
         shape(owned, CIN),

time: 79 us -> 81.1 us (1.027)
  waiting for transfers between devices: 8.21 us -> 9.79 us
    ppermute x3, waiting for transfers between devices: 7.24 us -> 8.82 us  [per_device(): lax.ppermute(piece, 'x', [(i, (i + offset) % 4) for i in range(4)])]
where the time goes in v6:
time: 81.1 us; the launch traced here: 80.6 us
  blocking collectives  38.1 us (47%)
  starting transfers between devices  24.8 us (31%)
  waiting for transfers between devices  9.79 us (12%)
  Pallas kernels  7.82 us (10%)
    all_to_all x1, blocking collectives, per_device(): totals = lax.all_to_all(total, 'y', 0, 0, tiled=True)  14.6 us
    all_to_all x1, blocking collectives, per_device(): ends = lax.all_to_all(end, 'z', 0, 0, tiled=True)  13.2 us
    all_to_all x1, blocking collectives, per_device(): carry = lax.all_to_all(carries, 'z', 0, 0, tiled=True)  10.4 us
    ppermute x3, starting transfers between devices, per_device(): lax.ppermute(piece, 'x', [(i, (i + offset) % 4) for i in range(4)])  9.92 us
    ppermute x1, starting transfers between devices, per_device(): other = lax.ppermute(shared, 'c', swap)  8.88 us
    ppermute x3, waiting for transfers between devices, per_device(): lax.ppermute(piece, 'x', [(i, (i + offset) % 4) for i in range(4)])  8.82 us
    pallas_call x8, Pallas kernels, call(): pl.pallas_call(kernel, out_shape=out, in_specs=[pl.BlockSpec(memory_space...  7.82 us
    ppermute x1, starting transfers between devices, per_device(): carry_other = lax.ppermute(carry, 'c', swap)  5.97 us
  transfers between devices with their start and end apart: 5, of which 3 were waited for; matrix products, arithmetic and copies ran while one was open for 0% of the time, Pallas kernels for 1%

profile of v6, /device:TPU:1, one launch (start us, length us, event | category | flops | bytes accessed | tf_op | source)
XLA Modules:
  0.0 80.6 jit_solution(1163414105737798653)
XLA Ops:
  0.0 4.6 %shard_map.55 = (f32[4360,128]{1,0:T(8,128)}, f32[8,32,128]{2,1,0:T(8,128)}) custom-call(bf16[8,16,16,256]{3,2,1,0:T(8,128)(2,1)} %x_hbm.3, bf16[3,3,256,128]{3,2,1,0:T(8,128)(2,1)} %w_hbm.1, s32[1,128]{1,0:T(1,128)} %bitcast.3, bf16[3,3,128,256]{3,2,1,0:T(8,128)(2,1)} %wout_ref.1), custom_call_target="tpu_custom_call" | custom-call | flops 1207959552 | bytes 3145728 | tf_op jit(solution)/shard_map/pallas_call | solution.py:179
  4.6 0.0 copy-start
  4.6 8.9 %collective-permute-start = (f32[4360,128]{1,0:T(8,128)}, f32[4360,128]{1,0:T(8,128)S(1)}, u32[]{:S(2)}, u32[]{:S(2)}) collective-permute-start(f32[4360,128]{1,0:T(8,128)} %get-tuple-element.9.own_ref), channel_id=1, source_target_pairs={{0,1},{1,0},{2,3},{3,2},{4,5},{5,4},{6,7},{7,6},{8,9},{9,8},{10,11... | collective-permute-start | bytes 6696968 | tf_op jit(solution)/shard_map/ppermute | solution.py:222
  13.5 13.2 %all_to_all.15.ends_ref = f32[8,32,128]{2,1,0:T(8,128)S(1)} all-to-all(f32[8,32,128]{2,1,0:T(8,128)} %get-tuple-element.10), channel_id=1, replica_groups=mesh['y'=8,'z'=8,'x'=4,'c'=2] {'z'}, dimensions={0} | all-to-all | bytes 262144 | tf_op jit(solution)/shard_map/all_to_all | solution.py:221
  26.7 0.0 copy-done.3
  26.7 14.6 %all_to_all.16.totals_ref = f32[8,32,128]{2,1,0:T(8,128)S(1)} all-to-all(f32[8,32,128]{2,1,0:T(8,128)S(1)} %shard_map.56), channel_id=1, replica_groups=mesh['y'=8,'z'=8,'x'=4,'c'=2] {'y'}, dimensions={0} | all-to-all | bytes 262144 | tf_op jit(solution)/shard_map/all_to_all | solution.py:224
  41.3 0.0 collective-permute-done.other_ref
  41.3 0.1 shard_map.57
  41.4 10.4 %all_to_all.17.carry_ref = f32[8,32,128]{2,1,0:T(8,128)S(1)} all-to-all(f32[8,32,128]{2,1,0:T(8,128)S(1)} %get-tuple-element.11), channel_id=1, replica_groups=mesh['y'=8,'z'=8,'x'=4,'c'=2] {'z'}, dimensions={0} | all-to-all | bytes 262144 | tf_op jit(solution)/shard_map/all_to_all | solution.py:230
  51.8 6.0 %collective-permute-start.1 = (f32[8,32,128]{2,1,0:T(8,128)S(1)}, f32[8,32,128]{2,1,0:T(8,128)S(1)}, u32[]{:S(2)}, u32[]{:S(2)}) collective-permute-start(f32[8,32,128]{2,1,0:T(8,128)S(1)} %all_to_all.17.carry_ref), channel_id=1, source_target_pairs={{0,1},{1,0},{2,3},{3,2},{4,5},{5,4},{6,7},{7,6},{8,9},{9,8},{10,11... | collective-permute-start | bytes 393224 | tf_op jit(solution)/shard_map/ppermute | solution.py:231
  57.8 1.0 %collective-permute-done.1.carry_other_ref.after_ref = f32[8,32,128]{2,1,0:T(8,128)S(1)} collective-permute-done((f32[8,32,128]{2,1,0:T(8,128)S(1)}, f32[8,32,128]{2,1,0:T(8,128)S(1)}, u32[]{:S(2)}, u32[]{:S(2)}) %collective-permute-start.1) | collective-permute-done | bytes 131104 | tf_op jit(solution)/shard_map/ppermute | solution.py:231
  58.8 0.5 shard_map.58.after_ref
  59.3 0.6 shard_map.59.after_ref
  59.9 0.0 copy-start.1
  59.9 0.0 copy-start.4
  59.9 0.6 shard_map.60.after_ref
  60.5 4.4 %collective-permute-start.4 = (f32[256,256]{1,0:T(8,128)S(1)}, f32[256,256]{1,0:T(8,128)S(1)}, u32[]{:S(2)}, u32[]{:S(2)}) collective-permute-start(f32[256,256]{1,0:T(8,128)S(1)} %shard_map.60.after_ref), channel_id=1, source_target_pairs={{0,6},{2,0},{4,2},{6,4},{1,7},{3,1},{5,3},{7,5},{8,14},{10,8},{12,... | collective-permute-start | bytes 786440 | tf_op jit(solution)/shard_map/ppermute | solution.py:244
  64.8 1.9 %collective-permute-start.3 = (f32[256,256]{1,0:T(8,128)S(1)}, f32[256,256]{1,0:T(8,128)S(1)}, u32[]{:S(2)}, u32[]{:S(2)}) collective-permute-start(f32[256,256]{1,0:T(8,128)S(1)} %shard_map.59.after_ref), channel_id=1, source_target_pairs={{0,2},{2,4},{4,6},{6,0},{1,3},{3,5},{5,7},{7,1},{8,10},{10,12},{12... | collective-permute-start | bytes 786440 | tf_op jit(solution)/shard_map/ppermute | solution.py:244
  66.8 3.6 %collective-permute-start.2 = (f32[256,256]{1,0:T(8,128)S(1)}, f32[256,256]{1,0:T(8,128)S(1)}, u32[]{:S(2)}, u32[]{:S(2)}) collective-permute-start(f32[256,256]{1,0:T(8,128)S(1)} %shard_map.58.after_ref), channel_id=1, source_target_pairs={{0,4},{2,6},{4,0},{6,2},{1,5},{3,7},{5,1},{7,3},{8,12},{10,14},{12... | collective-permute-start | bytes 786440 | tf_op jit(solution)/shard_map/ppermute | solution.py:244
  70.4 0.6 shard_map.61.own_ref
  71.1 0.0 collective-permute-done.4.third_ref
  71.1 5.0 %collective-permute-done.3.second_ref = f32[256,256]{1,0:T(8,128)S(1)} collective-permute-done((f32[256,256]{1,0:T(8,128)S(1)}, f32[256,256]{1,0:T(8,128)S(1)}, u32[]{:S(2)}, u32[]{:S(2)}) %collective-permute-start.3) | collective-permute-done | bytes 262176 | tf_op jit(solution)/shard_map/ppermute | solution.py:244
  76.1 3.8 %collective-permute-done.2.first_ref = f32[256,256]{1,0:T(8,128)S(1)} collective-permute-done((f32[256,256]{1,0:T(8,128)S(1)}, f32[256,256]{1,0:T(8,128)S(1)}, u32[]{:S(2)}, u32[]{:S(2)}) %collective-permute-start.2) | collective-permute-done | bytes 262176 | tf_op jit(solution)/shard_map/ppermute | solution.py:244
  79.9 0.7 shard_map.62
  (7 shorter events, 0.0 us)
Async XLA Ops:
  0.0 26.7 %copy-start.3 = (s32[128]{0:T(128)S(1)}, s32[128]{0:T(128)}, u32[]{:S(2)}) copy-start(s32[128]{0:T(128)} %param.7) | copy-start | bytes 1540
  0.0 41.3 %copy-start.2 = (bf16[3,3,128,256]{3,2,1,0:T(8,128)(2,1)S(1)}, bf16[3,3,128,256]{3,2,1,0:T(8,128)(2,1)}, u32[]{:S(2)}) copy-start(bf16[3,3,128,256]{3,2,1,0:T(8,128)(2,1)} %wout_ref.1) | copy-start | bytes 1769476
  4.6 54.1 %copy-start = (f32[4360,128]{1,0:T(8,128)S(1)}, f32[4360,128]{1,0:T(8,128)}, u32[]{:S(2)}) copy-start(f32[4360,128]{1,0:T(8,128)} %get-tuple-element.9.own_ref) | copy-start | bytes 6696964
  4.6 36.6 %collective-permute-start = (f32[4360,128]{1,0:T(8,128)}, f32[4360,128]{1,0:T(8,128)S(1)}, u32[]{:S(2)}, u32[]{:S(2)}) collective-permute-start(f32[4360,128]{1,0:T(8,128)} %get-tuple-element.9.own_ref), channel_id=1, source_target_pairs={{0,1},{1,0},{2,3},{3,2},{4,5},{5,4},{6,7},{7,6},{8,9},{9,8},{10,11... | collective-permute-start | bytes 6696968 | tf_op jit(solution)/shard_map/ppermute | solution.py:222
  51.8 6.9 %collective-permute-start.1 = (f32[8,32,128]{2,1,0:T(8,128)S(1)}, f32[8,32,128]{2,1,0:T(8,128)S(1)}, u32[]{:S(2)}, u32[]{:S(2)}) collective-permute-start(f32[8,32,128]{2,1,0:T(8,128)S(1)} %all_to_all.17.carry_ref), channel_id=1, source_target_pairs={{0,1},{1,0},{2,3},{3,2},{4,5},{5,4},{6,7},{7,6},{8,9},{9,8},{10,11... | collective-permute-start | bytes 393224 | tf_op jit(solution)/shard_map/ppermute | solution.py:231
  59.9 10.5 %copy-start.1 = (bf16[8,16,16,256]{3,2,1,0:T(8,128)(2,1)S(1)}, bf16[8,16,16,256]{3,2,1,0:T(8,128)(2,1)}, u32[]{:S(2)}) copy-start(bf16[8,16,16,256]{3,2,1,0:T(8,128)(2,1)} %x_hbm.3) | copy-start | bytes 3145732
  59.9 10.5 %copy-start.4 = (f32[256]{0:T(256)S(1)}, f32[256]{0:T(256)}, u32[]{:S(2)}) copy-start(f32[256]{0:T(256)} %param.9) | copy-start | bytes 3076
  60.5 10.6 %collective-permute-start.4 = (f32[256,256]{1,0:T(8,128)S(1)}, f32[256,256]{1,0:T(8,128)S(1)}, u32[]{:S(2)}, u32[]{:S(2)}) collective-permute-start(f32[256,256]{1,0:T(8,128)S(1)} %shard_map.60.after_ref), channel_id=1, source_target_pairs={{0,6},{2,0},{4,2},{6,4},{1,7},{3,1},{5,3},{7,5},{8,14},{10,8},{12,... | collective-permute-start | bytes 786440 | tf_op jit(solution)/shard_map/ppermute | solution.py:244
  64.8 11.3 %collective-permute-start.3 = (f32[256,256]{1,0:T(8,128)S(1)}, f32[256,256]{1,0:T(8,128)S(1)}, u32[]{:S(2)}, u32[]{:S(2)}) collective-permute-start(f32[256,256]{1,0:T(8,128)S(1)} %shard_map.59.after_ref), channel_id=1, source_target_pairs={{0,2},{2,4},{4,6},{6,0},{1,3},{3,5},{5,7},{7,1},{8,10},{10,12},{12... | collective-permute-start | bytes 786440 | tf_op jit(solution)/shard_map/ppermute | solution.py:244
  66.8 13.1 %collective-permute-start.2 = (f32[256,256]{1,0:T(8,128)S(1)}, f32[256,256]{1,0:T(8,128)S(1)}, u32[]{:S(2)}, u32[]{:S(2)}) collective-permute-start(f32[256,256]{1,0:T(8,128)S(1)} %shard_map.58.after_ref), channel_id=1, source_target_pairs={{0,4},{2,6},{4,0},{6,2},{1,5},{3,7},{5,1},{7,3},{8,12},{10,14},{12... | collective-permute-start | bytes 786440 | tf_op jit(solution)/shard_map/ppermute | solution.py:244

commit v7 on v6

--- a/solution.py
+++ b/solution.py
@@ -134,7 +134,7 @@
 
 
 def readout(offset, own_ref, other_ref, codes_ref, carry_ref, carry_other_ref, w_ref, spad):
-    chip = (lax.axis_index("x") + offset) % 4
+    chip = (lax.axis_index("x") + offset + 2 * offset * lax.axis_index("c")) % 4
     above = 4 * chip + 2 * lax.axis_index("c") - 1
     sides = (
         (own_ref, carry_ref, decay_of(codes_ref[...])),
@@ -185,6 +185,10 @@
         compiler_params=pltpu.CompilerParams(vmem_limit_bytes=limit << 20),
         cost_estimate=pl.CostEstimate(flops=flops, bytes_accessed=moved, transcendentals=0),
     )(*args)
+
+
+def ahead(offset):
+    return [(2 * x + c, 2 * ((x + (1 - 2 * c) * offset) % 4) + c) for x in range(4) for c in range(2)]
 
 
 def shape(*dims, dtype=F32):
@@ -241,7 +245,7 @@
             scratch=(padded,),
             flops=flops // 4,
         )
-        arrived.append(lax.ppermute(piece, "x", [(i, (i + offset) % 4) for i in range(4)]))
+        arrived.append(lax.ppermute(piece, ("x", "c"), ahead(offset)))
     own = call(
         near_kernel,
         shape(owned, CIN),

time: 81.1 us -> 79.9 us (0.985)
  waiting for transfers between devices: 9.79 us -> 8.64 us
    ppermute x3, waiting for transfers between devices: 8.82 us -> 7.67 us  [per_device(): arrived.append(lax.ppermute(piece, ('x', 'c'), ahead(offset)))]
where the time goes in v7:
time: 79.9 us; the launch traced here: 79.5 us
  blocking collectives  38.1 us (48%)
  starting transfers between devices  24.8 us (31%)
  waiting for transfers between devices  8.64 us (11%)
  Pallas kernels  7.81 us (10%)
    all_to_all x1, blocking collectives, per_device(): totals = lax.all_to_all(total, 'y', 0, 0, tiled=True)  14.6 us
    all_to_all x1, blocking collectives, per_device(): ends = lax.all_to_all(end, 'z', 0, 0, tiled=True)  13.2 us
    all_to_all x1, blocking collectives, per_device(): carry = lax.all_to_all(carries, 'z', 0, 0, tiled=True)  10.4 us
    ppermute x3, starting transfers between devices, per_device(): arrived.append(lax.ppermute(piece, ('x', 'c'), ahead(offset)))  9.92 us
    ppermute x1, starting transfers between devices, per_device(): other = lax.ppermute(shared, 'c', swap)  8.88 us
    pallas_call x8, Pallas kernels, call(): pl.pallas_call(kernel, out_shape=out, in_specs=[pl.BlockSpec(memory_space...  7.81 us
    ppermute x3, waiting for transfers between devices, per_device(): arrived.append(lax.ppermute(piece, ('x', 'c'), ahead(offset)))  7.67 us
    ppermute x1, starting transfers between devices, per_device(): carry_other = lax.ppermute(carry, 'c', swap)  5.97 us
  transfers between devices with their start and end apart: 5, of which 3 were waited for; matrix products, arithmetic and copies ran while one was open for 0% of the time, Pallas kernels for 1%

profile of v7, /device:TPU:1, one launch (start us, length us, event | category | flops | bytes accessed | tf_op | source)
XLA Modules:
  0.0 79.5 jit_solution(1242114438399091354)
XLA Ops:
  0.0 4.6 %shard_map.55 = (f32[4360,128]{1,0:T(8,128)}, f32[8,32,128]{2,1,0:T(8,128)}) custom-call(bf16[8,16,16,256]{3,2,1,0:T(8,128)(2,1)} %x_hbm.3, bf16[3,3,256,128]{3,2,1,0:T(8,128)(2,1)} %w_hbm.1, s32[1,128]{1,0:T(1,128)} %bitcast.3, bf16[3,3,128,256]{3,2,1,0:T(8,128)(2,1)} %wout_ref.1), custom_call_target="tpu_custom_call" | custom-call | flops 1207959552 | bytes 3145728 | tf_op jit(solution)/shard_map/pallas_call | solution.py:179
  4.6 0.0 copy-start
  4.6 8.9 %collective-permute-start = (f32[4360,128]{1,0:T(8,128)}, f32[4360,128]{1,0:T(8,128)S(1)}, u32[]{:S(2)}, u32[]{:S(2)}) collective-permute-start(f32[4360,128]{1,0:T(8,128)} %get-tuple-element.9.own_ref), channel_id=1, source_target_pairs={{0,1},{1,0},{2,3},{3,2},{4,5},{5,4},{6,7},{7,6},{8,9},{9,8},{10,11... | collective-permute-start | bytes 6696968 | tf_op jit(solution)/shard_map/ppermute | solution.py:226
  13.5 13.2 %all_to_all.15.ends_ref = f32[8,32,128]{2,1,0:T(8,128)S(1)} all-to-all(f32[8,32,128]{2,1,0:T(8,128)} %get-tuple-element.10), channel_id=1, replica_groups=mesh['y'=8,'z'=8,'x'=4,'c'=2] {'z'}, dimensions={0} | all-to-all | bytes 262144 | tf_op jit(solution)/shard_map/all_to_all | solution.py:225
  26.7 0.0 copy-done.3
  26.7 14.6 %all_to_all.16.totals_ref = f32[8,32,128]{2,1,0:T(8,128)S(1)} all-to-all(f32[8,32,128]{2,1,0:T(8,128)S(1)} %shard_map.56), channel_id=1, replica_groups=mesh['y'=8,'z'=8,'x'=4,'c'=2] {'y'}, dimensions={0} | all-to-all | bytes 262144 | tf_op jit(solution)/shard_map/all_to_all | solution.py:228
  41.3 0.0 collective-permute-done.other_ref
  41.3 0.1 shard_map.57
  41.4 10.4 %all_to_all.17.carry_ref = f32[8,32,128]{2,1,0:T(8,128)S(1)} all-to-all(f32[8,32,128]{2,1,0:T(8,128)S(1)} %get-tuple-element.11), channel_id=1, replica_groups=mesh['y'=8,'z'=8,'x'=4,'c'=2] {'z'}, dimensions={0} | all-to-all | bytes 262144 | tf_op jit(solution)/shard_map/all_to_all | solution.py:234
  51.8 6.0 %collective-permute-start.1 = (f32[8,32,128]{2,1,0:T(8,128)S(1)}, f32[8,32,128]{2,1,0:T(8,128)S(1)}, u32[]{:S(2)}, u32[]{:S(2)}) collective-permute-start(f32[8,32,128]{2,1,0:T(8,128)S(1)} %all_to_all.17.carry_ref), channel_id=1, source_target_pairs={{0,1},{1,0},{2,3},{3,2},{4,5},{5,4},{6,7},{7,6},{8,9},{9,8},{10,11... | collective-permute-start | bytes 393224 | tf_op jit(solution)/shard_map/ppermute | solution.py:235
  57.8 1.0 %collective-permute-done.1.carry_other_ref.after_ref = f32[8,32,128]{2,1,0:T(8,128)S(1)} collective-permute-done((f32[8,32,128]{2,1,0:T(8,128)S(1)}, f32[8,32,128]{2,1,0:T(8,128)S(1)}, u32[]{:S(2)}, u32[]{:S(2)}) %collective-permute-start.1) | collective-permute-done | bytes 131104 | tf_op jit(solution)/shard_map/ppermute | solution.py:235
  58.8 0.5 shard_map.58.after_ref
  59.3 0.6 shard_map.59.after_ref
  59.9 0.0 copy-start.1
  59.9 0.0 copy-start.4
  59.9 0.5 shard_map.60.after_ref
  60.5 3.1 %collective-permute-start.4 = (f32[256,256]{1,0:T(8,128)S(1)}, f32[256,256]{1,0:T(8,128)S(1)}, u32[]{:S(2)}, u32[]{:S(2)}) collective-permute-start(f32[256,256]{1,0:T(8,128)S(1)} %shard_map.60.after_ref), channel_id=1, source_target_pairs={{0,6},{1,3},{2,0},{3,5},{4,2},{5,7},{6,4},{7,1},{8,14},{9,11},{10,... | collective-permute-start | bytes 786440 | tf_op jit(solution)/shard_map/ppermute | solution.py:248
  63.6 3.4 %collective-permute-start.3 = (f32[256,256]{1,0:T(8,128)S(1)}, f32[256,256]{1,0:T(8,128)S(1)}, u32[]{:S(2)}, u32[]{:S(2)}) collective-permute-start(f32[256,256]{1,0:T(8,128)S(1)} %shard_map.59.after_ref), channel_id=1, source_target_pairs={{0,2},{1,7},{2,4},{3,1},{4,6},{5,3},{6,0},{7,5},{8,10},{9,15},{10,... | collective-permute-start | bytes 786440 | tf_op jit(solution)/shard_map/ppermute | solution.py:248
  67.0 3.4 %collective-permute-start.2 = (f32[256,256]{1,0:T(8,128)S(1)}, f32[256,256]{1,0:T(8,128)S(1)}, u32[]{:S(2)}, u32[]{:S(2)}) collective-permute-start(f32[256,256]{1,0:T(8,128)S(1)} %shard_map.58.after_ref), channel_id=1, source_target_pairs={{0,4},{1,5},{2,6},{3,7},{4,0},{5,1},{6,2},{7,3},{8,12},{9,13},{10,... | collective-permute-start | bytes 786440 | tf_op jit(solution)/shard_map/ppermute | solution.py:248
  70.4 0.6 shard_map.61.own_ref
  71.1 0.0 collective-permute-done.4.third_ref
  71.1 6.3 %collective-permute-done.3.second_ref = f32[256,256]{1,0:T(8,128)S(1)} collective-permute-done((f32[256,256]{1,0:T(8,128)S(1)}, f32[256,256]{1,0:T(8,128)S(1)}, u32[]{:S(2)}, u32[]{:S(2)}) %collective-permute-start.3) | collective-permute-done | bytes 262176 | tf_op jit(solution)/shard_map/ppermute | solution.py:248
  77.4 1.4 %collective-permute-done.2.first_ref = f32[256,256]{1,0:T(8,128)S(1)} collective-permute-done((f32[256,256]{1,0:T(8,128)S(1)}, f32[256,256]{1,0:T(8,128)S(1)}, u32[]{:S(2)}, u32[]{:S(2)}) %collective-permute-start.2) | collective-permute-done | bytes 262176 | tf_op jit(solution)/shard_map/ppermute | solution.py:248
  78.7 0.7 shard_map.62
  (7 shorter events, 0.0 us)
Async XLA Ops:
  0.0 26.7 %copy-start.3 = (s32[128]{0:T(128)S(1)}, s32[128]{0:T(128)}, u32[]{:S(2)}) copy-start(s32[128]{0:T(128)} %param.7) | copy-start | bytes 1540
  0.0 41.3 %copy-start.2 = (bf16[3,3,128,256]{3,2,1,0:T(8,128)(2,1)S(1)}, bf16[3,3,128,256]{3,2,1,0:T(8,128)(2,1)}, u32[]{:S(2)}) copy-start(bf16[3,3,128,256]{3,2,1,0:T(8,128)(2,1)} %wout_ref.1) | copy-start | bytes 1769476
  4.6 54.1 %copy-start = (f32[4360,128]{1,0:T(8,128)S(1)}, f32[4360,128]{1,0:T(8,128)}, u32[]{:S(2)}) copy-start(f32[4360,128]{1,0:T(8,128)} %get-tuple-element.9.own_ref) | copy-start | bytes 6696964
  4.6 36.6 %collective-permute-start = (f32[4360,128]{1,0:T(8,128)}, f32[4360,128]{1,0:T(8,128)S(1)}, u32[]{:S(2)}, u32[]{:S(2)}) collective-permute-start(f32[4360,128]{1,0:T(8,128)} %get-tuple-element.9.own_ref), channel_id=1, source_target_pairs={{0,1},{1,0},{2,3},{3,2},{4,5},{5,4},{6,7},{7,6},{8,9},{9,8},{10,11... | collective-permute-start | bytes 6696968 | tf_op jit(solution)/shard_map/ppermute | solution.py:226
  51.8 6.9 %collective-permute-start.1 = (f32[8,32,128]{2,1,0:T(8,128)S(1)}, f32[8,32,128]{2,1,0:T(8,128)S(1)}, u32[]{:S(2)}, u32[]{:S(2)}) collective-permute-start(f32[8,32,128]{2,1,0:T(8,128)S(1)} %all_to_all.17.carry_ref), channel_id=1, source_target_pairs={{0,1},{1,0},{2,3},{3,2},{4,5},{5,4},{6,7},{7,6},{8,9},{9,8},{10,11... | collective-permute-start | bytes 393224 | tf_op jit(solution)/shard_map/ppermute | solution.py:235
  59.9 10.5 %copy-start.1 = (bf16[8,16,16,256]{3,2,1,0:T(8,128)(2,1)S(1)}, bf16[8,16,16,256]{3,2,1,0:T(8,128)(2,1)}, u32[]{:S(2)}) copy-start(bf16[8,16,16,256]{3,2,1,0:T(8,128)(2,1)} %x_hbm.3) | copy-start | bytes 3145732
  59.9 10.5 %copy-start.4 = (f32[256]{0:T(256)S(1)}, f32[256]{0:T(256)}, u32[]{:S(2)}) copy-start(f32[256]{0:T(256)} %param.9) | copy-start | bytes 3076
  60.5 10.6 %collective-permute-start.4 = (f32[256,256]{1,0:T(8,128)S(1)}, f32[256,256]{1,0:T(8,128)S(1)}, u32[]{:S(2)}, u32[]{:S(2)}) collective-permute-start(f32[256,256]{1,0:T(8,128)S(1)} %shard_map.60.after_ref), channel_id=1, source_target_pairs={{0,6},{1,3},{2,0},{3,5},{4,2},{5,7},{6,4},{7,1},{8,14},{9,11},{10,... | collective-permute-start | bytes 786440 | tf_op jit(solution)/shard_map/ppermute | solution.py:248
  63.6 13.8 %collective-permute-start.3 = (f32[256,256]{1,0:T(8,128)S(1)}, f32[256,256]{1,0:T(8,128)S(1)}, u32[]{:S(2)}, u32[]{:S(2)}) collective-permute-start(f32[256,256]{1,0:T(8,128)S(1)} %shard_map.59.after_ref), channel_id=1, source_target_pairs={{0,2},{1,7},{2,4},{3,1},{4,6},{5,3},{6,0},{7,5},{8,10},{9,15},{10,... | collective-permute-start | bytes 786440 | tf_op jit(solution)/shard_map/ppermute | solution.py:248
  67.0 11.8 %collective-permute-start.2 = (f32[256,256]{1,0:T(8,128)S(1)}, f32[256,256]{1,0:T(8,128)S(1)}, u32[]{:S(2)}, u32[]{:S(2)}) collective-permute-start(f32[256,256]{1,0:T(8,128)S(1)} %shard_map.58.after_ref), channel_id=1, source_target_pairs={{0,4},{1,5},{2,6},{3,7},{4,0},{5,1},{6,2},{7,3},{8,12},{9,13},{10,... | collective-permute-start | bytes 786440 | tf_op jit(solution)/shard_map/ppermute | solution.py:248

commit v8 on v6

--- a/solution.py
+++ b/solution.py
@@ -134,7 +134,7 @@
 
 
 def readout(offset, own_ref, other_ref, codes_ref, carry_ref, carry_other_ref, w_ref, spad):
-    chip = (lax.axis_index("x") + offset) % 4
+    chip = lax.axis_index("x") ^ (offset ^ (2 * (offset % 2) * lax.axis_index("c")))
     above = 4 * chip + 2 * lax.axis_index("c") - 1
     sides = (
         (own_ref, carry_ref, decay_of(codes_ref[...])),
@@ -185,6 +185,10 @@
         compiler_params=pltpu.CompilerParams(vmem_limit_bytes=limit << 20),
         cost_estimate=pl.CostEstimate(flops=flops, bytes_accessed=moved, transcendentals=0),
     )(*args)
+
+
+def swaps(offset):
+    return [(2 * x + c, 2 * (x ^ offset ^ (2 * (offset % 2) * c)) + c) for x in range(4) for c in range(2)]
 
 
 def shape(*dims, dtype=F32):
@@ -241,7 +245,7 @@
             scratch=(padded,),
             flops=flops // 4,
         )
-        arrived.append(lax.ppermute(piece, "x", [(i, (i + offset) % 4) for i in range(4)]))
+        arrived.append(lax.ppermute(piece, ("x", "c"), swaps(offset)))
     own = call(
         near_kernel,
         shape(owned, CIN),

time: 81.1 us -> 79.4 us (0.979)
  waiting for transfers between devices: 9.79 us -> 8.71 us
    ppermute x3, waiting for transfers between devices: 8.82 us -> 7.74 us  [per_device(): arrived.append(lax.ppermute(piece, ('x', 'c'), swaps(offset)))]
where the time goes in v8:
time: 79.4 us; the launch traced here: 79 us
  blocking collectives  38.1 us (48%)
  starting transfers between devices  24.2 us (30%)
  waiting for transfers between devices  8.71 us (11%)
  Pallas kernels  7.8 us (10%)
    all_to_all x1, blocking collectives, per_device(): totals = lax.all_to_all(total, 'y', 0, 0, tiled=True)  14.6 us
    all_to_all x1, blocking collectives, per_device(): ends = lax.all_to_all(end, 'z', 0, 0, tiled=True)  13.2 us
    all_to_all x1, blocking collectives, per_device(): carry = lax.all_to_all(carries, 'z', 0, 0, tiled=True)  10.4 us
    ppermute x3, starting transfers between devices, per_device(): arrived.append(lax.ppermute(piece, ('x', 'c'), swaps(offset)))  9.39 us
    ppermute x1, starting transfers between devices, per_device(): other = lax.ppermute(shared, 'c', swap)  8.88 us
    pallas_call x8, Pallas kernels, call(): pl.pallas_call(kernel, out_shape=out, in_specs=[pl.BlockSpec(memory_space...  7.8 us
    ppermute x3, waiting for transfers between devices, per_device(): arrived.append(lax.ppermute(piece, ('x', 'c'), swaps(offset)))  7.74 us
    ppermute x1, starting transfers between devices, per_device(): carry_other = lax.ppermute(carry, 'c', swap)  5.97 us
  transfers between devices with their start and end apart: 5, of which 3 were waited for; matrix products, arithmetic and copies ran while one was open for 0% of the time, Pallas kernels for 1%

profile of v8, /device:TPU:1, one launch (start us, length us, event | category | flops | bytes accessed | tf_op | source)
XLA Modules:
  0.0 79.0 jit_solution(8081835473128947448)
XLA Ops:
  0.0 4.6 %shard_map.55 = (f32[4360,128]{1,0:T(8,128)}, f32[8,32,128]{2,1,0:T(8,128)}) custom-call(bf16[8,16,16,256]{3,2,1,0:T(8,128)(2,1)} %x_hbm.3, bf16[3,3,256,128]{3,2,1,0:T(8,128)(2,1)} %w_hbm.1, s32[1,128]{1,0:T(1,128)} %bitcast.3, bf16[3,3,128,256]{3,2,1,0:T(8,128)(2,1)} %wout_ref.1), custom_call_target="tpu_custom_call" | custom-call | flops 1207959552 | bytes 3145728 | tf_op jit(solution)/shard_map/pallas_call | solution.py:179
  4.6 0.0 copy-start
  4.6 8.9 %collective-permute-start = (f32[4360,128]{1,0:T(8,128)}, f32[4360,128]{1,0:T(8,128)S(1)}, u32[]{:S(2)}, u32[]{:S(2)}) collective-permute-start(f32[4360,128]{1,0:T(8,128)} %get-tuple-element.9.own_ref), channel_id=1, source_target_pairs={{0,1},{1,0},{2,3},{3,2},{4,5},{5,4},{6,7},{7,6},{8,9},{9,8},{10,11... | collective-permute-start | bytes 6696968 | tf_op jit(solution)/shard_map/ppermute | solution.py:226
  13.5 13.2 %all_to_all.15.ends_ref = f32[8,32,128]{2,1,0:T(8,128)S(1)} all-to-all(f32[8,32,128]{2,1,0:T(8,128)} %get-tuple-element.10), channel_id=1, replica_groups=mesh['y'=8,'z'=8,'x'=4,'c'=2] {'z'}, dimensions={0} | all-to-all | bytes 262144 | tf_op jit(solution)/shard_map/all_to_all | solution.py:225
  26.7 0.0 copy-done.3
  26.7 14.6 %all_to_all.16.totals_ref = f32[8,32,128]{2,1,0:T(8,128)S(1)} all-to-all(f32[8,32,128]{2,1,0:T(8,128)S(1)} %shard_map.56), channel_id=1, replica_groups=mesh['y'=8,'z'=8,'x'=4,'c'=2] {'y'}, dimensions={0} | all-to-all | bytes 262144 | tf_op jit(solution)/shard_map/all_to_all | solution.py:228
  41.3 0.0 collective-permute-done.other_ref
  41.3 0.1 shard_map.57
  41.4 10.4 %all_to_all.17.carry_ref = f32[8,32,128]{2,1,0:T(8,128)S(1)} all-to-all(f32[8,32,128]{2,1,0:T(8,128)S(1)} %get-tuple-element.11), channel_id=1, replica_groups=mesh['y'=8,'z'=8,'x'=4,'c'=2] {'z'}, dimensions={0} | all-to-all | bytes 262144 | tf_op jit(solution)/shard_map/all_to_all | solution.py:234
  51.8 6.0 %collective-permute-start.1 = (f32[8,32,128]{2,1,0:T(8,128)S(1)}, f32[8,32,128]{2,1,0:T(8,128)S(1)}, u32[]{:S(2)}, u32[]{:S(2)}) collective-permute-start(f32[8,32,128]{2,1,0:T(8,128)S(1)} %all_to_all.17.carry_ref), channel_id=1, source_target_pairs={{0,1},{1,0},{2,3},{3,2},{4,5},{5,4},{6,7},{7,6},{8,9},{9,8},{10,11... | collective-permute-start | bytes 393224 | tf_op jit(solution)/shard_map/ppermute | solution.py:235
  57.8 1.0 %collective-permute-done.1.carry_other_ref.after_ref = f32[8,32,128]{2,1,0:T(8,128)S(1)} collective-permute-done((f32[8,32,128]{2,1,0:T(8,128)S(1)}, f32[8,32,128]{2,1,0:T(8,128)S(1)}, u32[]{:S(2)}, u32[]{:S(2)}) %collective-permute-start.1) | collective-permute-done | bytes 131104 | tf_op jit(solution)/shard_map/ppermute | solution.py:235
  58.8 0.5 shard_map.58.after_ref
  59.3 0.5 shard_map.59.after_ref
  59.9 0.0 copy-start.1
  59.9 0.0 copy-start.4
  59.9 0.6 shard_map.60.after_ref
  60.5 3.1 %collective-permute-start.4 = (f32[256,256]{1,0:T(8,128)S(1)}, f32[256,256]{1,0:T(8,128)S(1)}, u32[]{:S(2)}, u32[]{:S(2)}) collective-permute-start(f32[256,256]{1,0:T(8,128)S(1)} %shard_map.60.after_ref), channel_id=1, source_target_pairs={{0,6},{1,3},{2,4},{3,1},{4,2},{5,7},{6,0},{7,5},{8,14},{9,11},{10,... | collective-permute-start | bytes 786440 | tf_op jit(solution)/shard_map/ppermute | solution.py:248
  63.6 3.7 %collective-permute-start.3 = (f32[256,256]{1,0:T(8,128)S(1)}, f32[256,256]{1,0:T(8,128)S(1)}, u32[]{:S(2)}, u32[]{:S(2)}) collective-permute-start(f32[256,256]{1,0:T(8,128)S(1)} %shard_map.59.after_ref), channel_id=1, source_target_pairs={{0,2},{1,7},{2,0},{3,5},{4,6},{5,3},{6,4},{7,1},{8,10},{9,15},{10,... | collective-permute-start | bytes 786440 | tf_op jit(solution)/shard_map/ppermute | solution.py:248
  67.3 2.6 %collective-permute-start.2 = (f32[256,256]{1,0:T(8,128)S(1)}, f32[256,256]{1,0:T(8,128)S(1)}, u32[]{:S(2)}, u32[]{:S(2)}) collective-permute-start(f32[256,256]{1,0:T(8,128)S(1)} %shard_map.58.after_ref), channel_id=1, source_target_pairs={{0,4},{1,5},{2,6},{3,7},{4,0},{5,1},{6,2},{7,3},{8,12},{9,13},{10,... | collective-permute-start | bytes 786440 | tf_op jit(solution)/shard_map/ppermute | solution.py:248
  69.9 0.6 shard_map.61.own_ref
  70.5 0.0 collective-permute-done.4.third_ref
  70.5 2.0 %collective-permute-done.3.second_ref = f32[256,256]{1,0:T(8,128)S(1)} collective-permute-done((f32[256,256]{1,0:T(8,128)S(1)}, f32[256,256]{1,0:T(8,128)S(1)}, u32[]{:S(2)}, u32[]{:S(2)}) %collective-permute-start.3) | collective-permute-done | bytes 262176 | tf_op jit(solution)/shard_map/ppermute | solution.py:248
  72.5 5.8 %collective-permute-done.2.first_ref = f32[256,256]{1,0:T(8,128)S(1)} collective-permute-done((f32[256,256]{1,0:T(8,128)S(1)}, f32[256,256]{1,0:T(8,128)S(1)}, u32[]{:S(2)}, u32[]{:S(2)}) %collective-permute-start.2) | collective-permute-done | bytes 262176 | tf_op jit(solution)/shard_map/ppermute | solution.py:248
  78.3 0.7 shard_map.62
  (7 shorter events, 0.0 us)
Async XLA Ops:
  0.0 26.7 %copy-start.3 = (s32[128]{0:T(128)S(1)}, s32[128]{0:T(128)}, u32[]{:S(2)}) copy-start(s32[128]{0:T(128)} %param.7) | copy-start | bytes 1540
  0.0 41.3 %copy-start.2 = (bf16[3,3,128,256]{3,2,1,0:T(8,128)(2,1)S(1)}, bf16[3,3,128,256]{3,2,1,0:T(8,128)(2,1)}, u32[]{:S(2)}) copy-start(bf16[3,3,128,256]{3,2,1,0:T(8,128)(2,1)} %wout_ref.1) | copy-start | bytes 1769476
  4.6 54.1 %copy-start = (f32[4360,128]{1,0:T(8,128)S(1)}, f32[4360,128]{1,0:T(8,128)}, u32[]{:S(2)}) copy-start(f32[4360,128]{1,0:T(8,128)} %get-tuple-element.9.own_ref) | copy-start | bytes 6696964
  4.6 36.6 %collective-permute-start = (f32[4360,128]{1,0:T(8,128)}, f32[4360,128]{1,0:T(8,128)S(1)}, u32[]{:S(2)}, u32[]{:S(2)}) collective-permute-start(f32[4360,128]{1,0:T(8,128)} %get-tuple-element.9.own_ref), channel_id=1, source_target_pairs={{0,1},{1,0},{2,3},{3,2},{4,5},{5,4},{6,7},{7,6},{8,9},{9,8},{10,11... | collective-permute-start | bytes 6696968 | tf_op jit(solution)/shard_map/ppermute | solution.py:226
  51.8 6.9 %collective-permute-start.1 = (f32[8,32,128]{2,1,0:T(8,128)S(1)}, f32[8,32,128]{2,1,0:T(8,128)S(1)}, u32[]{:S(2)}, u32[]{:S(2)}) collective-permute-start(f32[8,32,128]{2,1,0:T(8,128)S(1)} %all_to_all.17.carry_ref), channel_id=1, source_target_pairs={{0,1},{1,0},{2,3},{3,2},{4,5},{5,4},{6,7},{7,6},{8,9},{9,8},{10,11... | collective-permute-start | bytes 393224 | tf_op jit(solution)/shard_map/ppermute | solution.py:235
  59.9 10.0 %copy-start.1 = (bf16[8,16,16,256]{3,2,1,0:T(8,128)(2,1)S(1)}, bf16[8,16,16,256]{3,2,1,0:T(8,128)(2,1)}, u32[]{:S(2)}) copy-start(bf16[8,16,16,256]{3,2,1,0:T(8,128)(2,1)} %x_hbm.3) | copy-start | bytes 3145732
  59.9 10.0 %copy-start.4 = (f32[256]{0:T(256)S(1)}, f32[256]{0:T(256)}, u32[]{:S(2)}) copy-start(f32[256]{0:T(256)} %param.9) | copy-start | bytes 3076
  60.5 10.1 %collective-permute-start.4 = (f32[256,256]{1,0:T(8,128)S(1)}, f32[256,256]{1,0:T(8,128)S(1)}, u32[]{:S(2)}, u32[]{:S(2)}) collective-permute-start(f32[256,256]{1,0:T(8,128)S(1)} %shard_map.60.after_ref), channel_id=1, source_target_pairs={{0,6},{1,3},{2,4},{3,1},{4,2},{5,7},{6,0},{7,5},{8,14},{9,11},{10,... | collective-permute-start | bytes 786440 | tf_op jit(solution)/shard_map/ppermute | solution.py:248
  63.6 8.9 %collective-permute-start.3 = (f32[256,256]{1,0:T(8,128)S(1)}, f32[256,256]{1,0:T(8,128)S(1)}, u32[]{:S(2)}, u32[]{:S(2)}) collective-permute-start(f32[256,256]{1,0:T(8,128)S(1)} %shard_map.59.after_ref), channel_id=1, source_target_pairs={{0,2},{1,7},{2,0},{3,5},{4,6},{5,3},{6,4},{7,1},{8,10},{9,15},{10,... | collective-permute-start | bytes 786440 | tf_op jit(solution)/shard_map/ppermute | solution.py:248
  67.3 11.0 %collective-permute-start.2 = (f32[256,256]{1,0:T(8,128)S(1)}, f32[256,256]{1,0:T(8,128)S(1)}, u32[]{:S(2)}, u32[]{:S(2)}) collective-permute-start(f32[256,256]{1,0:T(8,128)S(1)} %shard_map.58.after_ref), channel_id=1, source_target_pairs={{0,4},{1,5},{2,6},{3,7},{4,0},{5,1},{6,2},{7,3},{8,12},{9,13},{10,... | collective-permute-start | bytes 786440 | tf_op jit(solution)/shard_map/ppermute | solution.py:248

commit v9 on v8

--- a/solution.py
+++ b/solution.py
@@ -14,7 +14,7 @@
 DECAY_AT = FRAMES * PIX
 WEIGHT_AT = DECAY_AT + 8
 SHARED = WEIGHT_AT + 18 * PD
-ORDER = (2, 1, 3)
+OPPOSITE, FIRST, LAST = 2, 1, 3
 F32, BF16 = jnp.float32, jnp.bfloat16
 
 
@@ -109,8 +109,8 @@
         out_ref[y] = total
 
 
-def mix_kernel(own_ref, first_ref, second_ref, third_ref, out_ref):
-    value = own_ref[...] + first_ref[...] + second_ref[...] + third_ref[...]
+def mix_kernel(own_ref, first_ref, last_ref, out_ref):
+    value = own_ref[...] + first_ref[...] + last_ref[...]
     half = 0.5 * value
     mixed = half + half * lax.erf(value * (0.5**0.5))
     out_ref[...] = mixed.astype(BF16)
@@ -162,7 +162,10 @@
 
 
 def far_kernel(offset, own_ref, other_ref, codes_ref, carry_ref, carry_other_ref, w_ref, after_ref, out_ref, spad):
-    out_ref[...] = readout(offset, own_ref, other_ref, codes_ref, carry_ref, carry_other_ref, w_ref, spad)
+    value = readout(offset, own_ref, other_ref, codes_ref, carry_ref, carry_other_ref, w_ref, spad)
+    if offset == LAST:
+        value = value + after_ref[...]
+    out_ref[...] = value
 
 
 def near_kernel(own_ref, other_ref, codes_ref, carry_ref, carry_other_ref, w_ref, after_ref, x_hbm, gain_ref,
@@ -235,17 +238,26 @@
     carry_other = lax.ppermute(carry, "c", swap)
     inputs = (shared, other, codes, carry, carry_other, weights)
     padded = pltpu.VMEM((FRAMES, 4, COLS, 2 * PD), BF16)
-    piece, arrived = carry_other, []
-    for offset in ORDER:
-        piece = call(
+
+    def far(offset, after, space):
+        return call(
             functools.partial(far_kernel, offset),
             shape(owned, CIN),
-            (*inputs, piece),
-            spaces=[pltpu.VMEM] * 6 + [pl.ANY],
+            (*inputs, after),
+            spaces=[pltpu.VMEM] * 6 + [space],
             scratch=(padded,),
             flops=flops // 4,
         )
-        arrived.append(lax.ppermute(piece, ("x", "c"), swaps(offset)))
+
+    def send(piece, to):
+        return lax.ppermute(piece, ("x", "c"), swaps(to))
+
+    opposite = far(OPPOSITE, carry_other, pl.ANY)
+    relayed = send(opposite, FIRST)
+    piece = far(FIRST, opposite, pl.ANY)
+    first = send(piece, FIRST)
+    piece = far(LAST, relayed, pltpu.VMEM)
+    last = send(piece, LAST)
     own = call(
         near_kernel,
         shape(owned, CIN),
@@ -254,7 +266,7 @@
         scratch=(padded, pltpu.VMEM((FRAMES, 2, COLS, CIN), BF16), pltpu.SemaphoreType.DMA),
         flops=flops // 4,
     )
-    mixed = call(mix_kernel, shape(owned, CIN, dtype=BF16), (own, *arrived))
+    mixed = call(mix_kernel, shape(owned, CIN, dtype=BF16), (own, first, last))
     return mixed.reshape(FRAMES, 2, COLS, CIN)
 
 

time: 79.4 us -> 77.6 us (0.977); the launches traced: 79 us -> 76.3 us
  waiting for transfers between devices: 8.71 us -> 6.64 us
    ppermute x3, waiting for transfers between devices: 7.74 us -> 5.68 us  [send(): return lax.ppermute(piece, ('x', 'c'), swaps(to))]
  transfers between devices with their start and end apart: 5 -> 5, of which waited for: 3 -> 4; matrix products, arithmetic and copies ran while one was open for 0% -> 0% of each run, Pallas kernels for 1% -> 2%
where the time goes in v9:
time: 77.6 us; the launch traced here: 76.3 us
  blocking collectives  38.1 us (49%)
  starting transfers between devices  23.7 us (31%)
  Pallas kernels  7.78 us (10%)
  waiting for transfers between devices  6.64 us (9%)
    all_to_all x1, blocking collectives, per_device(): totals = lax.all_to_all(total, 'y', 0, 0, tiled=True)  14.6 us
    all_to_all x1, blocking collectives, per_device(): ends = lax.all_to_all(end, 'z', 0, 0, tiled=True)  13.2 us
    all_to_all x1, blocking collectives, per_device(): carry = lax.all_to_all(carries, 'z', 0, 0, tiled=True)  10.4 us
    ppermute x1, starting transfers between devices, per_device(): other = lax.ppermute(shared, 'c', swap)  8.88 us
    ppermute x3, starting transfers between devices, send(): return lax.ppermute(piece, ('x', 'c'), swaps(to))  8.82 us
    pallas_call x8, Pallas kernels, call(): pl.pallas_call(kernel, out_shape=out, in_specs=[pl.BlockSpec(memory_space...  7.78 us
    ppermute x1, starting transfers between devices, per_device(): carry_other = lax.ppermute(carry, 'c', swap)  5.97 us
    ppermute x3, waiting for transfers between devices, send(): return lax.ppermute(piece, ('x', 'c'), swaps(to))  5.68 us
  transfers between devices with their start and end apart: 5, of which 4 were waited for; matrix products, arithmetic and copies ran while one was open for 0% of the time, Pallas kernels for 2%

profile of v9, /device:TPU:1, one launch (start us, length us, event | category | flops | bytes accessed | tf_op | source)
XLA Modules:
  0.0 76.3 jit_solution(8586189044809990326)
XLA Ops:
  0.0 4.6 %shard_map.55 = (f32[4360,128]{1,0:T(8,128)}, f32[8,32,128]{2,1,0:T(8,128)}) custom-call(bf16[8,16,16,256]{3,2,1,0:T(8,128)(2,1)} %x_hbm.3, bf16[3,3,256,128]{3,2,1,0:T(8,128)(2,1)} %w_hbm.1, s32[1,128]{1,0:T(1,128)} %bitcast.3, bf16[3,3,128,256]{3,2,1,0:T(8,128)(2,1)} %wout_ref.1), custom_call_target="tpu_custom_call" | custom-call | flops 1207959552 | bytes 3145728 | tf_op jit(solution)/shard_map/pallas_call | solution.py:182
  4.6 0.0 copy-start
  4.6 8.9 %collective-permute-start = (f32[4360,128]{1,0:T(8,128)}, f32[4360,128]{1,0:T(8,128)S(1)}, u32[]{:S(2)}, u32[]{:S(2)}) collective-permute-start(f32[4360,128]{1,0:T(8,128)} %get-tuple-element.9.own_ref), channel_id=1, source_target_pairs={{0,1},{1,0},{2,3},{3,2},{4,5},{5,4},{6,7},{7,6},{8,9},{9,8},{10,11... | collective-permute-start | bytes 6696968 | tf_op jit(solution)/shard_map/ppermute | solution.py:229
  13.5 13.2 %all_to_all.15.ends_ref = f32[8,32,128]{2,1,0:T(8,128)S(1)} all-to-all(f32[8,32,128]{2,1,0:T(8,128)} %get-tuple-element.10), channel_id=1, replica_groups=mesh['y'=8,'z'=8,'x'=4,'c'=2] {'z'}, dimensions={0} | all-to-all | bytes 262144 | tf_op jit(solution)/shard_map/all_to_all | solution.py:228
  26.7 0.0 copy-done.3
  26.7 14.6 %all_to_all.16.totals_ref = f32[8,32,128]{2,1,0:T(8,128)S(1)} all-to-all(f32[8,32,128]{2,1,0:T(8,128)S(1)} %shard_map.56), channel_id=1, replica_groups=mesh['y'=8,'z'=8,'x'=4,'c'=2] {'y'}, dimensions={0} | all-to-all | bytes 262144 | tf_op jit(solution)/shard_map/all_to_all | solution.py:231
  41.3 0.0 collective-permute-done.other_ref
  41.3 0.1 shard_map.57
  41.4 10.4 %all_to_all.17.carry_ref = f32[8,32,128]{2,1,0:T(8,128)S(1)} all-to-all(f32[8,32,128]{2,1,0:T(8,128)S(1)} %get-tuple-element.11), channel_id=1, replica_groups=mesh['y'=8,'z'=8,'x'=4,'c'=2] {'z'}, dimensions={0} | all-to-all | bytes 262144 | tf_op jit(solution)/shard_map/all_to_all | solution.py:237
  51.8 6.0 %collective-permute-start.1 = (f32[8,32,128]{2,1,0:T(8,128)S(1)}, f32[8,32,128]{2,1,0:T(8,128)S(1)}, u32[]{:S(2)}, u32[]{:S(2)}) collective-permute-start(f32[8,32,128]{2,1,0:T(8,128)S(1)} %all_to_all.17.carry_ref), channel_id=1, source_target_pairs={{0,1},{1,0},{2,3},{3,2},{4,5},{5,4},{6,7},{7,6},{8,9},{9,8},{10,11... | collective-permute-start | bytes 393224 | tf_op jit(solution)/shard_map/ppermute | solution.py:238
  57.8 1.0 %collective-permute-done.1.carry_other_ref.after_ref = f32[8,32,128]{2,1,0:T(8,128)S(1)} collective-permute-done((f32[8,32,128]{2,1,0:T(8,128)S(1)}, f32[8,32,128]{2,1,0:T(8,128)S(1)}, u32[]{:S(2)}, u32[]{:S(2)}) %collective-permute-start.1) | collective-permute-done | bytes 131104 | tf_op jit(solution)/shard_map/ppermute | solution.py:238
  58.8 0.5 shard_map.58.after_ref
  59.3 4.4 %collective-permute-start.2 = (f32[256,256]{1,0:T(8,128)S(1)}, f32[256,256]{1,0:T(8,128)S(1)}, u32[]{:S(2)}, u32[]{:S(2)}) collective-permute-start(f32[256,256]{1,0:T(8,128)S(1)} %shard_map.58.after_ref), channel_id=1, source_target_pairs={{0,2},{1,7},{2,0},{3,5},{4,6},{5,3},{6,4},{7,1},{8,10},{9,15},{10,... | collective-permute-start | bytes 786440 | tf_op jit(solution)/shard_map/ppermute | solution.py:253
  63.7 0.5 shard_map.61
  64.2 0.0 copy-start.1
  64.3 0.0 copy-start.4
  64.3 2.3 %collective-permute-start.3 = (f32[256,256]{1,0:T(8,128)S(1)}, f32[256,256]{1,0:T(8,128)S(1)}, u32[]{:S(2)}, u32[]{:S(2)}) collective-permute-start(f32[256,256]{1,0:T(8,128)S(1)} %shard_map.61), channel_id=1, source_target_pairs={{0,2},{1,7},{2,0},{3,5},{4,6},{5,3},{6,4},{7,1},{8,10},{9,15},{10,... | collective-permute-start | bytes 786440 | tf_op jit(solution)/shard_map/ppermute | solution.py:253
  66.5 1.1 %collective-permute-done.2.after_ref = f32[256,256]{1,0:T(8,128)S(1)} collective-permute-done((f32[256,256]{1,0:T(8,128)S(1)}, f32[256,256]{1,0:T(8,128)S(1)}, u32[]{:S(2)}, u32[]{:S(2)}) %collective-permute-start.2) | collective-permute-done | bytes 262176 | tf_op jit(solution)/shard_map/ppermute | solution.py:253
  67.6 0.6 shard_map.59.after_ref
  68.2 2.2 %collective-permute-start.4 = (f32[256,256]{1,0:T(8,128)S(1)}, f32[256,256]{1,0:T(8,128)S(1)}, u32[]{:S(2)}, u32[]{:S(2)}) collective-permute-start(f32[256,256]{1,0:T(8,128)S(1)} %shard_map.59.after_ref), channel_id=1, source_target_pairs={{0,6},{1,3},{2,4},{3,1},{4,2},{5,7},{6,0},{7,5},{8,14},{9,11},{10,... | collective-permute-start | bytes 786440 | tf_op jit(solution)/shard_map/ppermute | solution.py:253
  70.4 0.6 shard_map.60.own_ref
  71.0 1.7 %collective-permute-done.3.first_ref = f32[256,256]{1,0:T(8,128)S(1)} collective-permute-done((f32[256,256]{1,0:T(8,128)S(1)}, f32[256,256]{1,0:T(8,128)S(1)}, u32[]{:S(2)}, u32[]{:S(2)}) %collective-permute-start.3) | collective-permute-done | bytes 262176 | tf_op jit(solution)/shard_map/ppermute | solution.py:253
  72.7 2.9 %collective-permute-done.4.last_ref = f32[256,256]{1,0:T(8,128)S(1)} collective-permute-done((f32[256,256]{1,0:T(8,128)S(1)}, f32[256,256]{1,0:T(8,128)S(1)}, u32[]{:S(2)}, u32[]{:S(2)}) %collective-permute-start.4) | collective-permute-done | bytes 262176 | tf_op jit(solution)/shard_map/ppermute | solution.py:253
  75.6 0.7 shard_map.62
  (7 shorter events, 0.0 us)
Async XLA Ops:
  0.0 26.7 %copy-start.3 = (s32[128]{0:T(128)S(1)}, s32[128]{0:T(128)}, u32[]{:S(2)}) copy-start(s32[128]{0:T(128)} %param.7) | copy-start | bytes 1540
  0.0 41.3 %copy-start.2 = (bf16[3,3,128,256]{3,2,1,0:T(8,128)(2,1)S(1)}, bf16[3,3,128,256]{3,2,1,0:T(8,128)(2,1)}, u32[]{:S(2)}) copy-start(bf16[3,3,128,256]{3,2,1,0:T(8,128)(2,1)} %wout_ref.1) | copy-start | bytes 1769476
  4.6 54.1 %copy-start = (f32[4360,128]{1,0:T(8,128)S(1)}, f32[4360,128]{1,0:T(8,128)}, u32[]{:S(2)}) copy-start(f32[4360,128]{1,0:T(8,128)} %get-tuple-element.9.own_ref) | copy-start | bytes 6696964
  4.6 36.6 %collective-permute-start = (f32[4360,128]{1,0:T(8,128)}, f32[4360,128]{1,0:T(8,128)S(1)}, u32[]{:S(2)}, u32[]{:S(2)}) collective-permute-start(f32[4360,128]{1,0:T(8,128)} %get-tuple-element.9.own_ref), channel_id=1, source_target_pairs={{0,1},{1,0},{2,3},{3,2},{4,5},{5,4},{6,7},{7,6},{8,9},{9,8},{10,11... | collective-permute-start | bytes 6696968 | tf_op jit(solution)/shard_map/ppermute | solution.py:229
  51.8 6.9 %collective-permute-start.1 = (f32[8,32,128]{2,1,0:T(8,128)S(1)}, f32[8,32,128]{2,1,0:T(8,128)S(1)}, u32[]{:S(2)}, u32[]{:S(2)}) collective-permute-start(f32[8,32,128]{2,1,0:T(8,128)S(1)} %all_to_all.17.carry_ref), channel_id=1, source_target_pairs={{0,1},{1,0},{2,3},{3,2},{4,5},{5,4},{6,7},{7,6},{8,9},{9,8},{10,11... | collective-permute-start | bytes 393224 | tf_op jit(solution)/shard_map/ppermute | solution.py:238
  59.3 8.3 %collective-permute-start.2 = (f32[256,256]{1,0:T(8,128)S(1)}, f32[256,256]{1,0:T(8,128)S(1)}, u32[]{:S(2)}, u32[]{:S(2)}) collective-permute-start(f32[256,256]{1,0:T(8,128)S(1)} %shard_map.58.after_ref), channel_id=1, source_target_pairs={{0,2},{1,7},{2,0},{3,5},{4,6},{5,3},{6,4},{7,1},{8,10},{9,15},{10,... | collective-permute-start | bytes 786440 | tf_op jit(solution)/shard_map/ppermute | solution.py:253
  64.2 6.2 %copy-start.1 = (bf16[8,16,16,256]{3,2,1,0:T(8,128)(2,1)S(1)}, bf16[8,16,16,256]{3,2,1,0:T(8,128)(2,1)}, u32[]{:S(2)}) copy-start(bf16[8,16,16,256]{3,2,1,0:T(8,128)(2,1)} %x_hbm.3) | copy-start | bytes 3145732
  64.3 6.1 %copy-start.4 = (f32[256]{0:T(256)S(1)}, f32[256]{0:T(256)}, u32[]{:S(2)}) copy-start(f32[256]{0:T(256)} %param.9) | copy-start | bytes 3076
  64.3 8.5 %collective-permute-start.3 = (f32[256,256]{1,0:T(8,128)S(1)}, f32[256,256]{1,0:T(8,128)S(1)}, u32[]{:S(2)}, u32[]{:S(2)}) collective-permute-start(f32[256,256]{1,0:T(8,128)S(1)} %shard_map.61), channel_id=1, source_target_pairs={{0,2},{1,7},{2,0},{3,5},{4,6},{5,3},{6,4},{7,1},{8,10},{9,15},{10,... | collective-permute-start | bytes 786440 | tf_op jit(solution)/shard_map/ppermute | solution.py:253
  68.2 7.4 %collective-permute-start.4 = (f32[256,256]{1,0:T(8,128)S(1)}, f32[256,256]{1,0:T(8,128)S(1)}, u32[]{:S(2)}, u32[]{:S(2)}) collective-permute-start(f32[256,256]{1,0:T(8,128)S(1)} %shard_map.59.after_ref), channel_id=1, source_target_pairs={{0,6},{1,3},{2,4},{3,1},{4,2},{5,7},{6,0},{7,5},{8,14},{9,11},{10,... | collective-permute-start | bytes 786440 | tf_op jit(solution)/shard_map/ppermute | solution.py:253

commit v10 on v9

--- a/solution.py
+++ b/solution.py
@@ -134,7 +134,7 @@
 
 
 def readout(offset, own_ref, other_ref, codes_ref, carry_ref, carry_other_ref, w_ref, spad):
-    chip = lax.axis_index("x") ^ (offset ^ (2 * (offset % 2) * lax.axis_index("c")))
+    chip = lax.axis_index("x") ^ (offset ^ (2 * (offset % 2) * (1 - lax.axis_index("c"))))
     above = 4 * chip + 2 * lax.axis_index("c") - 1
     sides = (
         (own_ref, carry_ref, decay_of(codes_ref[...])),
@@ -162,10 +162,11 @@
 
 
 def far_kernel(offset, own_ref, other_ref, codes_ref, carry_ref, carry_other_ref, w_ref, after_ref, out_ref, spad):
-    value = readout(offset, own_ref, other_ref, codes_ref, carry_ref, carry_other_ref, w_ref, spad)
-    if offset == LAST:
-        value = value + after_ref[...]
-    out_ref[...] = value
+    out_ref[...] = readout(offset, own_ref, other_ref, codes_ref, carry_ref, carry_other_ref, w_ref, spad)
+
+
+def join_kernel(piece_ref, relayed_ref, after_ref, out_ref):
+    out_ref[...] = piece_ref[...] + relayed_ref[...]
 
 
 def near_kernel(own_ref, other_ref, codes_ref, carry_ref, carry_other_ref, w_ref, after_ref, x_hbm, gain_ref,
@@ -191,7 +192,7 @@
 
 
 def swaps(offset):
-    return [(2 * x + c, 2 * (x ^ offset ^ (2 * (offset % 2) * c)) + c) for x in range(4) for c in range(2)]
+    return [(2 * x + c, 2 * (x ^ offset ^ (2 * (offset % 2) * (1 - c))) + c) for x in range(4) for c in range(2)]
 
 
 def shape(*dims, dtype=F32):
@@ -239,12 +240,12 @@
     inputs = (shared, other, codes, carry, carry_other, weights)
     padded = pltpu.VMEM((FRAMES, 4, COLS, 2 * PD), BF16)
 
-    def far(offset, after, space):
+    def far(offset, after):
         return call(
             functools.partial(far_kernel, offset),
             shape(owned, CIN),
             (*inputs, after),
-            spaces=[pltpu.VMEM] * 6 + [space],
+            spaces=[pltpu.VMEM] * 6 + [pl.ANY],
             scratch=(padded,),
             flops=flops // 4,
         )
@@ -252,12 +253,11 @@
     def send(piece, to):
         return lax.ppermute(piece, ("x", "c"), swaps(to))
 
-    opposite = far(OPPOSITE, carry_other, pl.ANY)
+    opposite = far(OPPOSITE, carry_other)
     relayed = send(opposite, FIRST)
-    piece = far(FIRST, opposite, pl.ANY)
+    piece = far(FIRST, opposite)
     first = send(piece, FIRST)
-    piece = far(LAST, relayed, pltpu.VMEM)
-    last = send(piece, LAST)
+    piece = far(LAST, piece)
     own = call(
         near_kernel,
         shape(owned, CIN),
@@ -266,6 +266,10 @@
         scratch=(padded, pltpu.VMEM((FRAMES, 2, COLS, CIN), BF16), pltpu.SemaphoreType.DMA),
         flops=flops // 4,
     )
+    piece = call(
+        join_kernel, shape(owned, CIN), (piece, relayed, own), spaces=[pltpu.VMEM] * 2 + [pl.ANY]
+    )
+    last = send(piece, LAST)
     mixed = call(mix_kernel, shape(owned, CIN, dtype=BF16), (own, first, last))
     return mixed.reshape(FRAMES, 2, COLS, CIN)
 

time: 77.6 us -> 77.8 us (level); the launches traced: 76.3 us -> 77.4 us
  starting transfers between devices: 23.7 us -> 24.6 us
    ppermute x3, starting transfers between devices: 8.82 us -> 9.78 us  [send(): return lax.ppermute(piece, ('x', 'c'), swaps(to))]
    pallas_call x8 -> x9, Pallas kernels: 7.78 us -> 7.82 us  [call(): pl.pallas_call(kernel, out_shape=out, in_specs=[pl.BlockSpec(memory_space...]
  transfers between devices with their start and end apart: 5 -> 5, of which waited for: 4 -> 3; matrix products, arithmetic and copies ran while one was open for 0% -> 0% of each run, Pallas kernels for 2% -> 2%
where the time goes in v10:
time: 77.8 us; the launch traced here: 77.4 us
  blocking collectives  38.1 us (49%)
  starting transfers between devices  24.6 us (32%)
  Pallas kernels  7.82 us (10%)
  waiting for transfers between devices  6.67 us (9%)
    all_to_all x1, blocking collectives, per_device(): totals = lax.all_to_all(total, 'y', 0, 0, tiled=True)  14.6 us
    all_to_all x1, blocking collectives, per_device(): ends = lax.all_to_all(end, 'z', 0, 0, tiled=True)  13.2 us
    all_to_all x1, blocking collectives, per_device(): carry = lax.all_to_all(carries, 'z', 0, 0, tiled=True)  10.4 us
    ppermute x3, starting transfers between devices, send(): return lax.ppermute(piece, ('x', 'c'), swaps(to))  9.78 us
    ppermute x1, starting transfers between devices, per_device(): other = lax.ppermute(shared, 'c', swap)  8.88 us
    pallas_call x9, Pallas kernels, call(): pl.pallas_call(kernel, out_shape=out, in_specs=[pl.BlockSpec(memory_space...  7.82 us
    ppermute x1, starting transfers between devices, per_device(): carry_other = lax.ppermute(carry, 'c', swap)  5.97 us
    ppermute x3, waiting for transfers between devices, send(): return lax.ppermute(piece, ('x', 'c'), swaps(to))  5.7 us
  transfers between devices with their start and end apart: 5, of which 3 were waited for; matrix products, arithmetic and copies ran while one was open for 0% of the time, Pallas kernels for 2%

profile of v10, /device:TPU:1, one launch (start us, length us, event | category | flops | bytes accessed | tf_op | source)
XLA Modules:
  0.0 77.4 jit_solution(4641246946318434020)
XLA Ops:
  0.0 4.6 %shard_map.55 = (f32[4360,128]{1,0:T(8,128)}, f32[8,32,128]{2,1,0:T(8,128)}) custom-call(bf16[8,16,16,256]{3,2,1,0:T(8,128)(2,1)} %x_hbm.3, bf16[3,3,256,128]{3,2,1,0:T(8,128)(2,1)} %w_hbm.1, s32[1,128]{1,0:T(1,128)} %bitcast.3, bf16[3,3,128,256]{3,2,1,0:T(8,128)(2,1)} %wout_ref.1), custom_call_target="tpu_custom_call" | custom-call | flops 1207959552 | bytes 3145728 | tf_op jit(solution)/shard_map/pallas_call | solution.py:183
  4.6 0.0 copy-start
  4.6 8.9 %collective-permute-start = (f32[4360,128]{1,0:T(8,128)}, f32[4360,128]{1,0:T(8,128)S(1)}, u32[]{:S(2)}, u32[]{:S(2)}) collective-permute-start(f32[4360,128]{1,0:T(8,128)} %get-tuple-element.9.own_ref), channel_id=1, source_target_pairs={{0,1},{1,0},{2,3},{3,2},{4,5},{5,4},{6,7},{7,6},{8,9},{9,8},{10,11... | collective-permute-start | bytes 6696968 | tf_op jit(solution)/shard_map/ppermute | solution.py:230
  13.5 13.2 %all_to_all.15.ends_ref = f32[8,32,128]{2,1,0:T(8,128)S(1)} all-to-all(f32[8,32,128]{2,1,0:T(8,128)} %get-tuple-element.10), channel_id=1, replica_groups=mesh['y'=8,'z'=8,'x'=4,'c'=2] {'z'}, dimensions={0} | all-to-all | bytes 262144 | tf_op jit(solution)/shard_map/all_to_all | solution.py:229
  26.7 0.0 copy-done.3
  26.7 14.6 %all_to_all.16.totals_ref = f32[8,32,128]{2,1,0:T(8,128)S(1)} all-to-all(f32[8,32,128]{2,1,0:T(8,128)S(1)} %shard_map.56), channel_id=1, replica_groups=mesh['y'=8,'z'=8,'x'=4,'c'=2] {'y'}, dimensions={0} | all-to-all | bytes 262144 | tf_op jit(solution)/shard_map/all_to_all | solution.py:232
  41.3 0.0 collective-permute-done.other_ref
  41.3 0.1 shard_map.57
  41.4 10.4 %all_to_all.17.carry_ref = f32[8,32,128]{2,1,0:T(8,128)S(1)} all-to-all(f32[8,32,128]{2,1,0:T(8,128)S(1)} %get-tuple-element.11), channel_id=1, replica_groups=mesh['y'=8,'z'=8,'x'=4,'c'=2] {'z'}, dimensions={0} | all-to-all | bytes 262144 | tf_op jit(solution)/shard_map/all_to_all | solution.py:238
  51.8 6.0 %collective-permute-start.1 = (f32[8,32,128]{2,1,0:T(8,128)S(1)}, f32[8,32,128]{2,1,0:T(8,128)S(1)}, u32[]{:S(2)}, u32[]{:S(2)}) collective-permute-start(f32[8,32,128]{2,1,0:T(8,128)S(1)} %all_to_all.17.carry_ref), channel_id=1, source_target_pairs={{0,1},{1,0},{2,3},{3,2},{4,5},{5,4},{6,7},{7,6},{8,9},{9,8},{10,11... | collective-permute-start | bytes 393224 | tf_op jit(solution)/shard_map/ppermute | solution.py:239
  57.8 1.0 %collective-permute-done.1.carry_other_ref.after_ref = f32[8,32,128]{2,1,0:T(8,128)S(1)} collective-permute-done((f32[8,32,128]{2,1,0:T(8,128)S(1)}, f32[8,32,128]{2,1,0:T(8,128)S(1)}, u32[]{:S(2)}, u32[]{:S(2)}) %collective-permute-start.1) | collective-permute-done | bytes 131104 | tf_op jit(solution)/shard_map/ppermute | solution.py:239
  58.8 0.5 shard_map.58.after_ref
  59.3 3.1 %collective-permute-start.3 = (f32[256,256]{1,0:T(8,128)S(1)}, f32[256,256]{1,0:T(8,128)S(1)}, u32[]{:S(2)}, u32[]{:S(2)}) collective-permute-start(f32[256,256]{1,0:T(8,128)S(1)} %shard_map.58.after_ref), channel_id=1, source_target_pairs={{0,6},{1,3},{2,4},{3,1},{4,2},{5,7},{6,0},{7,5},{8,14},{9,11},{10,... | collective-permute-start | bytes 786440 | tf_op jit(solution)/shard_map/ppermute | solution.py:254
  62.4 0.6 shard_map.59.after_ref
  63.0 0.0 copy-start.1
  63.0 0.0 copy-start.4
  63.0 2.3 %collective-permute-start.2 = (f32[256,256]{1,0:T(8,128)S(1)}, f32[256,256]{1,0:T(8,128)S(1)}, u32[]{:S(2)}, u32[]{:S(2)}) collective-permute-start(f32[256,256]{1,0:T(8,128)S(1)} %shard_map.59.after_ref), channel_id=1, source_target_pairs={{0,6},{1,3},{2,4},{3,1},{4,2},{5,7},{6,0},{7,5},{8,14},{9,11},{10,... | collective-permute-start | bytes 786440 | tf_op jit(solution)/shard_map/ppermute | solution.py:254
  65.3 0.5 shard_map.60.after_ref.piece_ref
  65.9 0.6 shard_map.61.after_ref.own_ref
  66.5 0.2 collective-permute-done.3.relayed_ref
  66.8 4.4 %collective-permute-start.4 = (f32[256,256]{1,0:T(8,128)S(1)}, f32[256,256]{1,0:T(8,128)S(1)}, u32[]{:S(2)}, u32[]{:S(2)}) collective-permute-start(f32[256,256]{1,0:T(8,128)S(1)} %shard_map.62), channel_id=1, source_target_pairs={{0,2},{1,7},{2,0},{3,5},{4,6},{5,3},{6,4},{7,1},{8,10},{9,15},{10,... | collective-permute-start | bytes 786440 | tf_op jit(solution)/shard_map/ppermute | solution.py:254
  71.1 0.0 collective-permute-done.2.first_ref
  71.1 5.5 %collective-permute-done.4.last_ref = f32[256,256]{1,0:T(8,128)S(1)} collective-permute-done((f32[256,256]{1,0:T(8,128)S(1)}, f32[256,256]{1,0:T(8,128)S(1)}, u32[]{:S(2)}, u32[]{:S(2)}) %collective-permute-start.4) | collective-permute-done | bytes 262176 | tf_op jit(solution)/shard_map/ppermute | solution.py:254
  76.6 0.7 shard_map.63
  (8 shorter events, 0.1 us)
Async XLA Ops:
  0.0 26.7 %copy-start.3 = (s32[128]{0:T(128)S(1)}, s32[128]{0:T(128)}, u32[]{:S(2)}) copy-start(s32[128]{0:T(128)} %param.7) | copy-start | bytes 1540
  0.0 41.3 %copy-start.2 = (bf16[3,3,128,256]{3,2,1,0:T(8,128)(2,1)S(1)}, bf16[3,3,128,256]{3,2,1,0:T(8,128)(2,1)}, u32[]{:S(2)}) copy-start(bf16[3,3,128,256]{3,2,1,0:T(8,128)(2,1)} %wout_ref.1) | copy-start | bytes 1769476
  4.6 54.1 %copy-start = (f32[4360,128]{1,0:T(8,128)S(1)}, f32[4360,128]{1,0:T(8,128)}, u32[]{:S(2)}) copy-start(f32[4360,128]{1,0:T(8,128)} %get-tuple-element.9.own_ref) | copy-start | bytes 6696964
  4.6 36.6 %collective-permute-start = (f32[4360,128]{1,0:T(8,128)}, f32[4360,128]{1,0:T(8,128)S(1)}, u32[]{:S(2)}, u32[]{:S(2)}) collective-permute-start(f32[4360,128]{1,0:T(8,128)} %get-tuple-element.9.own_ref), channel_id=1, source_target_pairs={{0,1},{1,0},{2,3},{3,2},{4,5},{5,4},{6,7},{7,6},{8,9},{9,8},{10,11... | collective-permute-start | bytes 6696968 | tf_op jit(solution)/shard_map/ppermute | solution.py:230
  51.8 6.9 %collective-permute-start.1 = (f32[8,32,128]{2,1,0:T(8,128)S(1)}, f32[8,32,128]{2,1,0:T(8,128)S(1)}, u32[]{:S(2)}, u32[]{:S(2)}) collective-permute-start(f32[8,32,128]{2,1,0:T(8,128)S(1)} %all_to_all.17.carry_ref), channel_id=1, source_target_pairs={{0,1},{1,0},{2,3},{3,2},{4,5},{5,4},{6,7},{7,6},{8,9},{9,8},{10,11... | collective-permute-start | bytes 393224 | tf_op jit(solution)/shard_map/ppermute | solution.py:239
  59.3 7.4 %collective-permute-start.3 = (f32[256,256]{1,0:T(8,128)S(1)}, f32[256,256]{1,0:T(8,128)S(1)}, u32[]{:S(2)}, u32[]{:S(2)}) collective-permute-start(f32[256,256]{1,0:T(8,128)S(1)} %shard_map.58.after_ref), channel_id=1, source_target_pairs={{0,6},{1,3},{2,4},{3,1},{4,2},{5,7},{6,0},{7,5},{8,14},{9,11},{10,... | collective-permute-start | bytes 786440 | tf_op jit(solution)/shard_map/ppermute | solution.py:254
  63.0 2.9 %copy-start.1 = (bf16[8,16,16,256]{3,2,1,0:T(8,128)(2,1)S(1)}, bf16[8,16,16,256]{3,2,1,0:T(8,128)(2,1)}, u32[]{:S(2)}) copy-start(bf16[8,16,16,256]{3,2,1,0:T(8,128)(2,1)} %x_hbm.3) | copy-start | bytes 3145732
  63.0 2.9 %copy-start.4 = (f32[256]{0:T(256)S(1)}, f32[256]{0:T(256)}, u32[]{:S(2)}) copy-start(f32[256]{0:T(256)} %param.9) | copy-start | bytes 3076
  63.0 8.1 %collective-permute-start.2 = (f32[256,256]{1,0:T(8,128)S(1)}, f32[256,256]{1,0:T(8,128)S(1)}, u32[]{:S(2)}, u32[]{:S(2)}) collective-permute-start(f32[256,256]{1,0:T(8,128)S(1)} %shard_map.59.after_ref), channel_id=1, source_target_pairs={{0,6},{1,3},{2,4},{3,1},{4,2},{5,7},{6,0},{7,5},{8,14},{9,11},{10,... | collective-permute-start | bytes 786440 | tf_op jit(solution)/shard_map/ppermute | solution.py:254
  66.8 9.9 %collective-permute-start.4 = (f32[256,256]{1,0:T(8,128)S(1)}, f32[256,256]{1,0:T(8,128)S(1)}, u32[]{:S(2)}, u32[]{:S(2)}) collective-permute-start(f32[256,256]{1,0:T(8,128)S(1)} %shard_map.62), channel_id=1, source_target_pairs={{0,2},{1,7},{2,0},{3,5},{4,6},{5,3},{6,4},{7,1},{8,10},{9,15},{10,... | collective-permute-start | bytes 786440 | tf_op jit(solution)/shard_map/ppermute | solution.py:254

commit v11 on v10

--- a/solution.py
+++ b/solution.py
@@ -109,8 +109,8 @@
         out_ref[y] = total
 
 
-def mix_kernel(own_ref, first_ref, last_ref, out_ref):
-    value = own_ref[...] + first_ref[...] + last_ref[...]
+def mix_kernel(ready_ref, last_ref, out_ref):
+    value = ready_ref[...] + last_ref[...]
     half = 0.5 * value
     mixed = half + half * lax.erf(value * (0.5**0.5))
     out_ref[...] = mixed.astype(BF16)
@@ -134,7 +134,7 @@
 
 
 def readout(offset, own_ref, other_ref, codes_ref, carry_ref, carry_other_ref, w_ref, spad):
-    chip = lax.axis_index("x") ^ (offset ^ (2 * (offset % 2) * (1 - lax.axis_index("c"))))
+    chip = lax.axis_index("x") ^ (offset ^ (2 * (offset % 2) * lax.axis_index("c")))
     above = 4 * chip + 2 * lax.axis_index("c") - 1
     sides = (
         (own_ref, carry_ref, decay_of(codes_ref[...])),
@@ -192,7 +192,7 @@
 
 
 def swaps(offset):
-    return [(2 * x + c, 2 * (x ^ offset ^ (2 * (offset % 2) * (1 - c))) + c) for x in range(4) for c in range(2)]
+    return [(2 * x + c, 2 * (x ^ offset ^ (2 * (offset % 2) * c)) + c) for x in range(4) for c in range(2)]
 
 
 def shape(*dims, dtype=F32):
@@ -270,7 +270,10 @@
         join_kernel, shape(owned, CIN), (piece, relayed, own), spaces=[pltpu.VMEM] * 2 + [pl.ANY]
     )
     last = send(piece, LAST)
-    mixed = call(mix_kernel, shape(owned, CIN, dtype=BF16), (own, first, last))
+    ready = call(
+        join_kernel, shape(owned, CIN), (own, first, piece), spaces=[pltpu.VMEM] * 2 + [pl.ANY]
+    )
+    mixed = call(mix_kernel, shape(owned, CIN, dtype=BF16), (ready, last))
     return mixed.reshape(FRAMES, 2, COLS, CIN)
 
 

time: 77.8 us -> 77.1 us (level)
  starting transfers between devices: 24.6 us -> 23.6 us
    ppermute x3, starting transfers between devices: 9.78 us -> 8.71 us  [send(): return lax.ppermute(piece, ('x', 'c'), swaps(to))]
    pallas_call x9 -> x10, Pallas kernels: 7.82 us -> 7.85 us  [call(): pl.pallas_call(kernel, out_shape=out, in_specs=[pl.BlockSpec(memory_space...]
where the time goes in v11:
time: 77.1 us; the launch traced here: 75.9 us
  blocking collectives  38.1 us (49%)
  starting transfers between devices  23.6 us (31%)
  Pallas kernels  7.85 us (10%)
  waiting for transfers between devices  6.26 us (8%)
    all_to_all x1, blocking collectives, per_device(): totals = lax.all_to_all(total, 'y', 0, 0, tiled=True)  14.6 us
    all_to_all x1, blocking collectives, per_device(): ends = lax.all_to_all(end, 'z', 0, 0, tiled=True)  13.2 us
    all_to_all x1, blocking collectives, per_device(): carry = lax.all_to_all(carries, 'z', 0, 0, tiled=True)  10.4 us
    ppermute x1, starting transfers between devices, per_device(): other = lax.ppermute(shared, 'c', swap)  8.88 us
    ppermute x3, starting transfers between devices, send(): return lax.ppermute(piece, ('x', 'c'), swaps(to))  8.71 us
    pallas_call x10, Pallas kernels, call(): pl.pallas_call(kernel, out_shape=out, in_specs=[pl.BlockSpec(memory_space...  7.85 us
    ppermute x1, starting transfers between devices, per_device(): carry_other = lax.ppermute(carry, 'c', swap)  5.97 us
    ppermute x3, waiting for transfers between devices, send(): return lax.ppermute(piece, ('x', 'c'), swaps(to))  5.29 us
  transfers between devices with their start and end apart: 5, of which 3 were waited for; matrix products, arithmetic and copies ran while one was open for 0% of the time, Pallas kernels for 2%

profile of v11, /device:TPU:1, one launch (start us, length us, event | category | flops | bytes accessed | tf_op | source)
XLA Modules:
  0.0 75.9 jit_solution(7676581975967465463)
XLA Ops:
  0.0 4.6 %shard_map.55 = (f32[4360,128]{1,0:T(8,128)}, f32[8,32,128]{2,1,0:T(8,128)}) custom-call(bf16[8,16,16,256]{3,2,1,0:T(8,128)(2,1)} %x_hbm.3, bf16[3,3,256,128]{3,2,1,0:T(8,128)(2,1)} %w_hbm.1, s32[1,128]{1,0:T(1,128)} %bitcast.3, bf16[3,3,128,256]{3,2,1,0:T(8,128)(2,1)} %wout_ref.1), custom_call_target="tpu_custom_call" | custom-call | flops 1207959552 | bytes 3145728 | tf_op jit(solution)/shard_map/pallas_call | solution.py:183
  4.6 0.0 copy-start
  4.6 8.9 %collective-permute-start = (f32[4360,128]{1,0:T(8,128)}, f32[4360,128]{1,0:T(8,128)S(1)}, u32[]{:S(2)}, u32[]{:S(2)}) collective-permute-start(f32[4360,128]{1,0:T(8,128)} %get-tuple-element.9.own_ref), channel_id=1, source_target_pairs={{0,1},{1,0},{2,3},{3,2},{4,5},{5,4},{6,7},{7,6},{8,9},{9,8},{10,11... | collective-permute-start | bytes 6696968 | tf_op jit(solution)/shard_map/ppermute | solution.py:230
  13.5 13.2 %all_to_all.15.ends_ref = f32[8,32,128]{2,1,0:T(8,128)S(1)} all-to-all(f32[8,32,128]{2,1,0:T(8,128)} %get-tuple-element.10), channel_id=1, replica_groups=mesh['y'=8,'z'=8,'x'=4,'c'=2] {'z'}, dimensions={0} | all-to-all | bytes 262144 | tf_op jit(solution)/shard_map/all_to_all | solution.py:229
  26.7 0.0 copy-done.3
  26.7 14.6 %all_to_all.16.totals_ref = f32[8,32,128]{2,1,0:T(8,128)S(1)} all-to-all(f32[8,32,128]{2,1,0:T(8,128)S(1)} %shard_map.56), channel_id=1, replica_groups=mesh['y'=8,'z'=8,'x'=4,'c'=2] {'y'}, dimensions={0} | all-to-all | bytes 262144 | tf_op jit(solution)/shard_map/all_to_all | solution.py:232
  41.3 0.0 collective-permute-done.other_ref
  41.3 0.1 shard_map.57
  41.4 10.4 %all_to_all.17.carry_ref = f32[8,32,128]{2,1,0:T(8,128)S(1)} all-to-all(f32[8,32,128]{2,1,0:T(8,128)S(1)} %get-tuple-element.11), channel_id=1, replica_groups=mesh['y'=8,'z'=8,'x'=4,'c'=2] {'z'}, dimensions={0} | all-to-all | bytes 262144 | tf_op jit(solution)/shard_map/all_to_all | solution.py:238
  51.8 6.0 %collective-permute-start.1 = (f32[8,32,128]{2,1,0:T(8,128)S(1)}, f32[8,32,128]{2,1,0:T(8,128)S(1)}, u32[]{:S(2)}, u32[]{:S(2)}) collective-permute-start(f32[8,32,128]{2,1,0:T(8,128)S(1)} %all_to_all.17.carry_ref), channel_id=1, source_target_pairs={{0,1},{1,0},{2,3},{3,2},{4,5},{5,4},{6,7},{7,6},{8,9},{9,8},{10,11... | collective-permute-start | bytes 393224 | tf_op jit(solution)/shard_map/ppermute | solution.py:239
  57.8 1.0 %collective-permute-done.1.carry_other_ref.after_ref = f32[8,32,128]{2,1,0:T(8,128)S(1)} collective-permute-done((f32[8,32,128]{2,1,0:T(8,128)S(1)}, f32[8,32,128]{2,1,0:T(8,128)S(1)}, u32[]{:S(2)}, u32[]{:S(2)}) %collective-permute-start.1) | collective-permute-done | bytes 131104 | tf_op jit(solution)/shard_map/ppermute | solution.py:239
  58.8 0.5 shard_map.58.after_ref
  59.3 4.4 %collective-permute-start.3 = (f32[256,256]{1,0:T(8,128)S(1)}, f32[256,256]{1,0:T(8,128)S(1)}, u32[]{:S(2)}, u32[]{:S(2)}) collective-permute-start(f32[256,256]{1,0:T(8,128)S(1)} %shard_map.58.after_ref), channel_id=1, source_target_pairs={{0,2},{1,7},{2,0},{3,5},{4,6},{5,3},{6,4},{7,1},{8,10},{9,15},{10,... | collective-permute-start | bytes 786440 | tf_op jit(solution)/shard_map/ppermute | solution.py:254
  63.7 0.5 shard_map.59.after_ref
  64.2 0.0 copy-start.1
  64.3 0.0 copy-start.4
  64.3 2.3 %collective-permute-start.2 = (f32[256,256]{1,0:T(8,128)S(1)}, f32[256,256]{1,0:T(8,128)S(1)}, u32[]{:S(2)}, u32[]{:S(2)}) collective-permute-start(f32[256,256]{1,0:T(8,128)S(1)} %shard_map.59.after_ref), channel_id=1, source_target_pairs={{0,2},{1,7},{2,0},{3,5},{4,6},{5,3},{6,4},{7,1},{8,10},{9,15},{10,... | collective-permute-start | bytes 786440 | tf_op jit(solution)/shard_map/ppermute | solution.py:254
  66.5 0.6 shard_map.60.after_ref.piece_ref
  67.1 0.6 shard_map.61.after_ref.piece_ref
  67.7 0.0 collective-permute-done.3.relayed_ref
  67.8 2.1 %collective-permute-start.4 = (f32[256,256]{1,0:T(8,128)S(1)}, f32[256,256]{1,0:T(8,128)S(1)}, u32[]{:S(2)}, u32[]{:S(2)}) collective-permute-start(f32[256,256]{1,0:T(8,128)S(1)} %shard_map.62.after_ref), channel_id=1, source_target_pairs={{0,6},{1,3},{2,4},{3,1},{4,2},{5,7},{6,0},{7,5},{8,14},{9,11},{10,... | collective-permute-start | bytes 786440 | tf_op jit(solution)/shard_map/ppermute | solution.py:254
  69.9 2.9 %collective-permute-done.2.relayed_ref = f32[256,256]{1,0:T(8,128)S(1)} collective-permute-done((f32[256,256]{1,0:T(8,128)S(1)}, f32[256,256]{1,0:T(8,128)S(1)}, u32[]{:S(2)}, u32[]{:S(2)}) %collective-permute-start.2) | collective-permute-done | bytes 262176 | tf_op jit(solution)/shard_map/ppermute | solution.py:254
  72.8 2.4 %collective-permute-done.4.last_ref = f32[256,256]{1,0:T(8,128)S(1)} collective-permute-done((f32[256,256]{1,0:T(8,128)S(1)}, f32[256,256]{1,0:T(8,128)S(1)}, u32[]{:S(2)}, u32[]{:S(2)}) %collective-permute-start.4) | collective-permute-done | bytes 262176 | tf_op jit(solution)/shard_map/ppermute | solution.py:254
  75.2 0.7 shard_map.64
  (9 shorter events, 0.1 us)
Async XLA Ops:
  0.0 26.7 %copy-start.3 = (s32[128]{0:T(128)S(1)}, s32[128]{0:T(128)}, u32[]{:S(2)}) copy-start(s32[128]{0:T(128)} %param.7) | copy-start | bytes 1540
  0.0 41.3 %copy-start.2 = (bf16[3,3,128,256]{3,2,1,0:T(8,128)(2,1)S(1)}, bf16[3,3,128,256]{3,2,1,0:T(8,128)(2,1)}, u32[]{:S(2)}) copy-start(bf16[3,3,128,256]{3,2,1,0:T(8,128)(2,1)} %wout_ref.1) | copy-start | bytes 1769476
  4.6 54.1 %copy-start = (f32[4360,128]{1,0:T(8,128)S(1)}, f32[4360,128]{1,0:T(8,128)}, u32[]{:S(2)}) copy-start(f32[4360,128]{1,0:T(8,128)} %get-tuple-element.9.own_ref) | copy-start | bytes 6696964
  4.6 36.6 %collective-permute-start = (f32[4360,128]{1,0:T(8,128)}, f32[4360,128]{1,0:T(8,128)S(1)}, u32[]{:S(2)}, u32[]{:S(2)}) collective-permute-start(f32[4360,128]{1,0:T(8,128)} %get-tuple-element.9.own_ref), channel_id=1, source_target_pairs={{0,1},{1,0},{2,3},{3,2},{4,5},{5,4},{6,7},{7,6},{8,9},{9,8},{10,11... | collective-permute-start | bytes 6696968 | tf_op jit(solution)/shard_map/ppermute | solution.py:230
  51.8 6.9 %collective-permute-start.1 = (f32[8,32,128]{2,1,0:T(8,128)S(1)}, f32[8,32,128]{2,1,0:T(8,128)S(1)}, u32[]{:S(2)}, u32[]{:S(2)}) collective-permute-start(f32[8,32,128]{2,1,0:T(8,128)S(1)} %all_to_all.17.carry_ref), channel_id=1, source_target_pairs={{0,1},{1,0},{2,3},{3,2},{4,5},{5,4},{6,7},{7,6},{8,9},{9,8},{10,11... | collective-permute-start | bytes 393224 | tf_op jit(solution)/shard_map/ppermute | solution.py:239
  59.3 8.4 %collective-permute-start.3 = (f32[256,256]{1,0:T(8,128)S(1)}, f32[256,256]{1,0:T(8,128)S(1)}, u32[]{:S(2)}, u32[]{:S(2)}) collective-permute-start(f32[256,256]{1,0:T(8,128)S(1)} %shard_map.58.after_ref), channel_id=1, source_target_pairs={{0,2},{1,7},{2,0},{3,5},{4,6},{5,3},{6,4},{7,1},{8,10},{9,15},{10,... | collective-permute-start | bytes 786440 | tf_op jit(solution)/shard_map/ppermute | solution.py:254
  64.2 2.9 %copy-start.1 = (bf16[8,16,16,256]{3,2,1,0:T(8,128)(2,1)S(1)}, bf16[8,16,16,256]{3,2,1,0:T(8,128)(2,1)}, u32[]{:S(2)}) copy-start(bf16[8,16,16,256]{3,2,1,0:T(8,128)(2,1)} %x_hbm.3) | copy-start | bytes 3145732
  64.3 2.8 %copy-start.4 = (f32[256]{0:T(256)S(1)}, f32[256]{0:T(256)}, u32[]{:S(2)}) copy-start(f32[256]{0:T(256)} %param.9) | copy-start | bytes 3076
  64.3 8.5 %collective-permute-start.2 = (f32[256,256]{1,0:T(8,128)S(1)}, f32[256,256]{1,0:T(8,128)S(1)}, u32[]{:S(2)}, u32[]{:S(2)}) collective-permute-start(f32[256,256]{1,0:T(8,128)S(1)} %shard_map.59.after_ref), channel_id=1, source_target_pairs={{0,2},{1,7},{2,0},{3,5},{4,6},{5,3},{6,4},{7,1},{8,10},{9,15},{10,... | collective-permute-start | bytes 786440 | tf_op jit(solution)/shard_map/ppermute | solution.py:254
  67.8 7.4 %collective-permute-start.4 = (f32[256,256]{1,0:T(8,128)S(1)}, f32[256,256]{1,0:T(8,128)S(1)}, u32[]{:S(2)}, u32[]{:S(2)}) collective-permute-start(f32[256,256]{1,0:T(8,128)S(1)} %shard_map.62.after_ref), channel_id=1, source_target_pairs={{0,6},{1,3},{2,4},{3,1},{4,2},{5,7},{6,0},{7,5},{8,14},{9,11},{10,... | collective-permute-start | bytes 786440 | tf_op jit(solution)/shard_map/ppermute | solution.py:254

commit v12 on v10

--- a/solution.py
+++ b/solution.py
@@ -134,7 +134,7 @@
 
 
 def readout(offset, own_ref, other_ref, codes_ref, carry_ref, carry_other_ref, w_ref, spad):
-    chip = lax.axis_index("x") ^ (offset ^ (2 * (offset % 2) * (1 - lax.axis_index("c"))))
+    chip = lax.axis_index("x") ^ (offset ^ (2 * (offset % 2) * lax.axis_index("c")))
     above = 4 * chip + 2 * lax.axis_index("c") - 1
     sides = (
         (own_ref, carry_ref, decay_of(codes_ref[...])),
@@ -192,7 +192,7 @@
 
 
 def swaps(offset):
-    return [(2 * x + c, 2 * (x ^ offset ^ (2 * (offset % 2) * (1 - c))) + c) for x in range(4) for c in range(2)]
+    return [(2 * x + c, 2 * (x ^ offset ^ (2 * (offset % 2) * c)) + c) for x in range(4) for c in range(2)]
 
 
 def shape(*dims, dtype=F32):
@@ -258,6 +258,10 @@
     piece = far(FIRST, opposite)
     first = send(piece, FIRST)
     piece = far(LAST, piece)
+    piece = call(
+        join_kernel, shape(owned, CIN), (piece, relayed, piece), spaces=[pltpu.VMEM] * 2 + [pl.ANY]
+    )
+    last = send(piece, LAST)
     own = call(
         near_kernel,
         shape(owned, CIN),
@@ -266,10 +270,6 @@
         scratch=(padded, pltpu.VMEM((FRAMES, 2, COLS, CIN), BF16), pltpu.SemaphoreType.DMA),
         flops=flops // 4,
     )
-    piece = call(
-        join_kernel, shape(owned, CIN), (piece, relayed, own), spaces=[pltpu.VMEM] * 2 + [pl.ANY]
-    )
-    last = send(piece, LAST)
     mixed = call(mix_kernel, shape(owned, CIN, dtype=BF16), (own, first, last))
     return mixed.reshape(FRAMES, 2, COLS, CIN)
 

time: 77.8 us -> 77.1 us (level); the launches traced: 77.4 us -> 75.8 us
  starting transfers between devices: 24.6 us -> 23.7 us
    ppermute x3, starting transfers between devices: 9.78 us -> 8.82 us  [send(): return lax.ppermute(piece, ('x', 'c'), swaps(to))]
  transfers between devices with their start and end apart: 5 -> 5, of which waited for: 3 -> 4; matrix products, arithmetic and copies ran while one was open for 0% -> 0% of each run, Pallas kernels for 2% -> 2%
where the time goes in v12:
time: 77.1 us; the launch traced here: 75.8 us
  blocking collectives  38.1 us (49%)
  starting transfers between devices  23.7 us (31%)
  Pallas kernels  7.81 us (10%)
  waiting for transfers between devices  6.08 us (8%)
    all_to_all x1, blocking collectives, per_device(): totals = lax.all_to_all(total, 'y', 0, 0, tiled=True)  14.6 us
    all_to_all x1, blocking collectives, per_device(): ends = lax.all_to_all(end, 'z', 0, 0, tiled=True)  13.2 us
    all_to_all x1, blocking collectives, per_device(): carry = lax.all_to_all(carries, 'z', 0, 0, tiled=True)  10.4 us
    ppermute x1, starting transfers between devices, per_device(): other = lax.ppermute(shared, 'c', swap)  8.88 us
    ppermute x3, starting transfers between devices, send(): return lax.ppermute(piece, ('x', 'c'), swaps(to))  8.82 us
    pallas_call x9, Pallas kernels, call(): pl.pallas_call(kernel, out_shape=out, in_specs=[pl.BlockSpec(memory_space...  7.81 us
    ppermute x1, starting transfers between devices, per_device(): carry_other = lax.ppermute(carry, 'c', swap)  5.97 us
    ppermute x3, waiting for transfers between devices, send(): return lax.ppermute(piece, ('x', 'c'), swaps(to))  5.11 us
  transfers between devices with their start and end apart: 5, of which 4 were waited for; matrix products, arithmetic and copies ran while one was open for 0% of the time, Pallas kernels for 2%

profile of v12, /device:TPU:1, one launch (start us, length us, event | category | flops | bytes accessed | tf_op | source)
XLA Modules:
  0.0 75.8 jit_solution(13126265118821570637)
XLA Ops:
  0.0 4.6 %shard_map.55 = (f32[4360,128]{1,0:T(8,128)}, f32[8,32,128]{2,1,0:T(8,128)}) custom-call(bf16[8,16,16,256]{3,2,1,0:T(8,128)(2,1)} %x_hbm.3, bf16[3,3,256,128]{3,2,1,0:T(8,128)(2,1)} %w_hbm.1, s32[1,128]{1,0:T(1,128)} %bitcast.3, bf16[3,3,128,256]{3,2,1,0:T(8,128)(2,1)} %wout_ref.1), custom_call_target="tpu_custom_call" | custom-call | flops 1207959552 | bytes 3145728 | tf_op jit(solution)/shard_map/pallas_call | solution.py:183
  4.6 0.0 copy-start
  4.6 8.9 %collective-permute-start = (f32[4360,128]{1,0:T(8,128)}, f32[4360,128]{1,0:T(8,128)S(1)}, u32[]{:S(2)}, u32[]{:S(2)}) collective-permute-start(f32[4360,128]{1,0:T(8,128)} %get-tuple-element.9.own_ref), channel_id=1, source_target_pairs={{0,1},{1,0},{2,3},{3,2},{4,5},{5,4},{6,7},{7,6},{8,9},{9,8},{10,11... | collective-permute-start | bytes 6696968 | tf_op jit(solution)/shard_map/ppermute | solution.py:230
  13.5 13.2 %all_to_all.15.ends_ref = f32[8,32,128]{2,1,0:T(8,128)S(1)} all-to-all(f32[8,32,128]{2,1,0:T(8,128)} %get-tuple-element.10), channel_id=1, replica_groups=mesh['y'=8,'z'=8,'x'=4,'c'=2] {'z'}, dimensions={0} | all-to-all | bytes 262144 | tf_op jit(solution)/shard_map/all_to_all | solution.py:229
  26.7 0.0 copy-done.3
  26.7 14.6 %all_to_all.16.totals_ref = f32[8,32,128]{2,1,0:T(8,128)S(1)} all-to-all(f32[8,32,128]{2,1,0:T(8,128)S(1)} %shard_map.56), channel_id=1, replica_groups=mesh['y'=8,'z'=8,'x'=4,'c'=2] {'y'}, dimensions={0} | all-to-all | bytes 262144 | tf_op jit(solution)/shard_map/all_to_all | solution.py:232
  41.3 0.0 collective-permute-done.other_ref
  41.3 0.1 shard_map.57
  41.4 10.4 %all_to_all.17.carry_ref = f32[8,32,128]{2,1,0:T(8,128)S(1)} all-to-all(f32[8,32,128]{2,1,0:T(8,128)S(1)} %get-tuple-element.11), channel_id=1, replica_groups=mesh['y'=8,'z'=8,'x'=4,'c'=2] {'z'}, dimensions={0} | all-to-all | bytes 262144 | tf_op jit(solution)/shard_map/all_to_all | solution.py:238
  51.8 6.0 %collective-permute-start.1 = (f32[8,32,128]{2,1,0:T(8,128)S(1)}, f32[8,32,128]{2,1,0:T(8,128)S(1)}, u32[]{:S(2)}, u32[]{:S(2)}) collective-permute-start(f32[8,32,128]{2,1,0:T(8,128)S(1)} %all_to_all.17.carry_ref), channel_id=1, source_target_pairs={{0,1},{1,0},{2,3},{3,2},{4,5},{5,4},{6,7},{7,6},{8,9},{9,8},{10,11... | collective-permute-start | bytes 393224 | tf_op jit(solution)/shard_map/ppermute | solution.py:239
  57.8 1.0 %collective-permute-done.1.carry_other_ref.after_ref = f32[8,32,128]{2,1,0:T(8,128)S(1)} collective-permute-done((f32[8,32,128]{2,1,0:T(8,128)S(1)}, f32[8,32,128]{2,1,0:T(8,128)S(1)}, u32[]{:S(2)}, u32[]{:S(2)}) %collective-permute-start.1) | collective-permute-done | bytes 131104 | tf_op jit(solution)/shard_map/ppermute | solution.py:239
  58.8 0.5 shard_map.58.after_ref
  59.3 4.4 %collective-permute-start.2 = (f32[256,256]{1,0:T(8,128)S(1)}, f32[256,256]{1,0:T(8,128)S(1)}, u32[]{:S(2)}, u32[]{:S(2)}) collective-permute-start(f32[256,256]{1,0:T(8,128)S(1)} %shard_map.58.after_ref), channel_id=1, source_target_pairs={{0,2},{1,7},{2,0},{3,5},{4,6},{5,3},{6,4},{7,1},{8,10},{9,15},{10,... | collective-permute-start | bytes 786440 | tf_op jit(solution)/shard_map/ppermute | solution.py:254
  63.7 0.5 shard_map.59.after_ref
  64.2 0.0 copy-start.1
  64.3 0.0 copy-start.4
  64.3 2.3 %collective-permute-start.3 = (f32[256,256]{1,0:T(8,128)S(1)}, f32[256,256]{1,0:T(8,128)S(1)}, u32[]{:S(2)}, u32[]{:S(2)}) collective-permute-start(f32[256,256]{1,0:T(8,128)S(1)} %shard_map.59.after_ref), channel_id=1, source_target_pairs={{0,2},{1,7},{2,0},{3,5},{4,6},{5,3},{6,4},{7,1},{8,10},{9,15},{10,... | collective-permute-start | bytes 786440 | tf_op jit(solution)/shard_map/ppermute | solution.py:254
  66.5 0.6 shard_map.60.piece_ref.after_ref
  67.1 0.5 collective-permute-done.2.relayed_ref
  67.7 2.2 %collective-permute-start.4 = (f32[256,256]{1,0:T(8,128)S(1)}, f32[256,256]{1,0:T(8,128)S(1)}, u32[]{:S(2)}, u32[]{:S(2)}) collective-permute-start(f32[256,256]{1,0:T(8,128)S(1)} %shard_map.61.after_ref), channel_id=1, source_target_pairs={{0,6},{1,3},{2,4},{3,1},{4,2},{5,7},{6,0},{7,5},{8,14},{9,11},{10,... | collective-permute-start | bytes 786440 | tf_op jit(solution)/shard_map/ppermute | solution.py:254
  69.9 0.6 shard_map.62.own_ref
  70.5 2.2 %collective-permute-done.3.first_ref = f32[256,256]{1,0:T(8,128)S(1)} collective-permute-done((f32[256,256]{1,0:T(8,128)S(1)}, f32[256,256]{1,0:T(8,128)S(1)}, u32[]{:S(2)}, u32[]{:S(2)}) %collective-permute-start.3) | collective-permute-done | bytes 262176 | tf_op jit(solution)/shard_map/ppermute | solution.py:254
  72.7 2.4 %collective-permute-done.4.last_ref = f32[256,256]{1,0:T(8,128)S(1)} collective-permute-done((f32[256,256]{1,0:T(8,128)S(1)}, f32[256,256]{1,0:T(8,128)S(1)}, u32[]{:S(2)}, u32[]{:S(2)}) %collective-permute-start.4) | collective-permute-done | bytes 262176 | tf_op jit(solution)/shard_map/ppermute | solution.py:254
  75.1 0.7 shard_map.63
  (8 shorter events, 0.1 us)
Async XLA Ops:
  0.0 26.7 %copy-start.3 = (s32[128]{0:T(128)S(1)}, s32[128]{0:T(128)}, u32[]{:S(2)}) copy-start(s32[128]{0:T(128)} %param.7) | copy-start | bytes 1540
  0.0 41.3 %copy-start.2 = (bf16[3,3,128,256]{3,2,1,0:T(8,128)(2,1)S(1)}, bf16[3,3,128,256]{3,2,1,0:T(8,128)(2,1)}, u32[]{:S(2)}) copy-start(bf16[3,3,128,256]{3,2,1,0:T(8,128)(2,1)} %wout_ref.1) | copy-start | bytes 1769476
  4.6 54.1 %copy-start = (f32[4360,128]{1,0:T(8,128)S(1)}, f32[4360,128]{1,0:T(8,128)}, u32[]{:S(2)}) copy-start(f32[4360,128]{1,0:T(8,128)} %get-tuple-element.9.own_ref) | copy-start | bytes 6696964
  4.6 36.6 %collective-permute-start = (f32[4360,128]{1,0:T(8,128)}, f32[4360,128]{1,0:T(8,128)S(1)}, u32[]{:S(2)}, u32[]{:S(2)}) collective-permute-start(f32[4360,128]{1,0:T(8,128)} %get-tuple-element.9.own_ref), channel_id=1, source_target_pairs={{0,1},{1,0},{2,3},{3,2},{4,5},{5,4},{6,7},{7,6},{8,9},{9,8},{10,11... | collective-permute-start | bytes 6696968 | tf_op jit(solution)/shard_map/ppermute | solution.py:230
  51.8 6.9 %collective-permute-start.1 = (f32[8,32,128]{2,1,0:T(8,128)S(1)}, f32[8,32,128]{2,1,0:T(8,128)S(1)}, u32[]{:S(2)}, u32[]{:S(2)}) collective-permute-start(f32[8,32,128]{2,1,0:T(8,128)S(1)} %all_to_all.17.carry_ref), channel_id=1, source_target_pairs={{0,1},{1,0},{2,3},{3,2},{4,5},{5,4},{6,7},{7,6},{8,9},{9,8},{10,11... | collective-permute-start | bytes 393224 | tf_op jit(solution)/shard_map/ppermute | solution.py:239
  59.3 8.3 %collective-permute-start.2 = (f32[256,256]{1,0:T(8,128)S(1)}, f32[256,256]{1,0:T(8,128)S(1)}, u32[]{:S(2)}, u32[]{:S(2)}) collective-permute-start(f32[256,256]{1,0:T(8,128)S(1)} %shard_map.58.after_ref), channel_id=1, source_target_pairs={{0,2},{1,7},{2,0},{3,5},{4,6},{5,3},{6,4},{7,1},{8,10},{9,15},{10,... | collective-permute-start | bytes 786440 | tf_op jit(solution)/shard_map/ppermute | solution.py:254
  64.2 5.6 %copy-start.1 = (bf16[8,16,16,256]{3,2,1,0:T(8,128)(2,1)S(1)}, bf16[8,16,16,256]{3,2,1,0:T(8,128)(2,1)}, u32[]{:S(2)}) copy-start(bf16[8,16,16,256]{3,2,1,0:T(8,128)(2,1)} %x_hbm.3) | copy-start | bytes 3145732
  64.3 5.6 %copy-start.4 = (f32[256]{0:T(256)S(1)}, f32[256]{0:T(256)}, u32[]{:S(2)}) copy-start(f32[256]{0:T(256)} %param.9) | copy-start | bytes 3076
  64.3 8.5 %collective-permute-start.3 = (f32[256,256]{1,0:T(8,128)S(1)}, f32[256,256]{1,0:T(8,128)S(1)}, u32[]{:S(2)}, u32[]{:S(2)}) collective-permute-start(f32[256,256]{1,0:T(8,128)S(1)} %shard_map.59.after_ref), channel_id=1, source_target_pairs={{0,2},{1,7},{2,0},{3,5},{4,6},{5,3},{6,4},{7,1},{8,10},{9,15},{10,... | collective-permute-start | bytes 786440 | tf_op jit(solution)/shard_map/ppermute | solution.py:254
  67.7 7.4 %collective-permute-start.4 = (f32[256,256]{1,0:T(8,128)S(1)}, f32[256,256]{1,0:T(8,128)S(1)}, u32[]{:S(2)}, u32[]{:S(2)}) collective-permute-start(f32[256,256]{1,0:T(8,128)S(1)} %shard_map.61.after_ref), channel_id=1, source_target_pairs={{0,6},{1,3},{2,4},{3,1},{4,2},{5,7},{6,0},{7,5},{8,14},{9,11},{10,... | collective-permute-start | bytes 786440 | tf_op jit(solution)/shard_map/ppermute | solution.py:254
